TPU v7x, 256 devices: a whole 4x4x8 slice. The times are simulated.
256 devices in a mesh: lat: 32 (over x, z), lead: 8 (over y, core).
Axes of the slice: x: 4, y: 4, z: 8, core: 2. Of those that a mesh axis runs over, the one named last changes fastest.
Arguments:
- latent: bfloat16 [32, 256, 64, 256], P('lat', None, 'lead'), may hold values from -6 to 6
- conv_weight: bfloat16 [3, 3, 256, 256], replicated, may hold values from -0.125 to 0.125
- conv_bias: float32 [256], replicated, may hold values from -4 to 4
- norm_gain: float32 [256], replicated, may hold values from 0.1 to 1.9
- w_query: bfloat16 [256, 256], replicated, may hold values from -12 to 12
- w_key: bfloat16 [256, 256], replicated, may hold values from -0.25 to 0.25
- w_value: bfloat16 [256, 256], replicated, may hold values from -0.375 to 0.375
- w_out: bfloat16 [256, 256], replicated, may hold values from -0.375 to 0.375
Outputs:
- section_out: bfloat16 [32, 256, 64, 256], P('lat', None, 'lead')
All inputs are finite; a program needn't handle non-finite values.
Results may differ from a plain program's by a relative error of at most 0.014.
Values may be sent and summed in bfloat16 or wider, within the bound.
No kernel may reach another device: no remote copies, remote signals or barrier semaphores. Data moves between devices by JAX's collectives and lax.ppermute only.
A program may use at most 128 MiB of HBM per device.

v0:
```python
import math

import jax
import jax.numpy as jnp
from jax import lax
from jax.sharding import PartitionSpec as P

HD = 32


def padded_2(block, sides, width):
    for axis, dim in sides:
        count = lax.axis_size(axis)
        forward = [(i, i + 1) for i in range(count - 1)]
        backward = [(target, source) for source, target in forward]
        low = lax.ppermute(
            lax.slice_in_dim(block, block.shape[dim] - width, None, axis=dim), axis, forward
        )
        high = lax.ppermute(lax.slice_in_dim(block, 0, width, axis=dim), axis, backward)
        block = jnp.concatenate([low, block, high], axis=dim)
    return block


def attend(query, keys, values):
    chans = query.shape[-1]
    heads = chans // HD
    q_shape = query.shape
    query = query.reshape(-1, q_shape[-2], heads, HD)
    keys = keys.reshape(-1, keys.shape[-2], heads, HD)
    values = values.reshape(-1, values.shape[-2], heads, HD)
    scores = jnp.einsum(
        "pqhd,pkhd->phqk", query, keys, preferred_element_type=jnp.float32
    ) / math.sqrt(HD)
    top = jnp.max(scores, axis=-1, keepdims=True)
    expo = jnp.exp(scores - top)
    weights = (expo / jnp.sum(expo, axis=-1, keepdims=True)).astype(jnp.bfloat16)
    attended = jnp.einsum("phqk,pkhd->pqhd", weights, values, preferred_element_type=jnp.float32)
    return attended.astype(jnp.bfloat16).reshape(q_shape)


def project(normed, weight):
    shape = normed.shape
    flat = jnp.dot(normed.reshape(-1, shape[-1]), weight, preferred_element_type=jnp.float32)
    return flat.astype(jnp.bfloat16).reshape(shape)


def shards(latent, conv_weight, conv_bias, norm_gain, w_query, w_key, w_value, w_out):
    nrows, width, leads, chans = latent.shape
    extended = padded_2(latent, (("lat", 0),), 1)
    padded = jnp.pad(extended, ((0, 0), (1, 1), (0, 0), (0, 0)))
    acc = jnp.zeros((nrows * width * leads, chans), jnp.float32)
    for a in range(3):
        for b in range(3):
            piece = padded[a : a + nrows, b : b + width].reshape(-1, chans)
            acc = acc + jnp.dot(piece, conv_weight[a, b], preferred_element_type=jnp.float32)
    hidden = jax.nn.gelu(acc + conv_bias, approximate=True).astype(jnp.bfloat16)
    hidden_f = hidden.astype(jnp.float32)
    mean = jnp.mean(hidden_f, axis=-1, keepdims=True)
    var = jnp.mean((hidden_f - mean) ** 2, axis=-1, keepdims=True)
    normed = ((hidden_f - mean) * lax.rsqrt(var + 1e-05) * norm_gain).astype(jnp.bfloat16)
    normed = normed.reshape(nrows, width, leads, chans)
    block = lax.all_to_all(normed, "lead", split_axis=1, concat_axis=2, tiled=True)
    attended_px = attend(project(block, w_query), project(block, w_key), project(block, w_value))
    attended = lax.all_to_all(attended_px, "lead", split_axis=2, concat_axis=1, tiled=True)
    mixed = hidden_f + jnp.dot(
        attended.reshape(-1, chans), w_out, preferred_element_type=jnp.float32
    )
    return mixed.astype(jnp.bfloat16).reshape(nrows, width, leads, chans)


def solution(mesh):
    in_specs = (P("lat", None, "lead", None), P(), P(), P(), P(), P(), P(), P())
    out_specs = P("lat", None, "lead", None)
    return jax.shard_map(shards, mesh=mesh, in_specs=in_specs, out_specs=out_specs, check_vma=False)
```

profile of v0, /device:TPU:6, one launch (start us, length us, event | category | flops | bytes accessed | tf_op | source)
XLA Modules:
  0.0 127.0 jit_solution(6796232368115607537)
XLA Ops:
  0.0 0.0 copy-start
  0.0 0.0 copy-start.2
  0.0 8.1 %collective-permute-start.1 = (bf16[1,256,8,256]{3,2,1,0:T(8,128)(2,1)}, bf16[1,256,8,256]{3,2,1,0:T(8,128)(2,1)S(1)}, u32[]{:S(2)}, u32[]{:S(2)}) collective-permute-start(bf16[1,256,8,256]{3,2,1,0:T(8,128)(2,1)} %param.8), channel_id=1, source_target_pairs={{8,0},{16,8},{24,16},{32,24},{40,32},{48,40},{56,48},{64,56},{72,6... | collective-permute-start | bytes 3145736 | tf_op jit(solution)/shard_map/ppermute | solution.py:19
  8.2 1.9 %collective-permute-start = (bf16[1,256,8,256]{3,2,1,0:T(8,128)(2,1)}, bf16[1,256,8,256]{3,2,1,0:T(8,128)(2,1)S(1)}, u32[]{:S(2)}, u32[]{:S(2)}) collective-permute-start(bf16[1,256,8,256]{3,2,1,0:T(8,128)(2,1)} %param.8), channel_id=1, source_target_pairs={{0,8},{8,16},{16,24},{24,32},{32,40},{40,48},{48,56},{56,64},{64,7... | collective-permute-start | bytes 3145736 | tf_op jit(solution)/shard_map/ppermute | solution.py:16
  10.1 1.7 %fusion.46 = f32[2048,256]{1,0:T(8,128)S(1)} fusion(bf16[1,256,8,256]{3,2,1,0:T(8,128)(2,1)} %param.8, bf16[3,3,256,256]{3,2,1,0:T(8,128)(2,1)} %param.9), kind=kOutput, calls=%fused_computation.61 | convolution fusion | flops 268435456 | bytes 3276800 | tf_op jit(solution)/shard_map/dot_general | solution.py:55
  11.8 0.0 copy-start.4
  11.8 19.1 %collective-permute-done.1 = bf16[1,256,8,256]{3,2,1,0:T(8,128)(2,1)S(1)} collective-permute-done((bf16[1,256,8,256]{3,2,1,0:T(8,128)(2,1)}, bf16[1,256,8,256]{3,2,1,0:T(8,128)(2,1)S(1)}, u32[]{:S(2)}, u32[]{:S(2)}) %collective-permute-start.1) | collective-permute-done | bytes 1048608 | tf_op jit(solution)/shard_map/ppermute | solution.py:19
  30.9 6.1 %collective-permute-done = bf16[1,256,8,256]{3,2,1,0:T(8,128)(2,1)S(1)} collective-permute-done((bf16[1,256,8,256]{3,2,1,0:T(8,128)(2,1)}, bf16[1,256,8,256]{3,2,1,0:T(8,128)(2,1)S(1)}, u32[]{:S(2)}, u32[]{:S(2)}) %collective-permute-start) | collective-permute-done | bytes 1048608 | tf_op jit(solution)/shard_map/ppermute | solution.py:16
  37.0 0.0 copy-done.2
  37.0 0.6 fusion.11
  37.6 0.0 copy-done.4
  37.6 0.4 fusion.40
  38.0 0.4 fusion.41
  38.4 0.4 fusion.42
  38.9 0.4 fusion.43
  39.3 0.4 fusion.39
  39.8 0.4 fusion.48
  40.2 0.0 copy-start.8
  40.2 0.4 fusion.44
  40.6 0.2 copy-done.8
  40.9 0.0 copy-start.9
  40.9 1.7 %convert_reduce_fusion = (f32[2048]{0:T(1024)S(1)}, bf16[2048,256]{1,0:T(8,128)(2,1)S(1)}) fusion(f32[256]{0:T(256)S(1)} %copy-done.8, f32[2048,256]{1,0:T(8,128)S(1)} %fusion.39, f32[2048,256]{1,0:T(8,128)S(1)} %fusion.44, f32[2048,256]{1,0:T(8,128)S(1)} %fusion.40, bf16[3,3,256,256]{3,2,1,0:T(8,128)(2,1)S(1)} %copy-done.4, ...), kind=kOutput, calls=%fused_computation.17 | convolution fusion | flops 278919168 | bytes 19014656 | tf_op jit(solution)/shard_map/dot_general | solution.py:55
  42.6 0.6 fusion.19
  43.3 0.0 copy-done.9
  43.3 0.7 fusion.38
  44.0 20.4 %all_to_all.30 = bf16[1,256,8,256]{3,2,0,1:T(8,128)(2,1)S(1)} all-to-all(bf16[1,256,8,256]{3,2,0,1:T(8,128)(2,1)S(1)} %fusion.38), channel_id=1, replica_groups=mesh['lat'=32,'lead'=8] {'lead'}, dimensions={1} | all-to-all | bytes 2097152 | tf_op jit(solution)/shard_map/all_to_all | solution.py:62
  64.4 0.1 copy.33
  64.5 0.0 copy-done
  64.6 1.4 %convolution_convert_fusion = bf16[2048,256]{1,0:T(8,128)(2,1)} fusion(bf16[2048,256]{1,0:T(8,128)(2,1)S(1)} %bitcast.91, bf16[256,256]{1,0:T(8,128)(2,1)S(1)} %copy-done), kind=kOutput, calls=%fused_computation.25 | convolution fusion | flops 268959744 | bytes 2228224 | tf_op jit(solution)/shard_map/dot_general | solution.py:43
  66.0 1.5 %copy.36 = bf16[2048,256]{0,1:T(8,128)(2,1)S(1)} copy(bf16[2048,256]{1,0:T(8,128)(2,1)} %convolution_convert_fusion) | data formatting | bytes 2097152 | tf_op jit(solution)/shard_map/convert_element_type | solution.py:44
  67.4 0.0 copy-start.5
  67.5 0.0 copy-start.6
  67.5 3.2 %reshape_reshape.11 = bf16[32,64,8,32]{1,0,3,2:T(8,128)(2,1)} reshape(bf16[2048,256]{0,1:T(8,128)(2,1)S(1)} %copy.36) | data formatting | bytes 2097152 | tf_op jit(solution)/shard_map/reshape;reshape | solution.py:29
  70.7 0.0 copy-done.5
  70.7 0.4 convolution_convert_fusion.1
  71.1 0.0 copy-done.6
  71.1 1.4 %convolution_convert_fusion.2 = bf16[2048,256]{1,0:T(8,128)(2,1)} fusion(bf16[2048,256]{1,0:T(8,128)(2,1)S(1)} %bitcast.93, bf16[256,256]{1,0:T(8,128)(2,1)S(1)} %copy-done.6), kind=kOutput, calls=%fused_computation.27 | convolution fusion | flops 268959744 | bytes 2228224 | tf_op jit(solution)/shard_map/dot_general | solution.py:43
  72.5 2.3 %copy.34 = bf16[2048,256]{0,1:T(8,128)(2,1)} copy(bf16[2048,256]{1,0:T(8,128)(2,1)} %convolution_convert_fusion.2) | data formatting | bytes 2097152 | tf_op jit(solution)/shard_map/convert_element_type | solution.py:44
  74.8 0.6 copy.35
  75.4 3.2 %reshape_reshape.10 = bf16[32,64,8,32]{1,0,3,2:T(8,128)(2,1)} reshape(bf16[2048,256]{0,1:T(8,128)(2,1)S(1)} %copy.35) | data formatting | bytes 2097152 | tf_op jit(solution)/shard_map/reshape;reshape | solution.py:28
  78.6 0.0 copy-start.1
  78.6 4.6 %reshape_reshape.9 = bf16[32,64,8,32]{1,0,3,2:T(8,128)(2,1)} reshape(bf16[2048,256]{0,1:T(8,128)(2,1)} %copy.34) | data formatting | bytes 2097152 | tf_op jit(solution)/shard_map/reshape;reshape | solution.py:30
  83.1 0.0 copy-done.1
  83.2 4.4 %fusion.31 = f32[32,8,64,64]{2,3,1,0:T(8,128)S(1)} fusion(bf16[32,64,8,32]{1,0,3,2:T(8,128)(2,1)S(1)} %copy-done.1, bf16[32,64,8,32]{1,0,3,2:T(8,128)(2,1)} %reshape_reshape.10), kind=kOutput, calls=%fused_computation.42 | convolution fusion | flops 67108864 | bytes 6291456 | tf_op jit(solution)/shard_map/pqhd,pkhd->phqk/dot_general | solution.py:31
  87.5 0.0 copy-start.3
  87.5 12.2 %fusion.69 = (f32[32,8,64]{2,1,0:T(8,128)S(1)}, f32[32,8,64,64]{2,3,1,0:T(8,128)S(1)}) fusion(f32[32,8,64,64]{2,3,1,0:T(8,128)S(1)} %fusion.31), kind=kOutput, calls=%fused_computation.87 | output fusion | flops 4194367 | bytes 8454144 | tf_op jit(solution)/shard_map/sub | solution.py:35
  99.7 0.0 copy-done.3
  99.7 3.8 %fusion.34 = bf16[32,8,32,64]{3,2,1,0:T(8,128)(2,1)} fusion(f32[32,8,64,64]{2,3,1,0:T(8,128)S(1)} %get-tuple-element.8, f32[32,8,64]{2,1,0:T(8,128)S(1)} %get-tuple-element.7, bf16[32,64,8,32]{1,0,3,2:T(8,128)(2,1)S(1)} %copy-done.3), kind=kOutput, calls=%fused_computation.45 | convolution fusion | flops 69730304 | bytes 6356992 | tf_op jit(solution)/shard_map/phqk,pkhd->pqhd/dot_general | solution.py:37
  103.5 2.7 %copy.41 = bf16[1,32,64,256]{3,1,0,2:T(8,128)(2,1)S(1)} copy(bf16[1,32,64,256]{2,3,1,0:T(8,128)(2,1)} %bitcast.97) | data formatting | bytes 2097152 | tf_op jit(solution)/shard_map/reshape | solution.py:38
  106.2 18.5 %all_to_all.31 = bf16[1,32,64,256]{3,1,0,2:T(8,128)(2,1)S(1)} all-to-all(bf16[1,32,64,256]{3,1,0,2:T(8,128)(2,1)S(1)} %copy.41), channel_id=1, replica_groups=mesh['lat'=32,'lead'=8] {'lead'}, dimensions={2} | all-to-all | bytes 2097152 | tf_op jit(solution)/shard_map/all_to_all | solution.py:64
  124.7 0.0 copy-start.7
  124.7 0.6 copy.54
  125.3 0.1 copy.43
  125.4 0.2 copy-done.7
  125.6 1.4 %fusion.37 = bf16[1,256,8,256]{3,2,1,0:T(8,128)(2,1)} fusion(bf16[2048,256]{1,0:T(8,128)(2,1)S(1)} %bitcast.94, bf16[256,256]{1,0:T(8,128)(2,1)S(1)} %copy-done.7, bf16[2048,256]{1,0:T(8,128)(2,1)S(1)} %get-tuple-element.6), kind=kOutput, calls=%fused_computation.46 | convolution fusion | flops 270008320 | bytes 3276800 | tf_op jit(solution)/shard_map/dot_general | solution.py:65
  (2 shorter events, 0.0 us)
Async XLA Ops:
  0.0 64.5 %copy-start = (bf16[256,256]{1,0:T(8,128)(2,1)S(1)}, bf16[256,256]{1,0:T(8,128)(2,1)}, u32[]{:S(2)}) copy-start(bf16[256,256]{1,0:T(8,128)(2,1)} %param.13) | copy-start | bytes 393220
  0.0 37.0 %copy-start.2 = (bf16[1,256,8,256]{3,2,1,0:T(8,128)(2,1)S(1)}, bf16[1,256,8,256]{3,2,1,0:T(8,128)(2,1)}, u32[]{:S(2)}) copy-start(bf16[1,256,8,256]{3,2,1,0:T(8,128)(2,1)} %param.8) | copy-start | bytes 3145732
  0.0 30.9 %collective-permute-start.1 = (bf16[1,256,8,256]{3,2,1,0:T(8,128)(2,1)}, bf16[1,256,8,256]{3,2,1,0:T(8,128)(2,1)S(1)}, u32[]{:S(2)}, u32[]{:S(2)}) collective-permute-start(bf16[1,256,8,256]{3,2,1,0:T(8,128)(2,1)} %param.8), channel_id=1, source_target_pairs={{8,0},{16,8},{24,16},{32,24},{40,32},{48,40},{56,48},{64,56},{72,6... | collective-permute-start | bytes 3145736 | tf_op jit(solution)/shard_map/ppermute | solution.py:19
  8.2 28.8 %collective-permute-start = (bf16[1,256,8,256]{3,2,1,0:T(8,128)(2,1)}, bf16[1,256,8,256]{3,2,1,0:T(8,128)(2,1)S(1)}, u32[]{:S(2)}, u32[]{:S(2)}) collective-permute-start(bf16[1,256,8,256]{3,2,1,0:T(8,128)(2,1)} %param.8), channel_id=1, source_target_pairs={{0,8},{8,16},{16,24},{24,32},{32,40},{40,48},{48,56},{56,64},{64,7... | collective-permute-start | bytes 3145736 | tf_op jit(solution)/shard_map/ppermute | solution.py:16
  11.8 25.8 %copy-start.4 = (bf16[3,3,256,256]{3,2,1,0:T(8,128)(2,1)S(1)}, bf16[3,3,256,256]{3,2,1,0:T(8,128)(2,1)}, u32[]{:S(2)}) copy-start(bf16[3,3,256,256]{3,2,1,0:T(8,128)(2,1)} %param.9) | copy-start | bytes 3538948
  40.2 0.7 copy-start.8
  40.9 2.4 %copy-start.9 = (f32[256]{0:T(256)S(1)}, f32[256]{0:T(256)}, u32[]{:S(2)}) copy-start(f32[256]{0:T(256)} %param.11) | copy-start | bytes 3076
  67.4 3.2 %copy-start.5 = (bf16[256,256]{1,0:T(8,128)(2,1)S(1)}, bf16[256,256]{1,0:T(8,128)(2,1)}, u32[]{:S(2)}) copy-start(bf16[256,256]{1,0:T(8,128)(2,1)} %param.12) | copy-start | bytes 393220
  67.5 3.7 %copy-start.6 = (bf16[256,256]{1,0:T(8,128)(2,1)S(1)}, bf16[256,256]{1,0:T(8,128)(2,1)}, u32[]{:S(2)}) copy-start(bf16[256,256]{1,0:T(8,128)(2,1)} %param.14) | copy-start | bytes 393220
  78.6 4.6 %copy-start.1 = (bf16[32,64,8,32]{1,0,3,2:T(8,128)(2,1)S(1)}, bf16[32,64,8,32]{1,0,3,2:T(8,128)(2,1)}, u32[]{:S(2)}) copy-start(bf16[32,64,8,32]{1,0,3,2:T(8,128)(2,1)} %reshape_reshape.11) | copy-start | bytes 3145732
  87.5 12.2 %copy-start.3 = (bf16[32,64,8,32]{1,0,3,2:T(8,128)(2,1)S(1)}, bf16[32,64,8,32]{1,0,3,2:T(8,128)(2,1)}, u32[]{:S(2)}) copy-start(bf16[32,64,8,32]{1,0,3,2:T(8,128)(2,1)} %reshape_reshape.9) | copy-start | bytes 3145732
  124.7 0.9 copy-start.7
where the time goes:
time: 127 us
  blocking collectives  38.9 us (31%)
  waiting for transfers between devices  25.2 us (20%)
  local copies, waits for them, and re-layouts  19.3 us (15%)
  matrix products  19.2 us (15%)
  other arithmetic  14.1 us (11%)
  starting transfers between devices  10.1 us (8%)
    all_to_all x1, blocking collectives, shards(): lax.all_to_all(normed, 'lead', split_axis=1, concat_axis=2, tiled=True)  20.4 us
    ppermute x1, waiting for transfers between devices, padded_2(): lax.ppermute(lax.slice_in_dim(block, 0, width, axis=dim), axis, backward)  19.1 us
    all_to_all x1, blocking collectives, shards(): lax.all_to_all(attended_px, 'lead', split_axis=2, concat_axis=1, tiled=True)  18.5 us
    sub x1, other arithmetic, attend(): expo = jnp.exp(scores - top)  12.2 us
    ppermute x1, starting transfers between devices, padded_2(): lax.ppermute(lax.slice_in_dim(block, 0, width, axis=dim), axis, backward)  8.15 us
    dot_general x9, matrix products, shards(): jnp.dot(piece, conv_weight[a, b], preferred_element_type=jnp.float32)  6.44 us
    ppermute x1, waiting for transfers between devices, padded_2(): lax.ppermute(lax.slice_in_dim(block, block.shape[dim] - width, None, axis...  6.12 us
    another operation x1, local copies, waits for them, and re-layouts, attend(): values = values.reshape(-1, values.shape[-2], heads, HD)  4.55 us
  transfers between devices with their start and end apart: 2, of which 2 were waited for; matrix products, arithmetic and copies ran while one was open for 1% of the time, Pallas kernels for 0%

commit v1 on v0

v1 whole, which is shorter than its diff:
```python
import functools
import math

import jax
import jax.numpy as jnp
from jax import lax
from jax.experimental import pallas as pl
from jax.experimental.pallas import tpu as pltpu
from jax.sharding import PartitionSpec as P

HD = 32
NT = (((1,), (1,)), ((), ()))
F32 = jnp.float32
BF16 = jnp.bfloat16
Q_SCALE = math.log2(math.e) / math.sqrt(HD)
VMEM = pl.BlockSpec(memory_space=pltpu.VMEM)


def params(mib):
    return pltpu.CompilerParams(vmem_limit_bytes=mib << 20)


def cost(flops, nbytes, transcendentals=0):
    return pl.CostEstimate(
        flops=int(flops), bytes_accessed=int(nbytes), transcendentals=int(transcendentals)
    )


def gelu(x):
    return 0.5 * x * (1.0 + jnp.tanh(math.sqrt(2 / math.pi) * (x + 0.044715 * (x * x * x))))


def layer_norm(hidden, gain):
    hidden = hidden.astype(F32)
    centred = hidden - jnp.mean(hidden, axis=-1, keepdims=True)
    var = jnp.mean(centred * centred, axis=-1, keepdims=True)
    return (centred * lax.rsqrt(var + 1e-05) * gain).astype(BF16)


def taps(ref, start, count):
    size, leads, chans = ref.shape
    zero = jnp.zeros((1, leads, chans), ref.dtype)
    out = []
    for first in (start - 1, start, start + 1):
        low, high = max(first, 0), min(first + count, size)
        piece = ref[low:high]
        if low > first:
            piece = jnp.concatenate([zero, piece], axis=0)
        if high < first + count:
            piece = jnp.concatenate([piece, zero], axis=0)
        out.append(piece.reshape(count * leads, chans))
    return out


def conv_kernel(tile, offset, shift, up, mid, down, weight, bias, gain, hidden_out, normed_out):
    width, leads, chans = hidden_out.shape
    rows = (up, mid.at[pl.ds(shift, up.shape[0])], down)

    def conv(i):
        pieces = [piece for row in rows for piece in taps(row, i * tile + offset, tile)]
        return jnp.dot(jnp.concatenate(pieces, axis=1), weight[...], preferred_element_type=F32)

    def finish(i, acc):
        here = slice(i * tile, (i + 1) * tile)
        hidden = gelu(acc + bias[...]).astype(BF16)
        hidden_out[here] = hidden.reshape(tile, leads, chans)
        normed_out[here] = layer_norm(hidden, gain[...]).reshape(tile, leads, chans)

    acc = conv(0)
    for i in range(width // tile):
        later = conv(i + 1) if (i + 1) * tile < width else None
        finish(i, acc)
        acc = later


def conv_norm(up, mid, down, weight, bias, gain, start, width):
    _, leads, chans = mid.shape
    low = max(start - 1, 0)
    tile = math.gcd(width, 32)
    shape = jax.ShapeDtypeStruct((width, leads, chans), BF16)
    size = width * leads * chans
    return pl.pallas_call(
        functools.partial(conv_kernel, tile, start - low, low),
        out_shape=[shape, shape],
        in_specs=[VMEM] * 6,
        out_specs=[VMEM] * 2,
        compiler_params=params(40),
        cost_estimate=cost(size * 18 * chans, size * 10 + 18 * chans * chans, size),
    )(up, mid, down, weight, bias, gain)


def attend_kernel(block, x_ref, w_ref, ones_ref, out_ref):
    parts, pixels, leads, chans = x_ref.shape
    times, heads = parts * leads, chans // HD
    lane = lax.broadcasted_iota(jnp.int32, (times, chans), 1)
    masks = [(lane >= h * HD) & (lane < (h + 1) * HD) for h in range(heads)]
    low_half = lax.broadcasted_iota(jnp.int32, (times, 2 * times), 1) < times

    def by_head(x):
        return jnp.concatenate([jnp.where(m, x, jnp.zeros_like(x)) for m in masks], axis=0)

    def soft(scores):
        out = []
        for i in range(heads // 2):
            pair = scores[:, 2 * times * i : 2 * times * (i + 1)]
            top0 = jnp.max(jnp.where(low_half, pair, -jnp.inf), axis=1, keepdims=True)
            top1 = jnp.max(jnp.where(low_half, -jnp.inf, pair), axis=1, keepdims=True)
            out.append(jnp.exp2(pair - jnp.where(low_half, top0, top1)).astype(BF16))
        return jnp.concatenate(out, axis=1)

    def body(i, carry):
        first = i * block
        x = x_ref[:, pl.ds(first, block)].reshape(parts * block * leads, chans)
        qkv = jnp.dot(x, w_ref[...], preferred_element_type=F32)
        shape = (parts, block, leads, chans)
        query = (qkv[:, :chans] * Q_SCALE).astype(BF16).reshape(shape)
        keys = qkv[:, chans : 2 * chans].astype(BF16).reshape(shape)
        values = qkv[:, 2 * chans :].astype(BF16).reshape(shape)

        def pick(a, p):
            return a[:, p].reshape(times, chans)

        scores = [
            lax.dot_general(pick(query, p), by_head(pick(keys, p)), NT, preferred_element_type=F32)
            for p in range(block)
        ]
        expo = [soft(s) for s in scores]
        total = jnp.dot(jnp.concatenate(expo, axis=0), ones_ref[...], preferred_element_type=F32)
        mixed = [
            jnp.dot(expo[p], by_head(pick(values, p)), preferred_element_type=F32)
            for p in range(block)
        ]
        for p in range(block):
            attended = mixed[p] / total[p * times : (p + 1) * times]
            out_ref[:, first + p] = attended.astype(BF16).reshape(parts, leads, chans)
        return carry

    lax.fori_loop(0, pixels // block, body, 0)


def attend(x, w_qkv, ones):
    parts, pixels, leads, chans = x.shape
    size = x.size
    return pl.pallas_call(
        functools.partial(attend_kernel, math.gcd(pixels, 8)),
        out_shape=jax.ShapeDtypeStruct(x.shape, BF16),
        in_specs=[VMEM] * 3,
        out_specs=VMEM,
        compiler_params=params(32),
        cost_estimate=cost(size * chans * 20, size * 4 + 6 * chans * chans, size * 2),
    )(x, w_qkv, ones)


def exchange(x):
    return lax.all_to_all(x, "lead", split_axis=0, concat_axis=0, tiled=True)


def shards(latent, conv_weight, conv_bias, norm_gain, w_query, w_key, w_value, w_out):
    latent = latent[0]
    width, leads, chans = latent.shape
    lats, parts = lax.axis_size("lat"), lax.axis_size("lead")
    times = parts * leads
    w_conv = conv_weight.reshape(9 * chans, chans)
    w_qkv = jnp.concatenate([w_query, w_key, w_value], axis=1)
    ones = (jnp.arange(chans // HD * times)[:, None] // times == jnp.arange(chans)[None] // HD).astype(BF16)
    bias, gain = conv_bias.reshape(1, chans), norm_gain.reshape(1, chans)
    north = [(i, i + 1) for i in range(lats - 1)]
    south = [(i + 1, i) for i in range(lats - 1)]

    up = lax.ppermute(latent, "lat", north)
    down = lax.ppermute(latent, "lat", south)
    hidden, normed = conv_norm(up, latent, down, w_conv, bias, gain, 0, width)
    block = exchange(normed.reshape(parts, width // parts, leads, chans))
    attended = exchange(attend(block, w_qkv, ones)).reshape(-1, chans)
    mixed = hidden.reshape(-1, chans).astype(F32) + jnp.dot(attended, w_out, preferred_element_type=F32)
    return mixed.astype(BF16).reshape(1, width, leads, chans)


def solution(mesh):
    in_specs = (P("lat", None, "lead", None), P(), P(), P(), P(), P(), P(), P())
    out_specs = P("lat", None, "lead", None)
    return jax.shard_map(shards, mesh=mesh, in_specs=in_specs, out_specs=out_specs, check_vma=False)
```

time: 127 us -> 89 us (0.70)
  the two profiles are of different devices: /device:TPU:6 before, /device:TPU:100 now
where the time goes in v1:
time: 89 us; the launch traced here: 88.6 us
  waiting for transfers between devices  41.7 us (47%)
  blocking collectives  18.5 us (21%)
  starting transfers between devices  11.7 us (13%)
  Pallas kernels  10.8 us (12%)
  local copies, waits for them, and re-layouts  3.87 us (4%)
  other arithmetic  1.53 us (2%)
    ppermute x1, waiting for transfers between devices, shards(): up = lax.ppermute(latent, 'lat', north)  20.8 us
    all_to_all x1, blocking collectives, exchange(): return lax.all_to_all(x, 'lead', split_axis=0, concat_axis=0, tiled=True)  18.5 us
    all_to_all x1, waiting for transfers between devices, exchange(): return lax.all_to_all(x, 'lead', split_axis=0, concat_axis=0, tiled=True)  15.7 us
    pallas_call x1, Pallas kernels, attend(): pl.pallas_call(functools.partial(attend_kernel, math.gcd(pixels, 8)), out...  6.47 us
    ppermute x1, waiting for transfers between devices, shards(): down = lax.ppermute(latent, 'lat', south)  5.22 us
    ppermute x1, starting transfers between devices, shards(): up = lax.ppermute(latent, 'lat', north)  5.16 us
    all_to_all x1, starting transfers between devices, exchange(): return lax.all_to_all(x, 'lead', split_axis=0, concat_axis=0, tiled=True)  4.6 us
    pallas_call x1, Pallas kernels, conv_norm(): pl.pallas_call(functools.partial(conv_kernel, tile, start - low, low), ou...  4.31 us
  transfers between devices with their start and end apart: 3, of which 3 were waited for; matrix products, arithmetic and copies ran while one was open for 0% of the time, Pallas kernels for 0%

profile of v1, /device:TPU:100, one launch (start us, length us, event | category | flops | bytes accessed | tf_op | source)
XLA Modules:
  0.0 88.6 jit_solution(2175379120905295783)
XLA Ops:
  0.0 0.0 copy-start
  0.0 5.2 %collective-permute-start = (bf16[256,8,256]{2,1,0:T(8,128)(2,1)}, bf16[256,8,256]{2,1,0:T(8,128)(2,1)S(1)}, u32[]{:S(2)}, u32[]{:S(2)}) collective-permute-start(bf16[256,8,256]{2,1,0:T(8,128)(2,1)} %bitcast.14), channel_id=1, source_target_pairs={{0,8},{8,16},{16,24},{24,32},{32,40},{40,48},{48,56},{56,64},{64,7... | collective-permute-start | bytes 3145736 | tf_op jit(solution)/shard_map/ppermute | solution.py:170
  5.2 1.9 %collective-permute-start.1 = (bf16[256,8,256]{2,1,0:T(8,128)(2,1)}, bf16[256,8,256]{2,1,0:T(8,128)(2,1)S(1)}, u32[]{:S(2)}, u32[]{:S(2)}) collective-permute-start(bf16[256,8,256]{2,1,0:T(8,128)(2,1)} %bitcast.15), channel_id=1, source_target_pairs={{8,0},{16,8},{24,16},{32,24},{40,32},{48,40},{56,48},{64,56},{72,6... | collective-permute-start | bytes 3145736 | tf_op jit(solution)/shard_map/ppermute | solution.py:171
  7.1 20.8 %collective-permute-done.up = bf16[256,8,256]{2,1,0:T(8,128)(2,1)S(1)} collective-permute-done((bf16[256,8,256]{2,1,0:T(8,128)(2,1)}, bf16[256,8,256]{2,1,0:T(8,128)(2,1)S(1)}, u32[]{:S(2)}, u32[]{:S(2)}) %collective-permute-start) | collective-permute-done | bytes 1048608 | tf_op jit(solution)/shard_map/ppermute | solution.py:170
  27.9 5.2 %collective-permute-done.1.down = bf16[256,8,256]{2,1,0:T(8,128)(2,1)S(1)} collective-permute-done((bf16[256,8,256]{2,1,0:T(8,128)(2,1)}, bf16[256,8,256]{2,1,0:T(8,128)(2,1)S(1)}, u32[]{:S(2)}, u32[]{:S(2)}) %collective-permute-start.1) | collective-permute-done | bytes 1048608 | tf_op jit(solution)/shard_map/ppermute | solution.py:171
  33.1 0.0 copy-start.1
  33.1 1.3 %copy-done.1 = bf16[3,3,256,256]{3,2,1,0:T(8,128)(2,1)S(1)} copy-done((bf16[3,3,256,256]{3,2,1,0:T(8,128)(2,1)S(1)}, bf16[3,3,256,256]{3,2,1,0:T(8,128)(2,1)}, u32[]{:S(2)}) %copy-start.1) | copy-done | bytes 1179672
  34.4 0.0 copy-start.2
  34.4 1.2 %copy-done.2 = bf16[1,256,8,256]{3,2,1,0:T(8,128)(2,1)S(1)} copy-done((bf16[1,256,8,256]{3,2,1,0:T(8,128)(2,1)S(1)}, bf16[1,256,8,256]{3,2,1,0:T(8,128)(2,1)}, u32[]{:S(2)}) %copy-start.2) | copy-done | bytes 1048600
  35.6 0.0 copy-start.3
  35.6 0.7 copy-done.3
  36.3 0.0 copy-start.4
  36.3 0.7 copy-done.4
  37.0 4.3 %shard_map.82 = (bf16[256,8,256]{2,1,0:T(8,128)(2,1)S(1)}, bf16[256,8,256]{2,1,0:T(8,128)(2,1)}) custom-call(bf16[256,8,256]{2,1,0:T(8,128)(2,1)S(1)} %collective-permute-done.up, bf16[256,8,256]{2,1,0:T(8,128)(2,1)S(1)} %bitcast.16, bf16[256,8,256]{2,1,0:T(8,128)(2,1)S(1)} %collective-permute-done.1.down, bf16[2304,256]{1,0:T(8,128)(2,1)S(1)} %bitcast.13, ...), custom_call_target="tpu_custom_call" | custom-call | flops 2415919104 | bytes 6422528 | tf_op jit(solution)/shard_map/pallas_call | solution.py:82
  41.3 0.0 copy-start.5
  41.3 0.0 copy-start.6
  41.3 0.0 copy-start.7
  41.3 4.6 %all-to-all-start = ((bf16[8,32,8,256]{3,2,1,0:T(8,128)(2,1)}), bf16[8,32,8,256]{3,2,1,0:T(8,128)(2,1)S(1)}, u32[]{:S(2)}, u32[]{:S(2)}) async-start(bf16[8,32,8,256]{3,2,1,0:T(8,128)(2,1)} %bitcast.5), calls=%async_computation | async-start | bytes 2097152 | tf_op jit(solution)/shard_map/all_to_all | solution.py:155
  45.9 0.0 copy-done.5
  45.9 0.0 copy-done.6
  45.9 0.0 copy-done.7
  46.0 0.1 compare_convert_fusion.ones_ref
  46.1 15.7 %all-to-all-done.x_ref = bf16[8,32,8,256]{3,2,1,0:T(8,128)(2,1)S(1)} async-done(((bf16[8,32,8,256]{3,2,1,0:T(8,128)(2,1)}), bf16[8,32,8,256]{3,2,1,0:T(8,128)(2,1)S(1)}, u32[]{:S(2)}, u32[]{:S(2)}) %all-to-all-start) | async-done | bytes 1048608 | tf_op jit(solution)/shard_map/all_to_all | solution.py:155
  61.8 6.5 %shard_map.83 = bf16[8,32,8,256]{3,2,1,0:T(8,128)(2,1)S(1)} custom-call(bf16[8,32,8,256]{3,2,1,0:T(8,128)(2,1)S(1)} %all-to-all-done.x_ref, bf16[256,768]{1,0:T(8,128)(2,1)S(1)} %pad_maximum_fusion.w_ref, bf16[512,256]{1,0:T(8,128)(2,1)S(1)} %compare_convert_fusion.ones_ref), custom_call_target="tpu_custom_call" | custom-call | flops 2684354560 | bytes 2490368 | tf_op jit(solution)/shard_map/pallas_call | solution.py:144
  68.3 18.5 %all_to_all.10 = bf16[8,32,8,256]{3,2,1,0:T(8,128)(2,1)S(1)} all-to-all(bf16[8,32,8,256]{3,2,1,0:T(8,128)(2,1)S(1)} %shard_map.83), channel_id=1, replica_groups=mesh['lat'=32,'lead'=8] {'lead'}, dimensions={0} | all-to-all | bytes 2097152 | tf_op jit(solution)/shard_map/all_to_all | solution.py:155
  86.8 0.0 copy-done
  86.8 0.4 fusion.5
  87.3 1.4 %fusion.1 = bf16[1,256,8,256]{3,2,1,0:T(8,128)(2,1)} fusion(f32[2048,256]{1,0:T(8,128)S(1)} %fusion.5, bf16[256,8,256]{2,1,0:T(8,128)(2,1)S(1)} %get-tuple-element.7), kind=kLoop, calls=%fused_computation.2 | loop fusion | flops 1572864 | bytes 4194304 | tf_op jit(solution)/shard_map/reshape | solution.py:176
  (3 shorter events, 0.0 us)
Async XLA Ops:
  0.0 86.8 %copy-start = (bf16[256,256]{1,0:T(8,128)(2,1)S(1)}, bf16[256,256]{1,0:T(8,128)(2,1)}, u32[]{:S(2)}) copy-start(bf16[256,256]{1,0:T(8,128)(2,1)} %param.15) | copy-start | bytes 393220
  0.0 27.9 %collective-permute-start = (bf16[256,8,256]{2,1,0:T(8,128)(2,1)}, bf16[256,8,256]{2,1,0:T(8,128)(2,1)S(1)}, u32[]{:S(2)}, u32[]{:S(2)}) collective-permute-start(bf16[256,8,256]{2,1,0:T(8,128)(2,1)} %bitcast.14), channel_id=1, source_target_pairs={{0,8},{8,16},{16,24},{24,32},{32,40},{40,48},{48,56},{56,64},{64,7... | collective-permute-start | bytes 3145736 | tf_op jit(solution)/shard_map/ppermute | solution.py:170
  5.2 27.9 %collective-permute-start.1 = (bf16[256,8,256]{2,1,0:T(8,128)(2,1)}, bf16[256,8,256]{2,1,0:T(8,128)(2,1)S(1)}, u32[]{:S(2)}, u32[]{:S(2)}) collective-permute-start(bf16[256,8,256]{2,1,0:T(8,128)(2,1)} %bitcast.15), channel_id=1, source_target_pairs={{8,0},{16,8},{24,16},{32,24},{40,32},{48,40},{56,48},{64,56},{72,6... | collective-permute-start | bytes 3145736 | tf_op jit(solution)/shard_map/ppermute | solution.py:171
  33.1 1.3 %copy-start.1 = (bf16[3,3,256,256]{3,2,1,0:T(8,128)(2,1)S(1)}, bf16[3,3,256,256]{3,2,1,0:T(8,128)(2,1)}, u32[]{:S(2)}) copy-start(bf16[3,3,256,256]{3,2,1,0:T(8,128)(2,1)} %param.9) | copy-start | bytes 3538948
  34.4 1.2 %copy-start.2 = (bf16[1,256,8,256]{3,2,1,0:T(8,128)(2,1)S(1)}, bf16[1,256,8,256]{3,2,1,0:T(8,128)(2,1)}, u32[]{:S(2)}) copy-start(bf16[1,256,8,256]{3,2,1,0:T(8,128)(2,1)} %param.8) | copy-start | bytes 3145732
  35.6 0.7 copy-start.3
  36.3 0.7 copy-start.4
  41.3 4.6 %copy-start.5 = (bf16[256,256]{1,0:T(8,128)(2,1)S(1)}, bf16[256,256]{1,0:T(8,128)(2,1)}, u32[]{:S(2)}) copy-start(bf16[256,256]{1,0:T(8,128)(2,1)} %param.14) | copy-start | bytes 393220
  41.3 4.6 %copy-start.6 = (bf16[256,256]{1,0:T(8,128)(2,1)S(1)}, bf16[256,256]{1,0:T(8,128)(2,1)}, u32[]{:S(2)}) copy-start(bf16[256,256]{1,0:T(8,128)(2,1)} %param.13) | copy-start | bytes 393220
  41.3 4.6 %copy-start.7 = (bf16[256,256]{1,0:T(8,128)(2,1)S(1)}, bf16[256,256]{1,0:T(8,128)(2,1)}, u32[]{:S(2)}) copy-start(bf16[256,256]{1,0:T(8,128)(2,1)} %param.12) | copy-start | bytes 393220
  41.3 20.6 %all-to-all-start = ((bf16[8,32,8,256]{3,2,1,0:T(8,128)(2,1)}), bf16[8,32,8,256]{3,2,1,0:T(8,128)(2,1)S(1)}, u32[]{:S(2)}, u32[]{:S(2)}) async-start(bf16[8,32,8,256]{3,2,1,0:T(8,128)(2,1)} %bitcast.5), calls=%async_computation | async-start | bytes 2097152 | tf_op jit(solution)/shard_map/all_to_all | solution.py:155

commit v2 on v1

v2 whole, which is shorter than its diff:
```python
import functools
import math

import jax
import jax.numpy as jnp
from jax import lax
from jax.experimental import pallas as pl
from jax.experimental.pallas import tpu as pltpu
from jax.sharding import PartitionSpec as P

HD = 32
NT = (((1,), (1,)), ((), ()))
F32 = jnp.float32
BF16 = jnp.bfloat16
Q_SCALE = math.log2(math.e) / math.sqrt(HD)
VMEM = pl.BlockSpec(memory_space=pltpu.VMEM)
SMEM = pl.BlockSpec(memory_space=pltpu.SMEM)
ANY = pl.BlockSpec(memory_space=pl.ANY)
WIDTHS = (128, 128)


def in_vmem(*arrays):
    return [pltpu.with_memory_space_constraint(x, pltpu.VMEM) for x in arrays]


def params(mib):
    return pltpu.CompilerParams(vmem_limit_bytes=mib << 20)


def cost(flops, nbytes, transcendentals=0):
    return pl.CostEstimate(
        flops=int(flops), bytes_accessed=int(nbytes), transcendentals=int(transcendentals)
    )


def gelu(x):
    return 0.5 * x * (1.0 + jnp.tanh(math.sqrt(2 / math.pi) * (x + 0.044715 * (x * x * x))))


def layer_norm(hidden, gain):
    hidden = hidden.astype(F32)
    centred = hidden - jnp.mean(hidden, axis=-1, keepdims=True)
    var = jnp.mean(centred * centred, axis=-1, keepdims=True)
    return (centred * lax.rsqrt(var + 1e-05) * gain).astype(BF16)


def taps(ref, start, count):
    size, leads, chans = ref.shape
    zero = jnp.zeros((1, leads, chans), ref.dtype)
    out = []
    for first in (start - 1, start, start + 1):
        low, high = max(first, 0), min(first + count, size)
        piece = ref[low:high]
        if low > first:
            piece = jnp.concatenate([zero, piece], axis=0)
        if high < first + count:
            piece = jnp.concatenate([piece, zero], axis=0)
        out.append(piece.reshape(count * leads, chans))
    return jnp.concatenate(out, axis=1)


def row_weight(weight, row):
    return weight[3 * row : 3 * row + 3].reshape(3 * weight.shape[1], weight.shape[2])


def centre_kernel(tile, pieces, mid, weight, bias, out, *piece_refs):
    width, leads, chans = mid.shape
    for (low, high), piece in zip(pieces, piece_refs):
        piece[...] = mid[low:high]
    for i in range(width // tile):
        acc = jnp.dot(taps(mid, i * tile, tile), row_weight(weight, 1), preferred_element_type=F32)
        out[i * tile * leads : (i + 1) * tile * leads] = acc + bias[...]


def centre_conv(mid, weight, bias, pieces):
    width, leads, chans = mid.shape
    rows = width * leads
    return pl.pallas_call(
        functools.partial(centre_kernel, 32, pieces),
        out_shape=[pltpu.VMEM((rows, chans), F32)]
        + [pltpu.VMEM((high - low, leads, chans), BF16) for low, high in pieces],
        in_specs=[VMEM] * 3,
        out_specs=[VMEM] * (1 + len(pieces)),
        compiler_params=params(8),
        cost_estimate=cost(rows * chans * 6 * chans, rows * chans * 6),
    )(mid, weight, bias)


def place(lead, parts, k):
    chip, core = lax.div(lead, 2), lax.rem(lead, 2)
    return 2 * lax.rem(chip + k // 2, parts // 2) + (core if k % 2 == 0 else 1 - core)


def conv_kernel(tile, offset, start, lats, ids, up, down, acc_in, weight, gain, hidden_out, *refs):
    normed_out, (hidden, normed) = refs[:-2], refs[-2:]
    width, leads, chans = hidden.shape
    parts = 2 * len(normed_out)
    first, last = ids[0] == 0, ids[0] == lats - 1

    def conv(i):
        high, low = taps(up, i * tile + offset, tile), taps(down, i * tile + offset, tile)
        high = jnp.where(first, jnp.zeros_like(high), high)
        low = jnp.where(last, jnp.zeros_like(low), low)
        acc = jnp.dot(high, row_weight(weight, 0), preferred_element_type=F32)
        return acc + jnp.dot(low, row_weight(weight, 2), preferred_element_type=F32)

    def finish(i, acc):
        here = slice(i * tile, (i + 1) * tile)
        begin = (start + i * tile) * leads
        value = gelu(acc + acc_in[begin : begin + tile * leads]).astype(BF16)
        normed[here] = layer_norm(value, gain[...]).reshape(tile, leads, chans)
        hidden[here] = value.reshape(tile, leads, chans)

    acc = conv(0)
    for i in range(width // tile):
        later = conv(i + 1) if (i + 1) * tile < width else None
        finish(i, acc)
        acc = later
    count = width // parts
    for k in range(parts):
        there = pl.ds(place(ids[1], parts, k) * count, count)
        hidden_out[k] = hidden[there]
        normed_out[k // 2][k % 2] = normed[there]


def conv_norm(lats, parts, ids, up, down, acc, weight, gain, start, width):
    _, leads, chans = up.shape
    low = max(start - 1, 0)
    tile = math.gcd(width, 32)
    size = width * leads * chans
    part = (width // parts, leads, chans)
    out = pl.pallas_call(
        functools.partial(conv_kernel, tile, start - low, start, lats),
        out_shape=[pltpu.VMEM((parts, *part), BF16)]
        + [pltpu.VMEM((2, *part), BF16)] * (parts // 2),
        in_specs=[SMEM] + [VMEM] * 5,
        out_specs=[VMEM] * (1 + parts // 2),
        scratch_shapes=[pltpu.VMEM((width, leads, chans), BF16)] * 2,
        compiler_params=params(12),
        cost_estimate=cost(size * 12 * chans, size * 12, size),
    )(ids, *in_vmem(up, down, acc), weight, gain)
    return out[0], out[1:]


def attend_kernel(block, wq_ref, wk_ref, wv_ref, *refs):
    ones_ref, chips = refs[-1], len(refs) // 2 - 1
    near, far, outs = refs[:chips], refs[chips], refs[chips + 1 : -1]
    xs = [x for k in range(chips) for x in (near[k].at[0], far.at[k])]
    parts, (pixels, leads, chans) = len(xs), xs[0].shape
    times, heads = parts * leads, chans // HD
    lane = lax.broadcasted_iota(jnp.int32, (times, chans), 1)
    masks = [(lane >= h * HD) & (lane < (h + 1) * HD) for h in range(heads)]
    low_half = lax.broadcasted_iota(jnp.int32, (times, 2 * times), 1) < times
    for h in range(heads):
        ones_ref[h * times : (h + 1) * times] = masks[h].astype(F32).astype(BF16)

    def by_head(x):
        return jnp.concatenate([jnp.where(m, x, jnp.zeros_like(x)) for m in masks], axis=0)

    def soft(scores):
        out = []
        for i in range(heads // 2):
            pair = scores[:, 2 * times * i : 2 * times * (i + 1)]
            top0 = jnp.max(jnp.where(low_half, pair, -jnp.inf), axis=1, keepdims=True)
            top1 = jnp.max(jnp.where(low_half, -jnp.inf, pair), axis=1, keepdims=True)
            out.append(jnp.exp2(pair - jnp.where(low_half, top0, top1)).astype(BF16))
        return jnp.concatenate(out, axis=1)

    for i in range(pixels // block):
        first = i * block
        x = jnp.concatenate([x_ref[first : first + block] for x_ref in xs], axis=0)
        x = x.reshape(parts * block * leads, chans)

        def project(w_ref, scale=None):
            flat = jnp.dot(x, w_ref[...], preferred_element_type=F32)
            flat = (flat if scale is None else flat * scale).astype(BF16)
            rows = flat.reshape(parts, block, leads, chans)
            return [rows[:, p].reshape(times, chans) for p in range(block)]

        query, keys, values = project(wq_ref, Q_SCALE), project(wk_ref), project(wv_ref)
        scores = [
            lax.dot_general(q, by_head(k), NT, preferred_element_type=F32)
            for q, k in zip(query, keys)
        ]
        expo = [soft(s) for s in scores]
        total = jnp.dot(jnp.concatenate(expo, axis=0), ones_ref[...], preferred_element_type=F32)
        mixed = [jnp.dot(e, by_head(v), preferred_element_type=F32) for e, v in zip(expo, values)]
        for p in range(block):
            attended = mixed[p] / total[p * times : (p + 1) * times]
            attended = attended.astype(BF16).reshape(parts, leads, chans)
            for k in range(parts):
                outs[k // 2][k % 2, first + p] = attended[k]


def attend(near, far, w_query, w_key, w_value):
    chips, pixels, leads, chans = far.shape
    size, times = 2 * far.size, 2 * chips * leads
    return pl.pallas_call(
        functools.partial(attend_kernel, math.gcd(pixels, 8)),
        out_shape=[pltpu.VMEM(near[0].shape, BF16)] * chips,
        in_specs=[VMEM] * (4 + chips),
        out_specs=[VMEM] * chips,
        scratch_shapes=[pltpu.VMEM((chans // HD * times, chans), BF16)],
        compiler_params=params(16),
        cost_estimate=cost(size * chans * 20, size * 4 + 6 * chans * chans, size * 2),
    )(w_query, w_key, w_value, *in_vmem(*near, far))


def out_kernel(start, ids, hidden_ref, w_ref, *refs):
    out_hbm, held, sems = refs[-3:]
    parts, count, leads, chans = hidden_ref.shape
    near, far = refs[: parts // 2], refs[parts // 2]
    copies = []
    for k in range(parts):
        x = near[k // 2][0] if k % 2 == 0 else far[k // 2]
        acc = jnp.dot(x.reshape(count * leads, chans), w_ref[...], preferred_element_type=F32)
        acc = acc + hidden_ref[k].reshape(count * leads, chans).astype(F32)
        held[k] = acc.astype(BF16).reshape(count, leads, chans)
    for k in range(parts):
        there = pl.ds(start + place(ids[1], parts, k) * count, count)
        copies.append(pltpu.make_async_copy(held.at[k], out_hbm.at[there], sems.at[k]))
        copies[-1].start()
    for copy in copies:
        copy.wait()


def project_out(ids, near, far, hidden, w_out, whole, start, total):
    parts, _, leads, chans = hidden.shape
    args = [ids, *in_vmem(hidden), w_out, *in_vmem(*near, far)] + ([] if whole is None else [whole])
    return pl.pallas_call(
        functools.partial(out_kernel, start),
        out_shape=jax.ShapeDtypeStruct((total, leads, chans), BF16),
        in_specs=[SMEM] + [VMEM] * (3 + len(near)) + ([] if whole is None else [ANY]),
        out_specs=ANY,
        scratch_shapes=[pltpu.VMEM(hidden.shape, BF16), pltpu.SemaphoreType.DMA((parts,))],
        input_output_aliases={} if whole is None else {4 + len(near): 0},
        compiler_params=params(8),
        cost_estimate=cost(hidden.size * 2 * chans, hidden.size * 6),
    )(*args)


def gather_kernel(*refs):
    for k, ref in enumerate(refs[:-1]):
        refs[-1][k] = ref[1]


def ship(pieces, sign):
    chips = len(pieces)
    near = [pieces[0]] + [
        lax.ppermute(
            pieces[k], "lead", [(i, (i + 2 * sign * k) % (2 * chips)) for i in range(2 * chips)]
        )
        for k in range(1, chips)
    ]
    part = pieces[0].shape[1:]
    others = pl.pallas_call(
        gather_kernel,
        out_shape=pltpu.VMEM((chips, *part), BF16),
        in_specs=[VMEM] * chips,
        out_specs=VMEM,
        compiler_params=params(4),
        cost_estimate=cost(0, chips * pieces[0].size * 2),
    )(*in_vmem(*near))
    return near, lax.ppermute(others, "lead", [(i, i ^ 1) for i in range(2 * chips)])


def shards(latent, conv_weight, conv_bias, norm_gain, w_query, w_key, w_value, w_out):
    latent = latent[0]
    width, leads, chans = latent.shape
    lats, parts = lax.axis_size("lat"), lax.axis_size("lead")
    w_conv = conv_weight.reshape(9, chans, chans)
    bias, gain = conv_bias.reshape(1, chans), norm_gain.reshape(1, chans)
    north = [(i, (i + 1) % lats) for i in range(lats)]
    south = [(i, (i - 1) % lats) for i in range(lats)]
    ids = jnp.stack([lax.axis_index("lat"), lax.axis_index("lead")])

    starts = [sum(WIDTHS[:i]) for i in range(len(WIDTHS))]
    ranges = [(max(i - 1, 0), min(i + n + 1, width)) for i, n in zip(starts, WIDTHS)]
    acc, *pieces = centre_conv(latent, w_conv, bias, ranges[1:])
    sides = [
        (lax.ppermute(piece, "lat", north), lax.ppermute(piece, "lat", south))
        for piece in [latent[: ranges[0][1]], *pieces]
    ]
    hiddens, blocks = [], []
    for (up, down), start, count in zip(sides, starts, WIDTHS):
        hidden, normed = conv_norm(lats, parts, ids, up, down, acc, w_conv, gain, start, count)
        hiddens.append(hidden)
        blocks.append(ship(normed, 1))
    backs = [ship(attend(*block, w_query, w_key, w_value), -1) for block in blocks]
    out = None
    for back, hidden, start in zip(backs, hiddens, starts):
        out = project_out(ids, *back, hidden, w_out, out, start, width)
    return out[None]


def solution(mesh):
    in_specs = (P("lat", None, "lead", None), P(), P(), P(), P(), P(), P(), P())
    out_specs = P("lat", None, "lead", None)
    return jax.shard_map(shards, mesh=mesh, in_specs=in_specs, out_specs=out_specs, check_vma=False)
```

time: 89 us -> 78.3 us (0.88)
  the two profiles are of different devices: /device:TPU:100 before, /device:TPU:1 now
where the time goes in v2:
time: 78.3 us; the launch traced here: 78 us
  starting transfers between devices  37.9 us (48%)
  waiting for transfers between devices  17.9 us (23%)
  Pallas kernels  16.8 us (21%)
  local copies, waits for them, and re-layouts  5.07 us (6%)
    ppermute x12, starting transfers between devices, ship(): lax.ppermute(pieces[k], 'lead', [(i, (i + 2 * sign * k) % (2 * chips)) fo...  17 us
    ppermute x2, starting transfers between devices, shards(): lax.ppermute(piece, 'lat', south)  13.4 us
    ppermute x2, waiting for transfers between devices, shards(): lax.ppermute(piece, 'lat', north)  8.74 us
    ppermute x12, waiting for transfers between devices, ship(): lax.ppermute(pieces[k], 'lead', [(i, (i + 2 * sign * k) % (2 * chips)) fo...  7.94 us
    ppermute x4, starting transfers between devices, ship(): lax.ppermute(others, 'lead', [(i, i ^ 1) for i in range(2 * chips)])  7.45 us
    pallas_call x2, Pallas kernels, attend(): pl.pallas_call(functools.partial(attend_kernel, math.gcd(pixels, 8)), out...  6.24 us
    pallas_call x2, Pallas kernels, conv_norm(): pl.pallas_call(functools.partial(conv_kernel, tile, start - low, start, l...  5.39 us
    pallas_call x2, Pallas kernels, project_out(): pl.pallas_call(functools.partial(out_kernel, start), out_shape=jax.ShapeD...  3.41 us
  transfers between devices with their start and end apart: 20, of which 8 were waited for; matrix products, arithmetic and copies ran while one was open for 0% of the time, Pallas kernels for 19%

profile of v2, /device:TPU:1, one launch (start us, length us, event | category | flops | bytes accessed | tf_op | source)
XLA Modules:
  0.0 78.0 jit_solution(18291734798492180704)
XLA Ops:
  0.0 0.0 copy-start.4
  0.0 1.9 %slice_bitcast_fusion = bf16[129,8,256]{2,1,0:T(8,128)(2,1)} fusion(bf16[1,256,8,256]{3,2,1,0:T(8,128)(2,1)} %param.8), kind=kLoop, calls=%fused_computation | loop fusion | bytes 1056768 | tf_op jit(solution)/shard_map/slice | solution.py:282
  1.9 8.6 %collective-permute-start.11 = (bf16[129,8,256]{2,1,0:T(8,128)(2,1)}, bf16[129,8,256]{2,1,0:T(8,128)(2,1)}, u32[]{:S(2)}, u32[]{:S(2)}) collective-permute-start(bf16[129,8,256]{2,1,0:T(8,128)(2,1)} %slice_bitcast_fusion), channel_id=1, source_target_pairs={{0,248},{8,0},{16,8},{24,16},{32,24},{40,32},{48,40},{56,48},{64,5... | collective-permute-start | bytes 1585160 | tf_op jit(solution)/shard_map/ppermute | solution.py:281
  10.5 0.0 collective-permute-start.10
  10.5 0.0 copy-start
  10.5 1.3 %copy-done = bf16[3,3,256,256]{3,2,1,0:T(8,128)(2,1)S(1)} copy-done((bf16[3,3,256,256]{3,2,1,0:T(8,128)(2,1)S(1)}, bf16[3,3,256,256]{3,2,1,0:T(8,128)(2,1)}, u32[]{:S(2)}) %copy-start) | copy-done | bytes 1179672
  11.8 1.2 %copy-done.3 = bf16[1,256,8,256]{3,2,1,0:T(8,128)(2,1)S(1)} copy-done((bf16[1,256,8,256]{3,2,1,0:T(8,128)(2,1)S(1)}, bf16[1,256,8,256]{3,2,1,0:T(8,128)(2,1)}, u32[]{:S(2)}) %copy-start.3) | copy-done | bytes 1048600
  13.0 0.0 copy-start.8
  13.0 0.7 copy-done.8
  13.7 0.0 copy-start.1
  13.7 1.7 %shard_map.82 = (f32[2048,256]{1,0:T(8,128)S(1)}, bf16[129,8,256]{2,1,0:T(8,128)(2,1)}) custom-call(bf16[256,8,256]{2,1,0:T(8,128)(2,1)S(1)} %bitcast.12, bf16[9,256,256]{2,1,0:T(8,128)(2,1)S(1)} %bitcast.9, f32[1,256]{1,0:T(1,128)S(1)} %bitcast.15), custom_call_target="tpu_custom_call" | custom-call | flops 805306368 | bytes 3145728 | tf_op jit(solution)/shard_map/pallas_call | solution.py:78
  15.4 4.8 %collective-permute-start.1 = (bf16[129,8,256]{2,1,0:T(8,128)(2,1)}, bf16[129,8,256]{2,1,0:T(8,128)(2,1)}, u32[]{:S(2)}, u32[]{:S(2)}) collective-permute-start(bf16[129,8,256]{2,1,0:T(8,128)(2,1)} %get-tuple-element.25), channel_id=1, source_target_pairs={{0,248},{8,0},{16,8},{24,16},{32,24},{40,32},{48,40},{56,48},{64,5... | collective-permute-start | bytes 1585160 | tf_op jit(solution)/shard_map/ppermute | solution.py:281
  20.2 0.0 collective-permute-start
  20.2 0.1 pad_add_fusion.ids
  20.3 1.2 %collective-permute-done.11.down = bf16[129,8,256]{2,1,0:T(8,128)(2,1)} collective-permute-done((bf16[129,8,256]{2,1,0:T(8,128)(2,1)}, bf16[129,8,256]{2,1,0:T(8,128)(2,1)}, u32[]{:S(2)}, u32[]{:S(2)}) %collective-permute-start.11) | collective-permute-done | bytes 528416 | tf_op jit(solution)/shard_map/ppermute | solution.py:281
  21.5 5.2 %collective-permute-done.10.up = bf16[129,8,256]{2,1,0:T(8,128)(2,1)} collective-permute-done((bf16[129,8,256]{2,1,0:T(8,128)(2,1)}, bf16[129,8,256]{2,1,0:T(8,128)(2,1)}, u32[]{:S(2)}, u32[]{:S(2)}) %collective-permute-start.10) | collective-permute-done | bytes 528416 | tf_op jit(solution)/shard_map/ppermute | solution.py:281
  26.7 0.0 copy-done.4
  26.7 0.0 copy-done.1
  26.7 2.7 %shard_map.87 = (bf16[8,16,8,256]{3,2,1,0:T(8,128)(2,1)S(1)}, bf16[2,16,8,256]{3,2,1,0:T(8,128)(2,1)S(1)}, bf16[2,16,8,256]{3,2,1,0:T(8,128)(2,1)S(1)}, bf16[2,1...) custom-call(s32[2]{0:T(128)S(1)} %pad_add_fusion.ids, bf16[129,8,256]{2,1,0:T(8,128)(2,1)} %collective-permute-done.10.up, ...), custom_call_target="tpu_custom_call" | custom-call | flops 805306368 | bytes 3145728 | tf_op jit(solution)/shard_map/pallas_call | solution.py:132
  29.4 1.4 %collective-permute-start.12 = (bf16[2,16,8,256]{3,2,1,0:T(8,128)(2,1)S(1)}, bf16[2,16,8,256]{3,2,1,0:T(8,128)(2,1)S(1)}, u32[]{:S(2)}, u32[]{:S(2)}) collective-permute-start(bf16[2,16,8,256]{3,2,1,0:T(8,128)(2,1)S(1)} %get-tuple-element.38), channel_id=1, source_target_pairs={{0,2},{1,3},{2,4},{3,5},{4,6},{5,7},{6,0},{7,1},{8,10},{9,11},{10,... | collective-permute-start | bytes 393224 | tf_op jit(solution)/shard_map/ppermute | solution.py:250
  30.8 2.6 %collective-permute-start.13 = (bf16[2,16,8,256]{3,2,1,0:T(8,128)(2,1)S(1)}, bf16[2,16,8,256]{3,2,1,0:T(8,128)(2,1)S(1)}, u32[]{:S(2)}, u32[]{:S(2)}) collective-permute-start(bf16[2,16,8,256]{3,2,1,0:T(8,128)(2,1)S(1)} %get-tuple-element.39), channel_id=1, source_target_pairs={{0,4},{1,5},{2,6},{3,7},{4,0},{5,1},{6,2},{7,3},{8,12},{9,13},{10,... | collective-permute-start | bytes 393224 | tf_op jit(solution)/shard_map/ppermute | solution.py:250
  33.4 0.0 copy-start.6
  33.4 0.0 copy-start.7
  33.4 1.1 %collective-permute-start.14 = (bf16[2,16,8,256]{3,2,1,0:T(8,128)(2,1)S(1)}, bf16[2,16,8,256]{3,2,1,0:T(8,128)(2,1)S(1)}, u32[]{:S(2)}, u32[]{:S(2)}) collective-permute-start(bf16[2,16,8,256]{3,2,1,0:T(8,128)(2,1)S(1)} %get-tuple-element.40), channel_id=1, source_target_pairs={{0,6},{1,7},{2,0},{3,1},{4,2},{5,3},{6,4},{7,5},{8,14},{9,15},{10,... | collective-permute-start | bytes 393224 | tf_op jit(solution)/shard_map/ppermute | solution.py:250
  34.5 0.0 collective-permute-done.1.down
  34.5 3.5 %collective-permute-done.up = bf16[129,8,256]{2,1,0:T(8,128)(2,1)} collective-permute-done((bf16[129,8,256]{2,1,0:T(8,128)(2,1)}, bf16[129,8,256]{2,1,0:T(8,128)(2,1)}, u32[]{:S(2)}, u32[]{:S(2)}) %collective-permute-start) | collective-permute-done | bytes 528416 | tf_op jit(solution)/shard_map/ppermute | solution.py:281
  38.0 2.7 %shard_map.83 = (bf16[8,16,8,256]{3,2,1,0:T(8,128)(2,1)S(1)}, bf16[2,16,8,256]{3,2,1,0:T(8,128)(2,1)S(1)}, bf16[2,16,8,256]{3,2,1,0:T(8,128)(2,1)S(1)}, bf16[2,1...) custom-call(s32[2]{0:T(128)S(1)} %pad_add_fusion.ids, bf16[129,8,256]{2,1,0:T(8,128)(2,1)} %collective-permute-done.up, ...), custom_call_target="tpu_custom_call" | custom-call | flops 805306368 | bytes 3145728 | tf_op jit(solution)/shard_map/pallas_call | solution.py:132
  40.7 1.4 %collective-permute-start.2 = (bf16[2,16,8,256]{3,2,1,0:T(8,128)(2,1)S(1)}, bf16[2,16,8,256]{3,2,1,0:T(8,128)(2,1)S(1)}, u32[]{:S(2)}, u32[]{:S(2)}) collective-permute-start(bf16[2,16,8,256]{3,2,1,0:T(8,128)(2,1)S(1)} %get-tuple-element.29), channel_id=1, source_target_pairs={{0,2},{1,3},{2,4},{3,5},{4,6},{5,7},{6,0},{7,1},{8,10},{9,11},{10,... | collective-permute-start | bytes 393224 | tf_op jit(solution)/shard_map/ppermute | solution.py:250
  42.1 2.6 %collective-permute-start.3 = (bf16[2,16,8,256]{3,2,1,0:T(8,128)(2,1)S(1)}, bf16[2,16,8,256]{3,2,1,0:T(8,128)(2,1)S(1)}, u32[]{:S(2)}, u32[]{:S(2)}) collective-permute-start(bf16[2,16,8,256]{3,2,1,0:T(8,128)(2,1)S(1)} %get-tuple-element.30), channel_id=1, source_target_pairs={{0,4},{1,5},{2,6},{3,7},{4,0},{5,1},{6,2},{7,3},{8,12},{9,13},{10,... | collective-permute-start | bytes 393224 | tf_op jit(solution)/shard_map/ppermute | solution.py:250
  44.7 0.0 collective-permute-done.12.refs_1_
  44.7 1.1 %collective-permute-start.4 = (bf16[2,16,8,256]{3,2,1,0:T(8,128)(2,1)S(1)}, bf16[2,16,8,256]{3,2,1,0:T(8,128)(2,1)S(1)}, u32[]{:S(2)}, u32[]{:S(2)}) collective-permute-start(bf16[2,16,8,256]{3,2,1,0:T(8,128)(2,1)S(1)} %get-tuple-element.31), channel_id=1, source_target_pairs={{0,6},{1,7},{2,0},{3,1},{4,2},{5,3},{6,4},{7,5},{8,14},{9,15},{10,... | collective-permute-start | bytes 393224 | tf_op jit(solution)/shard_map/ppermute | solution.py:250
  45.8 0.0 collective-permute-done.13.refs_2_
  45.8 0.0 collective-permute-done.14.refs_3_
  45.8 2.8 %collective-permute-start.15 = (bf16[4,16,8,256]{3,2,1,0:T(8,128)(2,1)S(1)}, bf16[4,16,8,256]{3,2,1,0:T(8,128)(2,1)S(1)}, u32[]{:S(2)}, u32[]{:S(2)}) collective-permute-start(bf16[4,16,8,256]{3,2,1,0:T(8,128)(2,1)S(1)} %shard_map.88), channel_id=1, source_target_pairs={{0,1},{1,0},{2,3},{3,2},{4,5},{5,4},{6,7},{7,6},{8,9},{9,8},{10,11... | collective-permute-start | bytes 786440 | tf_op jit(solution)/shard_map/ppermute | solution.py:264
  48.6 0.0 collective-permute-done.2.refs_1_
  48.6 0.3 collective-permute-done.3.refs_2_
  48.9 0.9 %collective-permute-done.4.refs_3_ = bf16[2,16,8,256]{3,2,1,0:T(8,128)(2,1)S(1)} collective-permute-done((bf16[2,16,8,256]{3,2,1,0:T(8,128)(2,1)S(1)}, bf16[2,16,8,256]{3,2,1,0:T(8,128)(2,1)S(1)}, u32[]{:S(2)}, u32[]{:S(2)}) %collective-permute-start.4) | collective-permute-done | bytes 131104 | tf_op jit(solution)/shard_map/ppermute | solution.py:250
  49.8 2.5 %collective-permute-start.5 = (bf16[4,16,8,256]{3,2,1,0:T(8,128)(2,1)S(1)}, bf16[4,16,8,256]{3,2,1,0:T(8,128)(2,1)S(1)}, u32[]{:S(2)}, u32[]{:S(2)}) collective-permute-start(bf16[4,16,8,256]{3,2,1,0:T(8,128)(2,1)S(1)} %shard_map.84), channel_id=1, source_target_pairs={{0,1},{1,0},{2,3},{3,2},{4,5},{5,4},{6,7},{7,6},{8,9},{9,8},{10,11... | collective-permute-start | bytes 786440 | tf_op jit(solution)/shard_map/ppermute | solution.py:264
  52.4 0.0 collective-permute-done.15.refs_4_
  52.4 0.0 copy-done.5
  52.4 0.0 copy-done.6
  52.4 0.0 copy-done.7
  52.4 3.1 %shard_map.89 = (bf16[2,16,8,256]{3,2,1,0:T(8,128)(2,1)S(1)}, bf16[2,16,8,256]{3,2,1,0:T(8,128)(2,1)S(1)}, bf16[2,16,8,256]{3,2,1,0:T(8,128)(2,1)S(1)}, bf16[2,16,8,256]{3,2,1,0:T(8,128)(2,1)S(1)}) custom-call(bf16[256,256]{1,0:T(8,128)(2,1)S(1)} %copy-done.5, bf16[256,256]{1,0:T(8,128)(2,1)S(1)} %copy-done.6, bf16[256,256]{1,0:T(8,128)(2,1)S(1)} %copy-done.7, ...), custom_call_target="tpu_custom_call" | custom-call | flops 1342177280 | bytes 1441792 | tf_op jit(solution)/shard_map/pallas_call | solution.py:198
  55.5 2.4 %collective-permute-start.16 = (bf16[2,16,8,256]{3,2,1,0:T(8,128)(2,1)S(1)}, bf16[2,16,8,256]{3,2,1,0:T(8,128)(2,1)S(1)}, u32[]{:S(2)}, u32[]{:S(2)}) collective-permute-start(bf16[2,16,8,256]{3,2,1,0:T(8,128)(2,1)S(1)} %get-tuple-element.42), channel_id=1, source_target_pairs={{0,6},{1,7},{2,0},{3,1},{4,2},{5,3},{6,4},{7,5},{8,14},{9,15},{10,... | collective-permute-start | bytes 393224 | tf_op jit(solution)/shard_map/ppermute | solution.py:250
  57.9 0.3 collective-permute-start.17
  58.2 0.4 collective-permute-start.18
  58.7 0.0 collective-permute-done.5.refs_4_
  58.7 3.1 %shard_map.85 = (bf16[2,16,8,256]{3,2,1,0:T(8,128)(2,1)S(1)}, bf16[2,16,8,256]{3,2,1,0:T(8,128)(2,1)S(1)}, bf16[2,16,8,256]{3,2,1,0:T(8,128)(2,1)S(1)}, bf16[2,16,8,256]{3,2,1,0:T(8,128)(2,1)S(1)}) custom-call(bf16[256,256]{1,0:T(8,128)(2,1)S(1)} %copy-done.5, bf16[256,256]{1,0:T(8,128)(2,1)S(1)} %copy-done.6, bf16[256,256]{1,0:T(8,128)(2,1)S(1)} %copy-done.7, ...), custom_call_target="tpu_custom_call" | custom-call | flops 1342177280 | bytes 1441792 | tf_op jit(solution)/shard_map/pallas_call | solution.py:198
  61.8 2.3 %collective-permute-start.6 = (bf16[2,16,8,256]{3,2,1,0:T(8,128)(2,1)S(1)}, bf16[2,16,8,256]{3,2,1,0:T(8,128)(2,1)S(1)}, u32[]{:S(2)}, u32[]{:S(2)}) collective-permute-start(bf16[2,16,8,256]{3,2,1,0:T(8,128)(2,1)S(1)} %get-tuple-element.33), channel_id=1, source_target_pairs={{0,6},{1,7},{2,0},{3,1},{4,2},{5,3},{6,4},{7,5},{8,14},{9,15},{10,... | collective-permute-start | bytes 393224 | tf_op jit(solution)/shard_map/ppermute | solution.py:250
  64.1 1.5 %collective-permute-start.7 = (bf16[2,16,8,256]{3,2,1,0:T(8,128)(2,1)S(1)}, bf16[2,16,8,256]{3,2,1,0:T(8,128)(2,1)S(1)}, u32[]{:S(2)}, u32[]{:S(2)}) collective-permute-start(bf16[2,16,8,256]{3,2,1,0:T(8,128)(2,1)S(1)} %get-tuple-element.34), channel_id=1, source_target_pairs={{0,4},{1,5},{2,6},{3,7},{4,0},{5,1},{6,2},{7,3},{8,12},{9,13},{10,... | collective-permute-start | bytes 393224 | tf_op jit(solution)/shard_map/ppermute | solution.py:250
  65.6 0.0 collective-permute-done.16.refs_1_
  65.6 0.0 collective-permute-start.8
  65.6 0.0 collective-permute-done.17.refs_2_
  65.6 2.1 %collective-permute-done.18.refs_3_ = bf16[2,16,8,256]{3,2,1,0:T(8,128)(2,1)S(1)} collective-permute-done((bf16[2,16,8,256]{3,2,1,0:T(8,128)(2,1)S(1)}, bf16[2,16,8,256]{3,2,1,0:T(8,128)(2,1)S(1)}, u32[]{:S(2)}, u32[]{:S(2)}) %collective-permute-start.18) | collective-permute-done | bytes 131104 | tf_op jit(solution)/shard_map/ppermute | solution.py:250
  67.7 0.6 collective-permute-start.19
  68.3 0.0 collective-permute-done.6.refs_1_
  68.3 1.2 %collective-permute-done.7.refs_2_ = bf16[2,16,8,256]{3,2,1,0:T(8,128)(2,1)S(1)} collective-permute-done((bf16[2,16,8,256]{3,2,1,0:T(8,128)(2,1)S(1)}, bf16[2,16,8,256]{3,2,1,0:T(8,128)(2,1)S(1)}, u32[]{:S(2)}, u32[]{:S(2)}) %collective-permute-start.7) | collective-permute-done | bytes 131104 | tf_op jit(solution)/shard_map/ppermute | solution.py:250
  69.4 3.4 %collective-permute-done.8.refs_3_ = bf16[2,16,8,256]{3,2,1,0:T(8,128)(2,1)S(1)} collective-permute-done((bf16[2,16,8,256]{3,2,1,0:T(8,128)(2,1)S(1)}, bf16[2,16,8,256]{3,2,1,0:T(8,128)(2,1)S(1)}, u32[]{:S(2)}, u32[]{:S(2)}) %collective-permute-start.8) | collective-permute-done | bytes 131104 | tf_op jit(solution)/shard_map/ppermute | solution.py:250
  72.9 1.5 %collective-permute-start.9 = (bf16[4,16,8,256]{3,2,1,0:T(8,128)(2,1)S(1)}, bf16[4,16,8,256]{3,2,1,0:T(8,128)(2,1)S(1)}, u32[]{:S(2)}, u32[]{:S(2)}) collective-permute-start(bf16[4,16,8,256]{3,2,1,0:T(8,128)(2,1)S(1)} %shard_map.86), channel_id=1, source_target_pairs={{0,1},{1,0},{2,3},{3,2},{4,5},{5,4},{6,7},{7,6},{8,9},{9,8},{10,11... | collective-permute-start | bytes 786440 | tf_op jit(solution)/shard_map/ppermute | solution.py:264
  74.4 0.0 collective-permute-done.19.refs_4_
  74.4 0.0 copy-done.2
  74.4 1.7 %shard_map.91.refs_5_ = bf16[256,8,256]{2,1,0:T(8,128)(2,1)} custom-call(s32[2]{0:T(128)S(1)} %pad_add_fusion.ids, bf16[8,16,8,256]{3,2,1,0:T(8,128)(2,1)S(1)} %get-tuple-element.36.hidden_ref, bf16[256,256]{1,0:T(8,128)(2,1)S(1)} %copy-done.2, bf16[2,16,8,256]{3,2,1,0:T(8,128)(2,1)S(1)} %get-tuple-element.41.refs_0_, ...), custom_call_target="tpu_custom_call" | custom-call | flops 134217728 | bytes 1572864 | tf_op jit(solution)/shard_map/pallas_call | solution.py:230
  76.2 0.0 collective-permute-done.9.refs_4_
  76.2 1.7 %shard_map.92 = bf16[256,8,256]{2,1,0:T(8,128)(2,1)} custom-call(s32[2]{0:T(128)S(1)} %pad_add_fusion.ids, bf16[8,16,8,256]{3,2,1,0:T(8,128)(2,1)S(1)} %get-tuple-element.27.hidden_ref, bf16[256,256]{1,0:T(8,128)(2,1)S(1)} %copy-done.2, bf16[2,16,8,256]{3,2,1,0:T(8,128)(2,1)S(1)} %get-tuple-element.32.refs_0_, ...), custom_call_target="tpu_custom_call", output_to_operand_aliasing={{}: (8, {})} | custom-call | flops 134217728 | bytes 1572864 | tf_op jit(solution)/shard_map/pallas_call | solution.py:230
  (7 shorter events, 0.1 us)
Async XLA Ops:
  0.0 26.7 %copy-start.4 = (f32[256]{0:T(256)S(1)}, f32[256]{0:T(256)}, u32[]{:S(2)}) copy-start(f32[256]{0:T(256)} %param.11) | copy-start | bytes 3076
  1.9 19.6 %collective-permute-start.11 = (bf16[129,8,256]{2,1,0:T(8,128)(2,1)}, bf16[129,8,256]{2,1,0:T(8,128)(2,1)}, u32[]{:S(2)}, u32[]{:S(2)}) collective-permute-start(bf16[129,8,256]{2,1,0:T(8,128)(2,1)} %slice_bitcast_fusion), channel_id=1, source_target_pairs={{0,248},{8,0},{16,8},{24,16},{32,24},{40,32},{48,40},{56,48},{64,5... | collective-permute-start | bytes 1585160 | tf_op jit(solution)/shard_map/ppermute | solution.py:281
  10.5 16.2 %collective-permute-start.10 = (bf16[129,8,256]{2,1,0:T(8,128)(2,1)}, bf16[129,8,256]{2,1,0:T(8,128)(2,1)}, u32[]{:S(2)}, u32[]{:S(2)}) collective-permute-start(bf16[129,8,256]{2,1,0:T(8,128)(2,1)} %slice_bitcast_fusion), channel_id=1, source_target_pairs={{0,8},{8,16},{16,24},{24,32},{32,40},{40,48},{48,56},{56,64},{64,7... | collective-permute-start | bytes 1585160 | tf_op jit(solution)/shard_map/ppermute | solution.py:281
  10.5 1.3 %copy-start = (bf16[3,3,256,256]{3,2,1,0:T(8,128)(2,1)S(1)}, bf16[3,3,256,256]{3,2,1,0:T(8,128)(2,1)}, u32[]{:S(2)}) copy-start(bf16[3,3,256,256]{3,2,1,0:T(8,128)(2,1)} %param.9) | copy-start | bytes 3538948
  11.8 1.2 %copy-start.3 = (bf16[1,256,8,256]{3,2,1,0:T(8,128)(2,1)S(1)}, bf16[1,256,8,256]{3,2,1,0:T(8,128)(2,1)}, u32[]{:S(2)}) copy-start(bf16[1,256,8,256]{3,2,1,0:T(8,128)(2,1)} %param.8) | copy-start | bytes 3145732
  13.0 0.7 copy-start.8
  13.7 13.0 %copy-start.1 = (bf16[3,3,256,256]{3,2,1,0:T(8,128)(2,1)S(1)}, bf16[3,3,256,256]{3,2,1,0:T(8,128)(2,1)}, u32[]{:S(2)}) copy-start(bf16[3,3,256,256]{3,2,1,0:T(8,128)(2,1)} %param.9) | copy-start | bytes 3538948
  15.4 19.1 %collective-permute-start.1 = (bf16[129,8,256]{2,1,0:T(8,128)(2,1)}, bf16[129,8,256]{2,1,0:T(8,128)(2,1)}, u32[]{:S(2)}, u32[]{:S(2)}) collective-permute-start(bf16[129,8,256]{2,1,0:T(8,128)(2,1)} %get-tuple-element.25), channel_id=1, source_target_pairs={{0,248},{8,0},{16,8},{24,16},{32,24},{40,32},{48,40},{56,48},{64,5... | collective-permute-start | bytes 1585160 | tf_op jit(solution)/shard_map/ppermute | solution.py:281
  20.2 17.8 %collective-permute-start = (bf16[129,8,256]{2,1,0:T(8,128)(2,1)}, bf16[129,8,256]{2,1,0:T(8,128)(2,1)}, u32[]{:S(2)}, u32[]{:S(2)}) collective-permute-start(bf16[129,8,256]{2,1,0:T(8,128)(2,1)} %get-tuple-element.25), channel_id=1, source_target_pairs={{0,8},{8,16},{16,24},{24,32},{32,40},{40,48},{48,56},{56,64},{64,7... | collective-permute-start | bytes 1585160 | tf_op jit(solution)/shard_map/ppermute | solution.py:281
  29.4 15.3 %collective-permute-start.12 = (bf16[2,16,8,256]{3,2,1,0:T(8,128)(2,1)S(1)}, bf16[2,16,8,256]{3,2,1,0:T(8,128)(2,1)S(1)}, u32[]{:S(2)}, u32[]{:S(2)}) collective-permute-start(bf16[2,16,8,256]{3,2,1,0:T(8,128)(2,1)S(1)} %get-tuple-element.38), channel_id=1, source_target_pairs={{0,2},{1,3},{2,4},{3,5},{4,6},{5,7},{6,0},{7,1},{8,10},{9,11},{10,... | collective-permute-start | bytes 393224 | tf_op jit(solution)/shard_map/ppermute | solution.py:250
  30.8 15.0 %collective-permute-start.13 = (bf16[2,16,8,256]{3,2,1,0:T(8,128)(2,1)S(1)}, bf16[2,16,8,256]{3,2,1,0:T(8,128)(2,1)S(1)}, u32[]{:S(2)}, u32[]{:S(2)}) collective-permute-start(bf16[2,16,8,256]{3,2,1,0:T(8,128)(2,1)S(1)} %get-tuple-element.39), channel_id=1, source_target_pairs={{0,4},{1,5},{2,6},{3,7},{4,0},{5,1},{6,2},{7,3},{8,12},{9,13},{10,... | collective-permute-start | bytes 393224 | tf_op jit(solution)/shard_map/ppermute | solution.py:250
  33.4 19.0 %copy-start.5 = (bf16[256,256]{1,0:T(8,128)(2,1)S(1)}, bf16[256,256]{1,0:T(8,128)(2,1)}, u32[]{:S(2)}) copy-start(bf16[256,256]{1,0:T(8,128)(2,1)} %wq_ref.3) | copy-start | bytes 393220
  33.4 19.0 %copy-start.6 = (bf16[256,256]{1,0:T(8,128)(2,1)S(1)}, bf16[256,256]{1,0:T(8,128)(2,1)}, u32[]{:S(2)}) copy-start(bf16[256,256]{1,0:T(8,128)(2,1)} %wk_ref.3) | copy-start | bytes 393220
  33.4 19.0 %copy-start.7 = (bf16[256,256]{1,0:T(8,128)(2,1)S(1)}, bf16[256,256]{1,0:T(8,128)(2,1)}, u32[]{:S(2)}) copy-start(bf16[256,256]{1,0:T(8,128)(2,1)} %wv_ref.3) | copy-start | bytes 393220
  33.4 12.4 %collective-permute-start.14 = (bf16[2,16,8,256]{3,2,1,0:T(8,128)(2,1)S(1)}, bf16[2,16,8,256]{3,2,1,0:T(8,128)(2,1)S(1)}, u32[]{:S(2)}, u32[]{:S(2)}) collective-permute-start(bf16[2,16,8,256]{3,2,1,0:T(8,128)(2,1)S(1)} %get-tuple-element.40), channel_id=1, source_target_pairs={{0,6},{1,7},{2,0},{3,1},{4,2},{5,3},{6,4},{7,5},{8,14},{9,15},{10,... | collective-permute-start | bytes 393224 | tf_op jit(solution)/shard_map/ppermute | solution.py:250
  40.7 7.9 %collective-permute-start.2 = (bf16[2,16,8,256]{3,2,1,0:T(8,128)(2,1)S(1)}, bf16[2,16,8,256]{3,2,1,0:T(8,128)(2,1)S(1)}, u32[]{:S(2)}, u32[]{:S(2)}) collective-permute-start(bf16[2,16,8,256]{3,2,1,0:T(8,128)(2,1)S(1)} %get-tuple-element.29), channel_id=1, source_target_pairs={{0,2},{1,3},{2,4},{3,5},{4,6},{5,7},{6,0},{7,1},{8,10},{9,11},{10,... | collective-permute-start | bytes 393224 | tf_op jit(solution)/shard_map/ppermute | solution.py:250
  42.1 6.8 %collective-permute-start.3 = (bf16[2,16,8,256]{3,2,1,0:T(8,128)(2,1)S(1)}, bf16[2,16,8,256]{3,2,1,0:T(8,128)(2,1)S(1)}, u32[]{:S(2)}, u32[]{:S(2)}) collective-permute-start(bf16[2,16,8,256]{3,2,1,0:T(8,128)(2,1)S(1)} %get-tuple-element.30), channel_id=1, source_target_pairs={{0,4},{1,5},{2,6},{3,7},{4,0},{5,1},{6,2},{7,3},{8,12},{9,13},{10,... | collective-permute-start | bytes 393224 | tf_op jit(solution)/shard_map/ppermute | solution.py:250
  44.7 5.1 %collective-permute-start.4 = (bf16[2,16,8,256]{3,2,1,0:T(8,128)(2,1)S(1)}, bf16[2,16,8,256]{3,2,1,0:T(8,128)(2,1)S(1)}, u32[]{:S(2)}, u32[]{:S(2)}) collective-permute-start(bf16[2,16,8,256]{3,2,1,0:T(8,128)(2,1)S(1)} %get-tuple-element.31), channel_id=1, source_target_pairs={{0,6},{1,7},{2,0},{3,1},{4,2},{5,3},{6,4},{7,5},{8,14},{9,15},{10,... | collective-permute-start | bytes 393224 | tf_op jit(solution)/shard_map/ppermute | solution.py:250
  45.8 6.6 %collective-permute-start.15 = (bf16[4,16,8,256]{3,2,1,0:T(8,128)(2,1)S(1)}, bf16[4,16,8,256]{3,2,1,0:T(8,128)(2,1)S(1)}, u32[]{:S(2)}, u32[]{:S(2)}) collective-permute-start(bf16[4,16,8,256]{3,2,1,0:T(8,128)(2,1)S(1)} %shard_map.88), channel_id=1, source_target_pairs={{0,1},{1,0},{2,3},{3,2},{4,5},{5,4},{6,7},{7,6},{8,9},{9,8},{10,11... | collective-permute-start | bytes 786440 | tf_op jit(solution)/shard_map/ppermute | solution.py:264
  49.8 8.8 %collective-permute-start.5 = (bf16[4,16,8,256]{3,2,1,0:T(8,128)(2,1)S(1)}, bf16[4,16,8,256]{3,2,1,0:T(8,128)(2,1)S(1)}, u32[]{:S(2)}, u32[]{:S(2)}) collective-permute-start(bf16[4,16,8,256]{3,2,1,0:T(8,128)(2,1)S(1)} %shard_map.84), channel_id=1, source_target_pairs={{0,1},{1,0},{2,3},{3,2},{4,5},{5,4},{6,7},{7,6},{8,9},{9,8},{10,11... | collective-permute-start | bytes 786440 | tf_op jit(solution)/shard_map/ppermute | solution.py:264
  55.5 10.0 %collective-permute-start.16 = (bf16[2,16,8,256]{3,2,1,0:T(8,128)(2,1)S(1)}, bf16[2,16,8,256]{3,2,1,0:T(8,128)(2,1)S(1)}, u32[]{:S(2)}, u32[]{:S(2)}) collective-permute-start(bf16[2,16,8,256]{3,2,1,0:T(8,128)(2,1)S(1)} %get-tuple-element.42), channel_id=1, source_target_pairs={{0,6},{1,7},{2,0},{3,1},{4,2},{5,3},{6,4},{7,5},{8,14},{9,15},{10,... | collective-permute-start | bytes 393224 | tf_op jit(solution)/shard_map/ppermute | solution.py:250
  57.9 7.7 %collective-permute-start.17 = (bf16[2,16,8,256]{3,2,1,0:T(8,128)(2,1)S(1)}, bf16[2,16,8,256]{3,2,1,0:T(8,128)(2,1)S(1)}, u32[]{:S(2)}, u32[]{:S(2)}) collective-permute-start(bf16[2,16,8,256]{3,2,1,0:T(8,128)(2,1)S(1)} %get-tuple-element.43), channel_id=1, source_target_pairs={{0,4},{1,5},{2,6},{3,7},{4,0},{5,1},{6,2},{7,3},{8,12},{9,13},{10,... | collective-permute-start | bytes 393224 | tf_op jit(solution)/shard_map/ppermute | solution.py:250
  58.2 16.2 %copy-start.2 = (bf16[256,256]{1,0:T(8,128)(2,1)S(1)}, bf16[256,256]{1,0:T(8,128)(2,1)}, u32[]{:S(2)}) copy-start(bf16[256,256]{1,0:T(8,128)(2,1)} %w_ref.3) | copy-start | bytes 393220
  58.2 9.4 %collective-permute-start.18 = (bf16[2,16,8,256]{3,2,1,0:T(8,128)(2,1)S(1)}, bf16[2,16,8,256]{3,2,1,0:T(8,128)(2,1)S(1)}, u32[]{:S(2)}, u32[]{:S(2)}) collective-permute-start(bf16[2,16,8,256]{3,2,1,0:T(8,128)(2,1)S(1)} %get-tuple-element.44), channel_id=1, source_target_pairs={{0,2},{1,3},{2,4},{3,5},{4,6},{5,7},{6,0},{7,1},{8,10},{9,11},{10,... | collective-permute-start | bytes 393224 | tf_op jit(solution)/shard_map/ppermute | solution.py:250
  61.8 6.5 %collective-permute-start.6 = (bf16[2,16,8,256]{3,2,1,0:T(8,128)(2,1)S(1)}, bf16[2,16,8,256]{3,2,1,0:T(8,128)(2,1)S(1)}, u32[]{:S(2)}, u32[]{:S(2)}) collective-permute-start(bf16[2,16,8,256]{3,2,1,0:T(8,128)(2,1)S(1)} %get-tuple-element.33), channel_id=1, source_target_pairs={{0,6},{1,7},{2,0},{3,1},{4,2},{5,3},{6,4},{7,5},{8,14},{9,15},{10,... | collective-permute-start | bytes 393224 | tf_op jit(solution)/shard_map/ppermute | solution.py:250
  64.1 5.3 %collective-permute-start.7 = (bf16[2,16,8,256]{3,2,1,0:T(8,128)(2,1)S(1)}, bf16[2,16,8,256]{3,2,1,0:T(8,128)(2,1)S(1)}, u32[]{:S(2)}, u32[]{:S(2)}) collective-permute-start(bf16[2,16,8,256]{3,2,1,0:T(8,128)(2,1)S(1)} %get-tuple-element.34), channel_id=1, source_target_pairs={{0,4},{1,5},{2,6},{3,7},{4,0},{5,1},{6,2},{7,3},{8,12},{9,13},{10,... | collective-permute-start | bytes 393224 | tf_op jit(solution)/shard_map/ppermute | solution.py:250
  65.6 7.3 %collective-permute-start.8 = (bf16[2,16,8,256]{3,2,1,0:T(8,128)(2,1)S(1)}, bf16[2,16,8,256]{3,2,1,0:T(8,128)(2,1)S(1)}, u32[]{:S(2)}, u32[]{:S(2)}) collective-permute-start(bf16[2,16,8,256]{3,2,1,0:T(8,128)(2,1)S(1)} %get-tuple-element.35), channel_id=1, source_target_pairs={{0,2},{1,3},{2,4},{3,5},{4,6},{5,7},{6,0},{7,1},{8,10},{9,11},{10,... | collective-permute-start | bytes 393224 | tf_op jit(solution)/shard_map/ppermute | solution.py:250
  67.7 6.8 %collective-permute-start.19 = (bf16[4,16,8,256]{3,2,1,0:T(8,128)(2,1)S(1)}, bf16[4,16,8,256]{3,2,1,0:T(8,128)(2,1)S(1)}, u32[]{:S(2)}, u32[]{:S(2)}) collective-permute-start(bf16[4,16,8,256]{3,2,1,0:T(8,128)(2,1)S(1)} %shard_map.90), channel_id=1, source_target_pairs={{0,1},{1,0},{2,3},{3,2},{4,5},{5,4},{6,7},{7,6},{8,9},{9,8},{10,11... | collective-permute-start | bytes 786440 | tf_op jit(solution)/shard_map/ppermute | solution.py:264
  72.9 3.2 %collective-permute-start.9 = (bf16[4,16,8,256]{3,2,1,0:T(8,128)(2,1)S(1)}, bf16[4,16,8,256]{3,2,1,0:T(8,128)(2,1)S(1)}, u32[]{:S(2)}, u32[]{:S(2)}) collective-permute-start(bf16[4,16,8,256]{3,2,1,0:T(8,128)(2,1)S(1)} %shard_map.86), channel_id=1, source_target_pairs={{0,1},{1,0},{2,3},{3,2},{4,5},{5,4},{6,7},{7,6},{8,9},{9,8},{10,11... | collective-permute-start | bytes 786440 | tf_op jit(solution)/shard_map/ppermute | solution.py:264

commit v3 on v2

--- a/solution.py
+++ b/solution.py
@@ -59,6 +59,24 @@
     return jnp.concatenate(out, axis=1)
 
 
+def head_kernel(src, dst, sem):
+    copy = pltpu.make_async_copy(src.at[pl.ds(0, dst.shape[0])], dst, sem)
+    copy.start()
+    copy.wait()
+
+
+def head(x, count):
+    return pl.pallas_call(
+        head_kernel,
+        out_shape=pltpu.VMEM((count, *x.shape[1:]), x.dtype),
+        in_specs=[ANY],
+        out_specs=VMEM,
+        scratch_shapes=[pltpu.SemaphoreType.DMA],
+        compiler_params=params(4),
+        cost_estimate=cost(0, x.size * 2),
+    )(pltpu.with_memory_space_constraint(x, pltpu.HBM))
+
+
 def row_weight(weight, row):
     return weight[3 * row : 3 * row + 3].reshape(3 * weight.shape[1], weight.shape[2])
 
@@ -91,7 +109,7 @@
     return 2 * lax.rem(chip + k // 2, parts // 2) + (core if k % 2 == 0 else 1 - core)
 
 
-def conv_kernel(tile, offset, start, lats, ids, up, down, acc_in, weight, gain, hidden_out, *refs):
+def conv_kernel(tile, offset, start, lats, ids, down, up, acc_in, weight, gain, hidden_out, *refs):
     normed_out, (hidden, normed) = refs[:-2], refs[-2:]
     width, leads, chans = hidden.shape
     parts = 2 * len(normed_out)
@@ -138,13 +156,16 @@
         scratch_shapes=[pltpu.VMEM((width, leads, chans), BF16)] * 2,
         compiler_params=params(12),
         cost_estimate=cost(size * 12 * chans, size * 12, size),
-    )(ids, *in_vmem(up, down, acc), weight, gain)
+    )(ids, *in_vmem(down, up, acc), weight, gain)
     return out[0], out[1:]
 
 
-def attend_kernel(block, wq_ref, wk_ref, wv_ref, *refs):
-    ones_ref, chips = refs[-1], len(refs) // 2 - 1
-    near, far, outs = refs[:chips], refs[chips], refs[chips + 1 : -1]
+def attend_kernel(block, chips, wq_ref, wk_ref, wv_ref, *refs):
+    ones_ref, outs, far, near = refs[-1], refs[-1 - chips : -1], refs[chips], refs[:chips]
+    earlier = refs[chips + 1 : -1 - chips]
+    for ref, out in zip(earlier, outs):
+        out[:, : ref.shape[1]] = ref[...]
+    behind = earlier[0].shape[1] if earlier else 0
     xs = [x for k in range(chips) for x in (near[k].at[0], far.at[k])]
     parts, (pixels, leads, chans) = len(xs), xs[0].shape
     times, heads = parts * leads, chans // HD
@@ -189,79 +210,99 @@
             attended = mixed[p] / total[p * times : (p + 1) * times]
             attended = attended.astype(BF16).reshape(parts, leads, chans)
             for k in range(parts):
-                outs[k // 2][k % 2, first + p] = attended[k]
-
-
-def attend(near, far, w_query, w_key, w_value):
+                outs[k // 2][k % 2, behind + first + p] = attended[k]
+
+
+def attend(near, far, earlier, w_query, w_key, w_value):
     chips, pixels, leads, chans = far.shape
     size, times = 2 * far.size, 2 * chips * leads
+    behind = earlier[0].shape[1] if earlier else 0
     return pl.pallas_call(
-        functools.partial(attend_kernel, math.gcd(pixels, 8)),
-        out_shape=[pltpu.VMEM(near[0].shape, BF16)] * chips,
-        in_specs=[VMEM] * (4 + chips),
+        functools.partial(attend_kernel, math.gcd(pixels, 8), chips),
+        out_shape=[pltpu.VMEM((2, behind + pixels, leads, chans), BF16)] * chips,
+        in_specs=[VMEM] * (4 + chips + len(earlier)),
         out_specs=[VMEM] * chips,
         scratch_shapes=[pltpu.VMEM((chans // HD * times, chans), BF16)],
         compiler_params=params(16),
         cost_estimate=cost(size * chans * 20, size * 4 + 6 * chans * chans, size * 2),
-    )(w_query, w_key, w_value, *in_vmem(*near, far))
-
-
-def out_kernel(start, ids, hidden_ref, w_ref, *refs):
+    )(w_query, w_key, w_value, *in_vmem(*near, far, *earlier))
+
+
+def out_kernel(starts, core, chips, ids, w_ref, *refs):
+    hiddens, refs = refs[: len(starts)], refs[len(starts) :]
     out_hbm, held, sems = refs[-3:]
-    parts, count, leads, chans = hidden_ref.shape
-    near, far = refs[: parts // 2], refs[parts // 2]
+    _, count, leads, chans = held.shape
+    for i in range(chips):
+        x = refs[i][0] if core == 0 else refs[0][i]
+        hidden = jnp.concatenate([ref[2 * i + core] for ref in hiddens], axis=0)
+        acc = jnp.dot(x.reshape(count * leads, chans), w_ref[...], preferred_element_type=F32)
+        acc = acc + hidden.reshape(count * leads, chans).astype(F32)
+        held[i] = acc.astype(BF16).reshape(count, leads, chans)
     copies = []
-    for k in range(parts):
-        x = near[k // 2][0] if k % 2 == 0 else far[k // 2]
-        acc = jnp.dot(x.reshape(count * leads, chans), w_ref[...], preferred_element_type=F32)
-        acc = acc + hidden_ref[k].reshape(count * leads, chans).astype(F32)
-        held[k] = acc.astype(BF16).reshape(count, leads, chans)
-    for k in range(parts):
-        there = pl.ds(start + place(ids[1], parts, k) * count, count)
-        copies.append(pltpu.make_async_copy(held.at[k], out_hbm.at[there], sems.at[k]))
-        copies[-1].start()
+    for i in range(chips):
+        low = 0
+        for k, (start, ref) in enumerate(zip(starts, hiddens)):
+            width = ref.shape[1]
+            there = pl.ds(start + place(ids[1], 2 * chips, 2 * i + core) * width, width)
+            copies.append(
+                pltpu.make_async_copy(
+                    held.at[i, pl.ds(low, width)], out_hbm.at[there], sems.at[k, i]
+                )
+            )
+            copies[-1].start()
+            low += width
     for copy in copies:
         copy.wait()
 
 
-def project_out(ids, near, far, hidden, w_out, whole, start, total):
-    parts, _, leads, chans = hidden.shape
-    args = [ids, *in_vmem(hidden), w_out, *in_vmem(*near, far)] + ([] if whole is None else [whole])
+def project_out(core, ids, attended, hiddens, w_out, whole, starts, total):
+    parts, _, leads, chans = hiddens[0].shape
+    count = sum(hidden.shape[1] for hidden in hiddens)
+    chips = parts // 2
+    args = [ids, w_out, *in_vmem(*hiddens, *attended)] + ([] if whole is None else [whole])
     return pl.pallas_call(
-        functools.partial(out_kernel, start),
+        functools.partial(out_kernel, starts, core, chips),
         out_shape=jax.ShapeDtypeStruct((total, leads, chans), BF16),
-        in_specs=[SMEM] + [VMEM] * (3 + len(near)) + ([] if whole is None else [ANY]),
+        in_specs=[SMEM]
+        + [VMEM] * (1 + len(hiddens) + len(attended))
+        + ([] if whole is None else [ANY]),
         out_specs=ANY,
-        scratch_shapes=[pltpu.VMEM(hidden.shape, BF16), pltpu.SemaphoreType.DMA((parts,))],
-        input_output_aliases={} if whole is None else {4 + len(near): 0},
+        scratch_shapes=[
+            pltpu.VMEM((chips, count, leads, chans), BF16),
+            pltpu.SemaphoreType.DMA((len(starts), chips)),
+        ],
+        input_output_aliases={} if whole is None else {len(args) - 1: 0},
         compiler_params=params(8),
-        cost_estimate=cost(hidden.size * 2 * chans, hidden.size * 6),
+        cost_estimate=cost(total * leads * chans * chans, total * leads * chans * 3),
     )(*args)
 
 
 def gather_kernel(*refs):
-    for k, ref in enumerate(refs[:-1]):
-        refs[-1][k] = ref[1]
-
-
-def ship(pieces, sign):
+    for k in range(refs[-1].shape[0]):
+        refs[-1][k] = refs[k][1]
+
+
+def send(pieces, sign):
     chips = len(pieces)
-    near = [pieces[0]] + [
+    return [pieces[0]] + [
         lax.ppermute(
             pieces[k], "lead", [(i, (i + 2 * sign * k) % (2 * chips)) for i in range(2 * chips)]
         )
         for k in range(1, chips)
     ]
-    part = pieces[0].shape[1:]
+
+
+def swap(near, *before):
+    chips, part = len(near), near[0].shape[1:]
     others = pl.pallas_call(
         gather_kernel,
         out_shape=pltpu.VMEM((chips, *part), BF16),
-        in_specs=[VMEM] * chips,
+        in_specs=[VMEM] * chips + [ANY] * len(before),
         out_specs=VMEM,
         compiler_params=params(4),
-        cost_estimate=cost(0, chips * pieces[0].size * 2),
-    )(*in_vmem(*near))
-    return near, lax.ppermute(others, "lead", [(i, i ^ 1) for i in range(2 * chips)])
+        cost_estimate=cost(0, chips * near[0].size * 2),
+    )(*in_vmem(*near), *before)
+    return lax.ppermute(others, "lead", [(i, i ^ 1) for i in range(2 * chips)])
 
 
 def shards(latent, conv_weight, conv_bias, norm_gain, w_query, w_key, w_value, w_out):
@@ -279,17 +320,22 @@
     acc, *pieces = centre_conv(latent, w_conv, bias, ranges[1:])
     sides = [
         (lax.ppermute(piece, "lat", north), lax.ppermute(piece, "lat", south))
-        for piece in [latent[: ranges[0][1]], *pieces]
+        for piece in [head(latent, ranges[0][1]), *pieces]
     ]
-    hiddens, blocks = [], []
+    hiddens, arrived = [], []
     for (up, down), start, count in zip(sides, starts, WIDTHS):
         hidden, normed = conv_norm(lats, parts, ids, up, down, acc, w_conv, gain, start, count)
         hiddens.append(hidden)
-        blocks.append(ship(normed, 1))
-    backs = [ship(attend(*block, w_query, w_key, w_value), -1) for block in blocks]
-    out = None
-    for back, hidden, start in zip(backs, hiddens, starts):
-        out = project_out(ids, *back, hidden, w_out, out, start, width)
+        arrived.append(send(normed, 1))
+    mixed, before = [], hiddens[-1]
+    for near in arrived:
+        far = swap(near, before)
+        mixed = attend(near, far, mixed, w_query, w_key, w_value)
+        before = mixed[0]
+    near = send(mixed, -1)
+    far = swap(near)
+    out = project_out(0, ids, near, hiddens, w_out, None, starts, width)
+    out = project_out(1, ids, [far], hiddens, w_out, out, starts, width)
     return out[None]
 
 

time: 78.3 us -> 75.3 us (0.962)
  starting transfers between devices: 37.9 us -> 29.7 us
  waiting for transfers between devices: 17.9 us -> 23 us
  Pallas kernels: 16.8 us -> 18.8 us
  local copies, waits for them, and re-layouts: 5.07 us -> 3.19 us
    ppermute x16 -> x12, waiting for transfers between devices: 7.95 us -> 17.3 us  [the longest x9 16.1 us: send(): lax.ppermute(pieces[k], 'lead', [(i, (i + 2 * sign * k) % (2 * chips)) fo...]
    ppermute x16 -> x12, starting transfers between devices: 24.5 us -> 16.2 us  [the longest x9 13.3 us: send(): lax.ppermute(pieces[k], 'lead', [(i, (i + 2 * sign * k) % (2 * chips)) fo...]
    ppermute x2, waiting for transfers between devices: 8.74 us -> 5.7 us  [shards(): lax.ppermute(piece, 'lat', north)]
    ppermute x2, starting transfers between devices: 0.01 us -> 2.55 us  [shards(): lax.ppermute(piece, 'lat', north)]
    ppermute x2, starting transfers between devices: 13.4 us -> 11 us  [shards(): lax.ppermute(piece, 'lat', south)]
    pallas_call x8, Pallas kernels: 9.72 us -> 11.6 us  [the longest x2 6.22 us: attend(): pl.pallas_call(functools.partial(attend_kernel, math.gcd(pixels, 8), chip...]
    slice x1 -> x0, local copies, waits for them, and re-layouts: 1.88 us -> none  [shards(): latent[:ranges[0][1]]]
    ppermute x2, waiting for transfers between devices: 1.22 us -> 0.01 us  [shards(): lax.ppermute(piece, 'lat', south)]
  transfers between devices with their start and end apart: 20 -> 16, of which waited for: 8 -> 7; matrix products, arithmetic and copies ran while one was open for 0% -> 0% of each run, Pallas kernels for 19% -> 16%
where the time goes in v3:
time: 75.3 us; the launch traced here: 75.1 us
  starting transfers between devices  29.7 us (39%)
  waiting for transfers between devices  23 us (31%)
  Pallas kernels  18.8 us (25%)
  local copies, waits for them, and re-layouts  3.19 us (4%)
    ppermute x9, waiting for transfers between devices, send(): lax.ppermute(pieces[k], 'lead', [(i, (i + 2 * sign * k) % (2 * chips)) fo...  16.1 us
    ppermute x9, starting transfers between devices, send(): lax.ppermute(pieces[k], 'lead', [(i, (i + 2 * sign * k) % (2 * chips)) fo...  13.3 us
    ppermute x2, starting transfers between devices, shards(): lax.ppermute(piece, 'lat', south)  11 us
    pallas_call x2, Pallas kernels, attend(): pl.pallas_call(functools.partial(attend_kernel, math.gcd(pixels, 8), chip...  6.22 us
    ppermute x2, waiting for transfers between devices, shards(): lax.ppermute(piece, 'lat', north)  5.7 us
    pallas_call x2, Pallas kernels, conv_norm(): pl.pallas_call(functools.partial(conv_kernel, tile, start - low, start, l...  5.39 us
    pallas_call x2, Pallas kernels, project_out(): pl.pallas_call(functools.partial(out_kernel, starts, core, chips), out_sh...  3.39 us
    unnamed x18, local copies, waits for them, and re-layouts  3.19 us
  transfers between devices with their start and end apart: 16, of which 7 were waited for; matrix products, arithmetic and copies ran while one was open for 0% of the time, Pallas kernels for 16%

profile of v3, /device:TPU:1, one launch (start us, length us, event | category | flops | bytes accessed | tf_op | source)
XLA Modules:
  0.0 75.1 jit_solution(5620087181779755249)
XLA Ops:
  0.0 0.0 copy-start.1
  0.0 0.0 copy-start.4
  0.0 1.9 %shard_map.82 = bf16[129,8,256]{2,1,0:T(8,128)(2,1)} custom-call(bf16[256,8,256]{2,1,0:T(8,128)(2,1)} %bitcast.10), custom_call_target="tpu_custom_call" | custom-call | bytes 1048576 | tf_op jit(solution)/shard_map/pallas_call | solution.py:69
  2.0 2.5 %collective-permute-start.1 = (bf16[129,8,256]{2,1,0:T(8,128)(2,1)}, bf16[129,8,256]{2,1,0:T(8,128)(2,1)}, u32[]{:S(2)}, u32[]{:S(2)}) collective-permute-start(bf16[129,8,256]{2,1,0:T(8,128)(2,1)} %shard_map.82), channel_id=1, source_target_pairs={{0,8},{8,16},{16,24},{24,32},{32,40},{40,48},{48,56},{56,64},{64,7... | collective-permute-start | bytes 1585160 | tf_op jit(solution)/shard_map/ppermute | solution.py:322
  4.5 6.2 %collective-permute-start = (bf16[129,8,256]{2,1,0:T(8,128)(2,1)}, bf16[129,8,256]{2,1,0:T(8,128)(2,1)}, u32[]{:S(2)}, u32[]{:S(2)}) collective-permute-start(bf16[129,8,256]{2,1,0:T(8,128)(2,1)} %shard_map.82), channel_id=1, source_target_pairs={{0,248},{8,0},{16,8},{24,16},{32,24},{40,32},{48,40},{56,48},{64,5... | collective-permute-start | bytes 1585160 | tf_op jit(solution)/shard_map/ppermute | solution.py:322
  10.7 0.0 copy-start
  10.7 1.3 %copy-done = bf16[3,3,256,256]{3,2,1,0:T(8,128)(2,1)S(1)} copy-done((bf16[3,3,256,256]{3,2,1,0:T(8,128)(2,1)S(1)}, bf16[3,3,256,256]{3,2,1,0:T(8,128)(2,1)}, u32[]{:S(2)}) %copy-start) | copy-done | bytes 1179672
  12.0 0.0 copy-start.2
  12.0 1.2 %copy-done.2 = bf16[1,256,8,256]{3,2,1,0:T(8,128)(2,1)S(1)} copy-done((bf16[1,256,8,256]{3,2,1,0:T(8,128)(2,1)S(1)}, bf16[1,256,8,256]{3,2,1,0:T(8,128)(2,1)}, u32[]{:S(2)}) %copy-start.2) | copy-done | bytes 1048600
  13.2 0.0 copy-start.8
  13.2 0.7 copy-done.8
  13.9 1.8 %shard_map.83 = (f32[2048,256]{1,0:T(8,128)S(1)}, bf16[129,8,256]{2,1,0:T(8,128)(2,1)}) custom-call(bf16[256,8,256]{2,1,0:T(8,128)(2,1)S(1)} %bitcast.11, bf16[9,256,256]{2,1,0:T(8,128)(2,1)S(1)} %bitcast.7, f32[1,256]{1,0:T(1,128)S(1)} %bitcast.14), custom_call_target="tpu_custom_call" | custom-call | flops 805306368 | bytes 3145728 | tf_op jit(solution)/shard_map/pallas_call | solution.py:96
  15.7 0.0 collective-permute-start.3
  15.7 4.8 %collective-permute-start.2 = (bf16[129,8,256]{2,1,0:T(8,128)(2,1)}, bf16[129,8,256]{2,1,0:T(8,128)(2,1)}, u32[]{:S(2)}, u32[]{:S(2)}) collective-permute-start(bf16[129,8,256]{2,1,0:T(8,128)(2,1)} %get-tuple-element.27), channel_id=1, source_target_pairs={{0,248},{8,0},{16,8},{24,16},{32,24},{40,32},{48,40},{56,48},{64,5... | collective-permute-start | bytes 1585160 | tf_op jit(solution)/shard_map/ppermute | solution.py:322
  20.4 0.1 pad_add_fusion.ids
  20.5 2.2 %collective-permute-done.1.up = bf16[129,8,256]{2,1,0:T(8,128)(2,1)} collective-permute-done((bf16[129,8,256]{2,1,0:T(8,128)(2,1)}, bf16[129,8,256]{2,1,0:T(8,128)(2,1)}, u32[]{:S(2)}, u32[]{:S(2)}) %collective-permute-start.1) | collective-permute-done | bytes 528416 | tf_op jit(solution)/shard_map/ppermute | solution.py:322
  22.7 0.0 collective-permute-done.down
  22.7 0.0 copy-done.1
  22.7 0.0 copy-done.4
  22.7 2.7 %shard_map.84 = (bf16[8,16,8,256]{3,2,1,0:T(8,128)(2,1)S(1)}, bf16[2,16,8,256]{3,2,1,0:T(8,128)(2,1)S(1)}, bf16[2,16,8,256]{3,2,1,0:T(8,128)(2,1)S(1)}, bf16[2,1...) custom-call(s32[2]{0:T(128)S(1)} %pad_add_fusion.ids, bf16[129,8,256]{2,1,0:T(8,128)(2,1)} %collective-permute-done.down, ...), custom_call_target="tpu_custom_call" | custom-call | flops 805306368 | bytes 3145728 | tf_op jit(solution)/shard_map/pallas_call | solution.py:150
  25.4 1.4 %collective-permute-start.7 = (bf16[2,16,8,256]{3,2,1,0:T(8,128)(2,1)S(1)}, bf16[2,16,8,256]{3,2,1,0:T(8,128)(2,1)S(1)}, u32[]{:S(2)}, u32[]{:S(2)}) collective-permute-start(bf16[2,16,8,256]{3,2,1,0:T(8,128)(2,1)S(1)} %get-tuple-element.34), channel_id=1, source_target_pairs={{0,2},{1,3},{2,4},{3,5},{4,6},{5,7},{6,0},{7,1},{8,10},{9,11},{10,... | collective-permute-start | bytes 393224 | tf_op jit(solution)/shard_map/ppermute | solution.py:288
  26.8 2.6 %collective-permute-start.8 = (bf16[2,16,8,256]{3,2,1,0:T(8,128)(2,1)S(1)}, bf16[2,16,8,256]{3,2,1,0:T(8,128)(2,1)S(1)}, u32[]{:S(2)}, u32[]{:S(2)}) collective-permute-start(bf16[2,16,8,256]{3,2,1,0:T(8,128)(2,1)S(1)} %get-tuple-element.35), channel_id=1, source_target_pairs={{0,4},{1,5},{2,6},{3,7},{4,0},{5,1},{6,2},{7,3},{8,12},{9,13},{10,... | collective-permute-start | bytes 393224 | tf_op jit(solution)/shard_map/ppermute | solution.py:288
  29.4 0.0 copy-start.5
  29.4 0.0 copy-start.6
  29.4 0.0 copy-start.7
  29.4 1.1 %collective-permute-start.9 = (bf16[2,16,8,256]{3,2,1,0:T(8,128)(2,1)S(1)}, bf16[2,16,8,256]{3,2,1,0:T(8,128)(2,1)S(1)}, u32[]{:S(2)}, u32[]{:S(2)}) collective-permute-start(bf16[2,16,8,256]{3,2,1,0:T(8,128)(2,1)S(1)} %get-tuple-element.36), channel_id=1, source_target_pairs={{0,6},{1,7},{2,0},{3,1},{4,2},{5,3},{6,4},{7,5},{8,14},{9,15},{10,... | collective-permute-start | bytes 393224 | tf_op jit(solution)/shard_map/ppermute | solution.py:288
  30.5 3.5 %collective-permute-done.3.up = bf16[129,8,256]{2,1,0:T(8,128)(2,1)} collective-permute-done((bf16[129,8,256]{2,1,0:T(8,128)(2,1)}, bf16[129,8,256]{2,1,0:T(8,128)(2,1)}, u32[]{:S(2)}, u32[]{:S(2)}) %collective-permute-start.3) | collective-permute-done | bytes 528416 | tf_op jit(solution)/shard_map/ppermute | solution.py:322
  34.0 0.0 collective-permute-done.2.down
  34.0 2.7 %shard_map.85 = (bf16[8,16,8,256]{3,2,1,0:T(8,128)(2,1)S(1)}, bf16[2,16,8,256]{3,2,1,0:T(8,128)(2,1)S(1)}, bf16[2,16,8,256]{3,2,1,0:T(8,128)(2,1)S(1)}, bf16[2,1...) custom-call(s32[2]{0:T(128)S(1)} %pad_add_fusion.ids, bf16[129,8,256]{2,1,0:T(8,128)(2,1)} %collective-permute-done.2.down, ...), custom_call_target="tpu_custom_call" | custom-call | flops 805306368 | bytes 3145728 | tf_op jit(solution)/shard_map/pallas_call | solution.py:150
  36.7 0.0 collective-permute-done.7.refs_1_
  36.7 0.0 collective-permute-done.8.refs_2_
  36.7 0.0 collective-permute-done.9.refs_3_
  36.8 1.3 %collective-permute-start.10 = (bf16[4,16,8,256]{3,2,1,0:T(8,128)(2,1)S(1)}, bf16[4,16,8,256]{3,2,1,0:T(8,128)(2,1)S(1)}, u32[]{:S(2)}, u32[]{:S(2)}) collective-permute-start(bf16[4,16,8,256]{3,2,1,0:T(8,128)(2,1)S(1)} %shard_map.86), channel_id=1, source_target_pairs={{0,1},{1,0},{2,3},{3,2},{4,5},{5,4},{6,7},{7,6},{8,9},{9,8},{10,11... | collective-permute-start | bytes 786440 | tf_op jit(solution)/shard_map/ppermute | solution.py:305
  38.1 1.3 %collective-permute-start.4 = (bf16[2,16,8,256]{3,2,1,0:T(8,128)(2,1)S(1)}, bf16[2,16,8,256]{3,2,1,0:T(8,128)(2,1)S(1)}, u32[]{:S(2)}, u32[]{:S(2)}) collective-permute-start(bf16[2,16,8,256]{3,2,1,0:T(8,128)(2,1)S(1)} %get-tuple-element.30), channel_id=1, source_target_pairs={{0,2},{1,3},{2,4},{3,5},{4,6},{5,7},{6,0},{7,1},{8,10},{9,11},{10,... | collective-permute-start | bytes 393224 | tf_op jit(solution)/shard_map/ppermute | solution.py:288
  39.4 2.6 %collective-permute-start.5 = (bf16[2,16,8,256]{3,2,1,0:T(8,128)(2,1)S(1)}, bf16[2,16,8,256]{3,2,1,0:T(8,128)(2,1)S(1)}, u32[]{:S(2)}, u32[]{:S(2)}) collective-permute-start(bf16[2,16,8,256]{3,2,1,0:T(8,128)(2,1)S(1)} %get-tuple-element.31), channel_id=1, source_target_pairs={{0,4},{1,5},{2,6},{3,7},{4,0},{5,1},{6,2},{7,3},{8,12},{9,13},{10,... | collective-permute-start | bytes 393224 | tf_op jit(solution)/shard_map/ppermute | solution.py:288
  42.0 1.1 %collective-permute-start.6 = (bf16[2,16,8,256]{3,2,1,0:T(8,128)(2,1)S(1)}, bf16[2,16,8,256]{3,2,1,0:T(8,128)(2,1)S(1)}, u32[]{:S(2)}, u32[]{:S(2)}) collective-permute-start(bf16[2,16,8,256]{3,2,1,0:T(8,128)(2,1)S(1)} %get-tuple-element.32), channel_id=1, source_target_pairs={{0,6},{1,7},{2,0},{3,1},{4,2},{5,3},{6,4},{7,5},{8,14},{9,15},{10,... | collective-permute-start | bytes 393224 | tf_op jit(solution)/shard_map/ppermute | solution.py:288
  43.1 0.0 collective-permute-done.10.refs_4_
  43.1 0.0 copy-done.5
  43.1 0.0 copy-done.6
  43.1 0.0 copy-done.7
  43.1 3.1 %shard_map.87 = (bf16[2,16,8,256]{3,2,1,0:T(8,128)(2,1)S(1)}, bf16[2,16,8,256]{3,2,1,0:T(8,128)(2,1)S(1)}, bf16[2,16,8,256]{3,2,1,0:T(8,128)(2,1)S(1)}, bf16[2,16,8,256]{3,2,1,0:T(8,128)(2,1)S(1)}) custom-call(bf16[256,256]{1,0:T(8,128)(2,1)S(1)} %copy-done.5, bf16[256,256]{1,0:T(8,128)(2,1)S(1)} %copy-done.6, bf16[256,256]{1,0:T(8,128)(2,1)S(1)} %copy-done.7, ...), custom_call_target="tpu_custom_call" | custom-call | flops 1342177280 | bytes 1441792 | tf_op jit(solution)/shard_map/pallas_call | solution.py:220
  46.2 0.0 collective-permute-done.4.refs_1_
  46.2 2.2 %collective-permute-done.5.refs_2_ = bf16[2,16,8,256]{3,2,1,0:T(8,128)(2,1)S(1)} collective-permute-done((bf16[2,16,8,256]{3,2,1,0:T(8,128)(2,1)S(1)}, bf16[2,16,8,256]{3,2,1,0:T(8,128)(2,1)S(1)}, u32[]{:S(2)}, u32[]{:S(2)}) %collective-permute-start.5) | collective-permute-done | bytes 131104 | tf_op jit(solution)/shard_map/ppermute | solution.py:288
  48.4 0.0 collective-permute-done.6.refs_3_
  48.4 1.0 %collective-permute-start.11 = (bf16[4,16,8,256]{3,2,1,0:T(8,128)(2,1)S(1)}, bf16[4,16,8,256]{3,2,1,0:T(8,128)(2,1)S(1)}, u32[]{:S(2)}, u32[]{:S(2)}) collective-permute-start(bf16[4,16,8,256]{3,2,1,0:T(8,128)(2,1)S(1)} %shard_map.88), channel_id=1, source_target_pairs={{0,1},{1,0},{2,3},{3,2},{4,5},{5,4},{6,7},{7,6},{8,9},{9,8},{10,11... | collective-permute-start | bytes 786440 | tf_op jit(solution)/shard_map/ppermute | solution.py:305
  49.4 1.2 %collective-permute-done.11.refs_4_ = bf16[4,16,8,256]{3,2,1,0:T(8,128)(2,1)S(1)} collective-permute-done((bf16[4,16,8,256]{3,2,1,0:T(8,128)(2,1)S(1)}, bf16[4,16,8,256]{3,2,1,0:T(8,128)(2,1)S(1)}, u32[]{:S(2)}, u32[]{:S(2)}) %collective-permute-start.11) | collective-permute-done | bytes 262176 | tf_op jit(solution)/shard_map/ppermute | solution.py:305
  50.5 0.0 copy-start.3
  50.5 3.1 %shard_map.89 = (bf16[2,32,8,256]{3,2,1,0:T(8,128)(2,1)S(1)}, bf16[2,32,8,256]{3,2,1,0:T(8,128)(2,1)S(1)}, bf16[2,32,8,256]{3,2,1,0:T(8,128)(2,1)S(1)}, bf16[2,32,8,256]{3,2,1,0:T(8,128)(2,1)S(1)}) custom-call(bf16[256,256]{1,0:T(8,128)(2,1)S(1)} %copy-done.5, bf16[256,256]{1,0:T(8,128)(2,1)S(1)} %copy-done.6, bf16[256,256]{1,0:T(8,128)(2,1)S(1)} %copy-done.7, ...), custom_call_target="tpu_custom_call" | custom-call | flops 1342177280 | bytes 1441792 | tf_op jit(solution)/shard_map/pallas_call | solution.py:220
  53.7 1.9 %collective-permute-start.12 = (bf16[2,32,8,256]{3,2,1,0:T(8,128)(2,1)S(1)}, bf16[2,32,8,256]{3,2,1,0:T(8,128)(2,1)S(1)}, u32[]{:S(2)}, u32[]{:S(2)}) collective-permute-start(bf16[2,32,8,256]{3,2,1,0:T(8,128)(2,1)S(1)} %get-tuple-element.42), channel_id=1, source_target_pairs={{0,6},{1,7},{2,0},{3,1},{4,2},{5,3},{6,4},{7,5},{8,14},{9,15},{10,... | collective-permute-start | bytes 786440 | tf_op jit(solution)/shard_map/ppermute | solution.py:288
  55.5 0.9 %collective-permute-start.13 = (bf16[2,32,8,256]{3,2,1,0:T(8,128)(2,1)S(1)}, bf16[2,32,8,256]{3,2,1,0:T(8,128)(2,1)S(1)}, u32[]{:S(2)}, u32[]{:S(2)}) collective-permute-start(bf16[2,32,8,256]{3,2,1,0:T(8,128)(2,1)S(1)} %get-tuple-element.43), channel_id=1, source_target_pairs={{0,4},{1,5},{2,6},{3,7},{4,0},{5,1},{6,2},{7,3},{8,12},{9,13},{10,... | collective-permute-start | bytes 786440 | tf_op jit(solution)/shard_map/ppermute | solution.py:288
  56.4 0.5 collective-permute-start.14
  56.9 4.4 %collective-permute-done.12.refs_1_.refs_3_ = bf16[2,32,8,256]{3,2,1,0:T(8,128)(2,1)S(1)} collective-permute-done((bf16[2,32,8,256]{3,2,1,0:T(8,128)(2,1)S(1)}, bf16[2,32,8,256]{3,2,1,0:T(8,128)(2,1)S(1)}, u32[]{:S(2)}, u32[]{:S(2)}) %collective-permute-start.12) | collective-permute-done | bytes 262176 | tf_op jit(solution)/shard_map/ppermute | solution.py:288
  61.3 3.0 %collective-permute-done.13.refs_2_.refs_4_ = bf16[2,32,8,256]{3,2,1,0:T(8,128)(2,1)S(1)} collective-permute-done((bf16[2,32,8,256]{3,2,1,0:T(8,128)(2,1)S(1)}, bf16[2,32,8,256]{3,2,1,0:T(8,128)(2,1)S(1)}, u32[]{:S(2)}, u32[]{:S(2)}) %collective-permute-start.13) | collective-permute-done | bytes 262176 | tf_op jit(solution)/shard_map/ppermute | solution.py:288
  64.3 6.6 %collective-permute-done.14.refs_3_.refs_5_ = bf16[2,32,8,256]{3,2,1,0:T(8,128)(2,1)S(1)} collective-permute-done((bf16[2,32,8,256]{3,2,1,0:T(8,128)(2,1)S(1)}, bf16[2,32,8,256]{3,2,1,0:T(8,128)(2,1)S(1)}, u32[]{:S(2)}, u32[]{:S(2)}) %collective-permute-start.14) | collective-permute-done | bytes 262176 | tf_op jit(solution)/shard_map/ppermute | solution.py:288
  70.9 0.6 collective-permute-start.15
  71.5 0.0 copy-done.3
  71.5 1.7 %shard_map.91.refs_3_ = bf16[256,8,256]{2,1,0:T(8,128)(2,1)} custom-call(s32[2]{0:T(128)S(1)} %pad_add_fusion.ids, bf16[256,256]{1,0:T(8,128)(2,1)S(1)} %copy-done.3, bf16[8,16,8,256]{3,2,1,0:T(8,128)(2,1)S(1)} %get-tuple-element.26.refs_0_, bf16[8,16,8,256]{3,2,1,0:T(8,128)(2,1)S(1)} %get-tuple-element.28.refs_4_.refs_1_, ...), custom_call_target="tpu_custom_call" | custom-call | flops 134217728 | bytes 1572864 | tf_op jit(solution)/shard_map/pallas_call | solution.py:263
  73.2 0.0 collective-permute-done.15.refs_2_
  73.2 1.7 %shard_map.92 = bf16[256,8,256]{2,1,0:T(8,128)(2,1)} custom-call(s32[2]{0:T(128)S(1)} %pad_add_fusion.ids, bf16[256,256]{1,0:T(8,128)(2,1)S(1)} %copy-done.3, bf16[8,16,8,256]{3,2,1,0:T(8,128)(2,1)S(1)} %get-tuple-element.26.refs_0_, bf16[8,16,8,256]{3,2,1,0:T(8,128)(2,1)S(1)} %get-tuple-element.28.refs_4_.refs_1_, ...), custom_call_target="tpu_custom_call", output_to_operand_aliasing={{}: (5, {})} | custom-call | flops 134217728 | bytes 1572864 | tf_op jit(solution)/shard_map/pallas_call | solution.py:263
  (3 shorter events, 0.1 us)
Async XLA Ops:
  0.0 22.7 %copy-start.1 = (bf16[3,3,256,256]{3,2,1,0:T(8,128)(2,1)S(1)}, bf16[3,3,256,256]{3,2,1,0:T(8,128)(2,1)}, u32[]{:S(2)}) copy-start(bf16[3,3,256,256]{3,2,1,0:T(8,128)(2,1)} %param.9) | copy-start | bytes 3538948
  0.0 22.7 %copy-start.4 = (f32[256]{0:T(256)S(1)}, f32[256]{0:T(256)}, u32[]{:S(2)}) copy-start(f32[256]{0:T(256)} %param.11) | copy-start | bytes 3076
  2.0 20.7 %collective-permute-start.1 = (bf16[129,8,256]{2,1,0:T(8,128)(2,1)}, bf16[129,8,256]{2,1,0:T(8,128)(2,1)}, u32[]{:S(2)}, u32[]{:S(2)}) collective-permute-start(bf16[129,8,256]{2,1,0:T(8,128)(2,1)} %shard_map.82), channel_id=1, source_target_pairs={{0,8},{8,16},{16,24},{24,32},{32,40},{40,48},{48,56},{56,64},{64,7... | collective-permute-start | bytes 1585160 | tf_op jit(solution)/shard_map/ppermute | solution.py:322
  4.5 18.2 %collective-permute-start = (bf16[129,8,256]{2,1,0:T(8,128)(2,1)}, bf16[129,8,256]{2,1,0:T(8,128)(2,1)}, u32[]{:S(2)}, u32[]{:S(2)}) collective-permute-start(bf16[129,8,256]{2,1,0:T(8,128)(2,1)} %shard_map.82), channel_id=1, source_target_pairs={{0,248},{8,0},{16,8},{24,16},{32,24},{40,32},{48,40},{56,48},{64,5... | collective-permute-start | bytes 1585160 | tf_op jit(solution)/shard_map/ppermute | solution.py:322
  10.7 1.3 %copy-start = (bf16[3,3,256,256]{3,2,1,0:T(8,128)(2,1)S(1)}, bf16[3,3,256,256]{3,2,1,0:T(8,128)(2,1)}, u32[]{:S(2)}) copy-start(bf16[3,3,256,256]{3,2,1,0:T(8,128)(2,1)} %param.9) | copy-start | bytes 3538948
  12.0 1.2 %copy-start.2 = (bf16[1,256,8,256]{3,2,1,0:T(8,128)(2,1)S(1)}, bf16[1,256,8,256]{3,2,1,0:T(8,128)(2,1)}, u32[]{:S(2)}) copy-start(bf16[1,256,8,256]{3,2,1,0:T(8,128)(2,1)} %param.8) | copy-start | bytes 3145732
  13.2 0.7 copy-start.8
  15.7 18.4 %collective-permute-start.3 = (bf16[129,8,256]{2,1,0:T(8,128)(2,1)}, bf16[129,8,256]{2,1,0:T(8,128)(2,1)}, u32[]{:S(2)}, u32[]{:S(2)}) collective-permute-start(bf16[129,8,256]{2,1,0:T(8,128)(2,1)} %get-tuple-element.27), channel_id=1, source_target_pairs={{0,8},{8,16},{16,24},{24,32},{32,40},{40,48},{48,56},{56,64},{64,7... | collective-permute-start | bytes 1585160 | tf_op jit(solution)/shard_map/ppermute | solution.py:322
  15.7 18.4 %collective-permute-start.2 = (bf16[129,8,256]{2,1,0:T(8,128)(2,1)}, bf16[129,8,256]{2,1,0:T(8,128)(2,1)}, u32[]{:S(2)}, u32[]{:S(2)}) collective-permute-start(bf16[129,8,256]{2,1,0:T(8,128)(2,1)} %get-tuple-element.27), channel_id=1, source_target_pairs={{0,248},{8,0},{16,8},{24,16},{32,24},{40,32},{48,40},{56,48},{64,5... | collective-permute-start | bytes 1585160 | tf_op jit(solution)/shard_map/ppermute | solution.py:322
  25.4 11.3 %collective-permute-start.7 = (bf16[2,16,8,256]{3,2,1,0:T(8,128)(2,1)S(1)}, bf16[2,16,8,256]{3,2,1,0:T(8,128)(2,1)S(1)}, u32[]{:S(2)}, u32[]{:S(2)}) collective-permute-start(bf16[2,16,8,256]{3,2,1,0:T(8,128)(2,1)S(1)} %get-tuple-element.34), channel_id=1, source_target_pairs={{0,2},{1,3},{2,4},{3,5},{4,6},{5,7},{6,0},{7,1},{8,10},{9,11},{10,... | collective-permute-start | bytes 393224 | tf_op jit(solution)/shard_map/ppermute | solution.py:288
  26.8 9.9 %collective-permute-start.8 = (bf16[2,16,8,256]{3,2,1,0:T(8,128)(2,1)S(1)}, bf16[2,16,8,256]{3,2,1,0:T(8,128)(2,1)S(1)}, u32[]{:S(2)}, u32[]{:S(2)}) collective-permute-start(bf16[2,16,8,256]{3,2,1,0:T(8,128)(2,1)S(1)} %get-tuple-element.35), channel_id=1, source_target_pairs={{0,4},{1,5},{2,6},{3,7},{4,0},{5,1},{6,2},{7,3},{8,12},{9,13},{10,... | collective-permute-start | bytes 393224 | tf_op jit(solution)/shard_map/ppermute | solution.py:288
  29.4 13.7 %copy-start.5 = (bf16[256,256]{1,0:T(8,128)(2,1)S(1)}, bf16[256,256]{1,0:T(8,128)(2,1)}, u32[]{:S(2)}) copy-start(bf16[256,256]{1,0:T(8,128)(2,1)} %wq_ref.3) | copy-start | bytes 393220
  29.4 13.7 %copy-start.6 = (bf16[256,256]{1,0:T(8,128)(2,1)S(1)}, bf16[256,256]{1,0:T(8,128)(2,1)}, u32[]{:S(2)}) copy-start(bf16[256,256]{1,0:T(8,128)(2,1)} %wk_ref.3) | copy-start | bytes 393220
  29.4 13.7 %copy-start.7 = (bf16[256,256]{1,0:T(8,128)(2,1)S(1)}, bf16[256,256]{1,0:T(8,128)(2,1)}, u32[]{:S(2)}) copy-start(bf16[256,256]{1,0:T(8,128)(2,1)} %wv_ref.3) | copy-start | bytes 393220
  29.4 7.3 %collective-permute-start.9 = (bf16[2,16,8,256]{3,2,1,0:T(8,128)(2,1)S(1)}, bf16[2,16,8,256]{3,2,1,0:T(8,128)(2,1)S(1)}, u32[]{:S(2)}, u32[]{:S(2)}) collective-permute-start(bf16[2,16,8,256]{3,2,1,0:T(8,128)(2,1)S(1)} %get-tuple-element.36), channel_id=1, source_target_pairs={{0,6},{1,7},{2,0},{3,1},{4,2},{5,3},{6,4},{7,5},{8,14},{9,15},{10,... | collective-permute-start | bytes 393224 | tf_op jit(solution)/shard_map/ppermute | solution.py:288
  36.8 6.3 %collective-permute-start.10 = (bf16[4,16,8,256]{3,2,1,0:T(8,128)(2,1)S(1)}, bf16[4,16,8,256]{3,2,1,0:T(8,128)(2,1)S(1)}, u32[]{:S(2)}, u32[]{:S(2)}) collective-permute-start(bf16[4,16,8,256]{3,2,1,0:T(8,128)(2,1)S(1)} %shard_map.86), channel_id=1, source_target_pairs={{0,1},{1,0},{2,3},{3,2},{4,5},{5,4},{6,7},{7,6},{8,9},{9,8},{10,11... | collective-permute-start | bytes 786440 | tf_op jit(solution)/shard_map/ppermute | solution.py:305
  38.1 8.1 %collective-permute-start.4 = (bf16[2,16,8,256]{3,2,1,0:T(8,128)(2,1)S(1)}, bf16[2,16,8,256]{3,2,1,0:T(8,128)(2,1)S(1)}, u32[]{:S(2)}, u32[]{:S(2)}) collective-permute-start(bf16[2,16,8,256]{3,2,1,0:T(8,128)(2,1)S(1)} %get-tuple-element.30), channel_id=1, source_target_pairs={{0,2},{1,3},{2,4},{3,5},{4,6},{5,7},{6,0},{7,1},{8,10},{9,11},{10,... | collective-permute-start | bytes 393224 | tf_op jit(solution)/shard_map/ppermute | solution.py:288
  39.4 9.0 %collective-permute-start.5 = (bf16[2,16,8,256]{3,2,1,0:T(8,128)(2,1)S(1)}, bf16[2,16,8,256]{3,2,1,0:T(8,128)(2,1)S(1)}, u32[]{:S(2)}, u32[]{:S(2)}) collective-permute-start(bf16[2,16,8,256]{3,2,1,0:T(8,128)(2,1)S(1)} %get-tuple-element.31), channel_id=1, source_target_pairs={{0,4},{1,5},{2,6},{3,7},{4,0},{5,1},{6,2},{7,3},{8,12},{9,13},{10,... | collective-permute-start | bytes 393224 | tf_op jit(solution)/shard_map/ppermute | solution.py:288
  42.0 6.4 %collective-permute-start.6 = (bf16[2,16,8,256]{3,2,1,0:T(8,128)(2,1)S(1)}, bf16[2,16,8,256]{3,2,1,0:T(8,128)(2,1)S(1)}, u32[]{:S(2)}, u32[]{:S(2)}) collective-permute-start(bf16[2,16,8,256]{3,2,1,0:T(8,128)(2,1)S(1)} %get-tuple-element.32), channel_id=1, source_target_pairs={{0,6},{1,7},{2,0},{3,1},{4,2},{5,3},{6,4},{7,5},{8,14},{9,15},{10,... | collective-permute-start | bytes 393224 | tf_op jit(solution)/shard_map/ppermute | solution.py:288
  48.4 2.1 %collective-permute-start.11 = (bf16[4,16,8,256]{3,2,1,0:T(8,128)(2,1)S(1)}, bf16[4,16,8,256]{3,2,1,0:T(8,128)(2,1)S(1)}, u32[]{:S(2)}, u32[]{:S(2)}) collective-permute-start(bf16[4,16,8,256]{3,2,1,0:T(8,128)(2,1)S(1)} %shard_map.88), channel_id=1, source_target_pairs={{0,1},{1,0},{2,3},{3,2},{4,5},{5,4},{6,7},{7,6},{8,9},{9,8},{10,11... | collective-permute-start | bytes 786440 | tf_op jit(solution)/shard_map/ppermute | solution.py:305
  50.5 20.9 %copy-start.3 = (bf16[256,256]{1,0:T(8,128)(2,1)S(1)}, bf16[256,256]{1,0:T(8,128)(2,1)}, u32[]{:S(2)}) copy-start(bf16[256,256]{1,0:T(8,128)(2,1)} %w_ref.3) | copy-start | bytes 393220
  53.7 7.6 %collective-permute-start.12 = (bf16[2,32,8,256]{3,2,1,0:T(8,128)(2,1)S(1)}, bf16[2,32,8,256]{3,2,1,0:T(8,128)(2,1)S(1)}, u32[]{:S(2)}, u32[]{:S(2)}) collective-permute-start(bf16[2,32,8,256]{3,2,1,0:T(8,128)(2,1)S(1)} %get-tuple-element.42), channel_id=1, source_target_pairs={{0,6},{1,7},{2,0},{3,1},{4,2},{5,3},{6,4},{7,5},{8,14},{9,15},{10,... | collective-permute-start | bytes 786440 | tf_op jit(solution)/shard_map/ppermute | solution.py:288
  55.5 8.7 %collective-permute-start.13 = (bf16[2,32,8,256]{3,2,1,0:T(8,128)(2,1)S(1)}, bf16[2,32,8,256]{3,2,1,0:T(8,128)(2,1)S(1)}, u32[]{:S(2)}, u32[]{:S(2)}) collective-permute-start(bf16[2,32,8,256]{3,2,1,0:T(8,128)(2,1)S(1)} %get-tuple-element.43), channel_id=1, source_target_pairs={{0,4},{1,5},{2,6},{3,7},{4,0},{5,1},{6,2},{7,3},{8,12},{9,13},{10,... | collective-permute-start | bytes 786440 | tf_op jit(solution)/shard_map/ppermute | solution.py:288
  56.4 14.5 %collective-permute-start.14 = (bf16[2,32,8,256]{3,2,1,0:T(8,128)(2,1)S(1)}, bf16[2,32,8,256]{3,2,1,0:T(8,128)(2,1)S(1)}, u32[]{:S(2)}, u32[]{:S(2)}) collective-permute-start(bf16[2,32,8,256]{3,2,1,0:T(8,128)(2,1)S(1)} %get-tuple-element.44), channel_id=1, source_target_pairs={{0,2},{1,3},{2,4},{3,5},{4,6},{5,7},{6,0},{7,1},{8,10},{9,11},{10,... | collective-permute-start | bytes 786440 | tf_op jit(solution)/shard_map/ppermute | solution.py:288
  70.9 2.3 %collective-permute-start.15 = (bf16[4,32,8,256]{3,2,1,0:T(8,128)(2,1)S(1)}, bf16[4,32,8,256]{3,2,1,0:T(8,128)(2,1)S(1)}, u32[]{:S(2)}, u32[]{:S(2)}) collective-permute-start(bf16[4,32,8,256]{3,2,1,0:T(8,128)(2,1)S(1)} %shard_map.90), channel_id=1, source_target_pairs={{0,1},{1,0},{2,3},{3,2},{4,5},{5,4},{6,7},{7,6},{8,9},{9,8},{10,11... | collective-permute-start | bytes 1572872 | tf_op jit(solution)/shard_map/ppermute | solution.py:305

commit v4 on v3

--- a/solution.py
+++ b/solution.py
@@ -59,10 +59,16 @@
     return jnp.concatenate(out, axis=1)
 
 
-def head_kernel(src, dst, sem):
-    copy = pltpu.make_async_copy(src.at[pl.ds(0, dst.shape[0])], dst, sem)
-    copy.start()
-    copy.wait()
+def head_kernel(src, dst, sems):
+    count, ways = dst.shape[0], sems.shape[0]
+    cuts = [count * i // ways for i in range(ways + 1)]
+    copies = []
+    for i, (low, high) in enumerate(zip(cuts, cuts[1:])):
+        here = pl.ds(low, high - low)
+        copies.append(pltpu.make_async_copy(src.at[here], dst.at[here], sems.at[i]))
+        copies[-1].start()
+    for copy in copies:
+        copy.wait()
 
 
 def head(x, count):
@@ -71,7 +77,7 @@
         out_shape=pltpu.VMEM((count, *x.shape[1:]), x.dtype),
         in_specs=[ANY],
         out_specs=VMEM,
-        scratch_shapes=[pltpu.SemaphoreType.DMA],
+        scratch_shapes=[pltpu.SemaphoreType.DMA((8,))],
         compiler_params=params(4),
         cost_estimate=cost(0, x.size * 2),
     )(pltpu.with_memory_space_constraint(x, pltpu.HBM))
@@ -162,10 +168,6 @@
 
 def attend_kernel(block, chips, wq_ref, wk_ref, wv_ref, *refs):
     ones_ref, outs, far, near = refs[-1], refs[-1 - chips : -1], refs[chips], refs[:chips]
-    earlier = refs[chips + 1 : -1 - chips]
-    for ref, out in zip(earlier, outs):
-        out[:, : ref.shape[1]] = ref[...]
-    behind = earlier[0].shape[1] if earlier else 0
     xs = [x for k in range(chips) for x in (near[k].at[0], far.at[k])]
     parts, (pixels, leads, chans) = len(xs), xs[0].shape
     times, heads = parts * leads, chans // HD
@@ -210,22 +212,21 @@
             attended = mixed[p] / total[p * times : (p + 1) * times]
             attended = attended.astype(BF16).reshape(parts, leads, chans)
             for k in range(parts):
-                outs[k // 2][k % 2, behind + first + p] = attended[k]
-
-
-def attend(near, far, earlier, w_query, w_key, w_value):
+                outs[k // 2][k % 2, first + p] = attended[k]
+
+
+def attend(near, far, w_query, w_key, w_value):
     chips, pixels, leads, chans = far.shape
     size, times = 2 * far.size, 2 * chips * leads
-    behind = earlier[0].shape[1] if earlier else 0
     return pl.pallas_call(
         functools.partial(attend_kernel, math.gcd(pixels, 8), chips),
-        out_shape=[pltpu.VMEM((2, behind + pixels, leads, chans), BF16)] * chips,
-        in_specs=[VMEM] * (4 + chips + len(earlier)),
+        out_shape=[pltpu.VMEM((2, pixels, leads, chans), BF16)] * chips,
+        in_specs=[VMEM] * (4 + chips),
         out_specs=[VMEM] * chips,
         scratch_shapes=[pltpu.VMEM((chans // HD * times, chans), BF16)],
         compiler_params=params(16),
         cost_estimate=cost(size * chans * 20, size * 4 + 6 * chans * chans, size * 2),
-    )(w_query, w_key, w_value, *in_vmem(*near, far, *earlier))
+    )(w_query, w_key, w_value, *in_vmem(*near, far))
 
 
 def out_kernel(starts, core, chips, ids, w_ref, *refs):
@@ -233,7 +234,10 @@
     out_hbm, held, sems = refs[-3:]
     _, count, leads, chans = held.shape
     for i in range(chips):
-        x = refs[i][0] if core == 0 else refs[0][i]
+        if core == 0:
+            x = jnp.concatenate([refs[k * chips + i][0] for k in range(len(starts))], axis=0)
+        else:
+            x = refs[0][i]
         hidden = jnp.concatenate([ref[2 * i + core] for ref in hiddens], axis=0)
         acc = jnp.dot(x.reshape(count * leads, chans), w_ref[...], preferred_element_type=F32)
         acc = acc + hidden.reshape(count * leads, chans).astype(F32)
@@ -277,9 +281,13 @@
     )(*args)
 
 
-def gather_kernel(*refs):
-    for k in range(refs[-1].shape[0]):
-        refs[-1][k] = refs[k][1]
+def gather_kernel(chunks, chips, *refs):
+    out, low = refs[-1], 0
+    for near in [refs[i * chips : (i + 1) * chips] for i in range(chunks)]:
+        width = near[0].shape[1]
+        for k, ref in enumerate(near):
+            out[k, low : low + width] = ref[1]
+        low += width
 
 
 def send(pieces, sign):
@@ -292,16 +300,18 @@
     ]
 
 
-def swap(near, *before):
-    chips, part = len(near), near[0].shape[1:]
+def swap(nears, *before):
+    chips, leads, chans = len(nears[0]), *nears[0][0].shape[2:]
+    count = sum(near[0].shape[1] for near in nears)
+    flat = [x for near in nears for x in near]
     others = pl.pallas_call(
-        gather_kernel,
-        out_shape=pltpu.VMEM((chips, *part), BF16),
-        in_specs=[VMEM] * chips + [ANY] * len(before),
+        functools.partial(gather_kernel, len(nears), chips),
+        out_shape=pltpu.VMEM((chips, count, leads, chans), BF16),
+        in_specs=[VMEM] * len(flat) + [ANY] * len(before),
         out_specs=VMEM,
         compiler_params=params(4),
-        cost_estimate=cost(0, chips * near[0].size * 2),
-    )(*in_vmem(*near), *before)
+        cost_estimate=cost(0, chips * count * leads * chans * 4),
+    )(*in_vmem(*flat), *before)
     return lax.ppermute(others, "lead", [(i, i ^ 1) for i in range(2 * chips)])
 
 
@@ -327,13 +337,13 @@
         hidden, normed = conv_norm(lats, parts, ids, up, down, acc, w_conv, gain, start, count)
         hiddens.append(hidden)
         arrived.append(send(normed, 1))
-    mixed, before = [], hiddens[-1]
+    returned, before = [], hiddens[-1]
     for near in arrived:
-        far = swap(near, before)
-        mixed = attend(near, far, mixed, w_query, w_key, w_value)
+        mixed = attend(near, swap([near], before), w_query, w_key, w_value)
+        returned.append(send(mixed, -1))
         before = mixed[0]
-    near = send(mixed, -1)
-    far = swap(near)
+    far = swap(returned)
+    near = [x for pieces in returned for x in pieces]
     out = project_out(0, ids, near, hiddens, w_out, None, starts, width)
     out = project_out(1, ids, [far], hiddens, w_out, out, starts, width)
     return out[None]

time: 75.3 us -> 72.2 us (0.959)
  waiting for transfers between devices: 23 us -> 16 us
  starting transfers between devices: 29.7 us -> 33.5 us
    ppermute x9 -> x12, waiting for transfers between devices: 16.1 us -> 10.3 us  [send(): lax.ppermute(pieces[k], 'lead', [(i, (i + 2 * sign * k) % (2 * chips)) fo...]
    ppermute x9 -> x12, starting transfers between devices: 13.3 us -> 16.4 us  [send(): lax.ppermute(pieces[k], 'lead', [(i, (i + 2 * sign * k) % (2 * chips)) fo...]
    ppermute x3, waiting for transfers between devices: 1.17 us -> 0.01 us  [swap(): return lax.ppermute(others, 'lead', [(i, i ^ 1) for i in range(2 * chips)])]
  transfers between devices with their start and end apart: 16 -> 19, of which waited for: 7 -> 7; matrix products, arithmetic and copies ran while one was open for 0% -> 0% of each run, Pallas kernels for 16% -> 21%
where the time goes in v4:
time: 72.2 us; the launch traced here: 72 us
  starting transfers between devices  33.5 us (46%)
  Pallas kernels  18.9 us (26%)
  waiting for transfers between devices  16 us (22%)
  local copies, waits for them, and re-layouts  3.19 us (4%)
    ppermute x12, starting transfers between devices, send(): lax.ppermute(pieces[k], 'lead', [(i, (i + 2 * sign * k) % (2 * chips)) fo...  16.4 us
    ppermute x2, starting transfers between devices, shards(): lax.ppermute(piece, 'lat', south)  11 us
    ppermute x12, waiting for transfers between devices, send(): lax.ppermute(pieces[k], 'lead', [(i, (i + 2 * sign * k) % (2 * chips)) fo...  10.3 us
    pallas_call x2, Pallas kernels, attend(): pl.pallas_call(functools.partial(attend_kernel, math.gcd(pixels, 8), chip...  6.24 us
    ppermute x2, waiting for transfers between devices, shards(): lax.ppermute(piece, 'lat', north)  5.72 us
    pallas_call x2, Pallas kernels, conv_norm(): pl.pallas_call(functools.partial(conv_kernel, tile, start - low, start, l...  5.39 us
    ppermute x3, starting transfers between devices, swap(): return lax.ppermute(others, 'lead', [(i, i ^ 1) for i in range(2 * chips)])  3.55 us
    pallas_call x2, Pallas kernels, project_out(): pl.pallas_call(functools.partial(out_kernel, starts, core, chips), out_sh...  3.39 us
  transfers between devices with their start and end apart: 19, of which 7 were waited for; matrix products, arithmetic and copies ran while one was open for 0% of the time, Pallas kernels for 21%

profile of v4, /device:TPU:1, one launch (start us, length us, event | category | flops | bytes accessed | tf_op | source)
XLA Modules:
  0.0 72.0 jit_solution(9194208634493669043)
XLA Ops:
  0.0 0.0 copy-start.1
  0.0 0.0 copy-start.4
  0.0 2.1 %shard_map.82 = bf16[129,8,256]{2,1,0:T(8,128)(2,1)} custom-call(bf16[256,8,256]{2,1,0:T(8,128)(2,1)} %bitcast.10), custom_call_target="tpu_custom_call" | custom-call | bytes 1048576 | tf_op jit(solution)/shard_map/pallas_call | solution.py:75
  2.1 2.5 %collective-permute-start.1 = (bf16[129,8,256]{2,1,0:T(8,128)(2,1)}, bf16[129,8,256]{2,1,0:T(8,128)(2,1)}, u32[]{:S(2)}, u32[]{:S(2)}) collective-permute-start(bf16[129,8,256]{2,1,0:T(8,128)(2,1)} %shard_map.82), channel_id=1, source_target_pairs={{0,8},{8,16},{16,24},{24,32},{32,40},{40,48},{48,56},{56,64},{64,7... | collective-permute-start | bytes 1585160 | tf_op jit(solution)/shard_map/ppermute | solution.py:332
  4.6 6.2 %collective-permute-start = (bf16[129,8,256]{2,1,0:T(8,128)(2,1)}, bf16[129,8,256]{2,1,0:T(8,128)(2,1)}, u32[]{:S(2)}, u32[]{:S(2)}) collective-permute-start(bf16[129,8,256]{2,1,0:T(8,128)(2,1)} %shard_map.82), channel_id=1, source_target_pairs={{0,248},{8,0},{16,8},{24,16},{32,24},{40,32},{48,40},{56,48},{64,5... | collective-permute-start | bytes 1585160 | tf_op jit(solution)/shard_map/ppermute | solution.py:332
  10.8 0.0 copy-start
  10.8 1.3 %copy-done = bf16[3,3,256,256]{3,2,1,0:T(8,128)(2,1)S(1)} copy-done((bf16[3,3,256,256]{3,2,1,0:T(8,128)(2,1)S(1)}, bf16[3,3,256,256]{3,2,1,0:T(8,128)(2,1)}, u32[]{:S(2)}) %copy-start) | copy-done | bytes 1179672
  12.1 0.0 copy-start.2
  12.1 1.2 %copy-done.2 = bf16[1,256,8,256]{3,2,1,0:T(8,128)(2,1)S(1)} copy-done((bf16[1,256,8,256]{3,2,1,0:T(8,128)(2,1)S(1)}, bf16[1,256,8,256]{3,2,1,0:T(8,128)(2,1)}, u32[]{:S(2)}) %copy-start.2) | copy-done | bytes 1048600
  13.3 0.0 copy-start.8
  13.3 0.7 copy-done.8
  14.0 1.7 %shard_map.83 = (f32[2048,256]{1,0:T(8,128)S(1)}, bf16[129,8,256]{2,1,0:T(8,128)(2,1)}) custom-call(bf16[256,8,256]{2,1,0:T(8,128)(2,1)S(1)} %bitcast.11, bf16[9,256,256]{2,1,0:T(8,128)(2,1)S(1)} %bitcast.7, f32[1,256]{1,0:T(1,128)S(1)} %bitcast.14), custom_call_target="tpu_custom_call" | custom-call | flops 805306368 | bytes 3145728 | tf_op jit(solution)/shard_map/pallas_call | solution.py:102
  15.8 0.0 collective-permute-start.3
  15.8 4.8 %collective-permute-start.2 = (bf16[129,8,256]{2,1,0:T(8,128)(2,1)}, bf16[129,8,256]{2,1,0:T(8,128)(2,1)}, u32[]{:S(2)}, u32[]{:S(2)}) collective-permute-start(bf16[129,8,256]{2,1,0:T(8,128)(2,1)} %get-tuple-element.27), channel_id=1, source_target_pairs={{0,248},{8,0},{16,8},{24,16},{32,24},{40,32},{48,40},{56,48},{64,5... | collective-permute-start | bytes 1585160 | tf_op jit(solution)/shard_map/ppermute | solution.py:332
  20.5 0.1 pad_add_fusion.ids
  20.6 2.2 %collective-permute-done.1.up = bf16[129,8,256]{2,1,0:T(8,128)(2,1)} collective-permute-done((bf16[129,8,256]{2,1,0:T(8,128)(2,1)}, bf16[129,8,256]{2,1,0:T(8,128)(2,1)}, u32[]{:S(2)}, u32[]{:S(2)}) %collective-permute-start.1) | collective-permute-done | bytes 528416 | tf_op jit(solution)/shard_map/ppermute | solution.py:332
  22.8 0.0 collective-permute-done.down
  22.8 0.0 copy-done.1
  22.8 0.0 copy-done.4
  22.8 2.7 %shard_map.84 = (bf16[8,16,8,256]{3,2,1,0:T(8,128)(2,1)S(1)}, bf16[2,16,8,256]{3,2,1,0:T(8,128)(2,1)S(1)}, bf16[2,16,8,256]{3,2,1,0:T(8,128)(2,1)S(1)}, bf16[2,1...) custom-call(s32[2]{0:T(128)S(1)} %pad_add_fusion.ids, bf16[129,8,256]{2,1,0:T(8,128)(2,1)} %collective-permute-done.down, ...), custom_call_target="tpu_custom_call" | custom-call | flops 805306368 | bytes 3145728 | tf_op jit(solution)/shard_map/pallas_call | solution.py:156
  25.5 1.4 %collective-permute-start.4 = (bf16[2,16,8,256]{3,2,1,0:T(8,128)(2,1)S(1)}, bf16[2,16,8,256]{3,2,1,0:T(8,128)(2,1)S(1)}, u32[]{:S(2)}, u32[]{:S(2)}) collective-permute-start(bf16[2,16,8,256]{3,2,1,0:T(8,128)(2,1)S(1)} %get-tuple-element.30), channel_id=1, source_target_pairs={{0,2},{1,3},{2,4},{3,5},{4,6},{5,7},{6,0},{7,1},{8,10},{9,11},{10,... | collective-permute-start | bytes 393224 | tf_op jit(solution)/shard_map/ppermute | solution.py:296
  26.9 2.6 %collective-permute-start.5 = (bf16[2,16,8,256]{3,2,1,0:T(8,128)(2,1)S(1)}, bf16[2,16,8,256]{3,2,1,0:T(8,128)(2,1)S(1)}, u32[]{:S(2)}, u32[]{:S(2)}) collective-permute-start(bf16[2,16,8,256]{3,2,1,0:T(8,128)(2,1)S(1)} %get-tuple-element.31), channel_id=1, source_target_pairs={{0,4},{1,5},{2,6},{3,7},{4,0},{5,1},{6,2},{7,3},{8,12},{9,13},{10,... | collective-permute-start | bytes 393224 | tf_op jit(solution)/shard_map/ppermute | solution.py:296
  29.5 0.0 copy-start.5
  29.5 0.0 copy-start.6
  29.5 0.0 copy-start.7
  29.5 1.1 %collective-permute-start.6 = (bf16[2,16,8,256]{3,2,1,0:T(8,128)(2,1)S(1)}, bf16[2,16,8,256]{3,2,1,0:T(8,128)(2,1)S(1)}, u32[]{:S(2)}, u32[]{:S(2)}) collective-permute-start(bf16[2,16,8,256]{3,2,1,0:T(8,128)(2,1)S(1)} %get-tuple-element.32), channel_id=1, source_target_pairs={{0,6},{1,7},{2,0},{3,1},{4,2},{5,3},{6,4},{7,5},{8,14},{9,15},{10,... | collective-permute-start | bytes 393224 | tf_op jit(solution)/shard_map/ppermute | solution.py:296
  30.6 3.5 %collective-permute-done.3.up = bf16[129,8,256]{2,1,0:T(8,128)(2,1)} collective-permute-done((bf16[129,8,256]{2,1,0:T(8,128)(2,1)}, bf16[129,8,256]{2,1,0:T(8,128)(2,1)}, u32[]{:S(2)}, u32[]{:S(2)}) %collective-permute-start.3) | collective-permute-done | bytes 528416 | tf_op jit(solution)/shard_map/ppermute | solution.py:332
  34.1 0.0 collective-permute-done.2.down
  34.1 2.7 %shard_map.85 = (bf16[8,16,8,256]{3,2,1,0:T(8,128)(2,1)S(1)}, bf16[2,16,8,256]{3,2,1,0:T(8,128)(2,1)S(1)}, bf16[2,16,8,256]{3,2,1,0:T(8,128)(2,1)S(1)}, bf16[2,1...) custom-call(s32[2]{0:T(128)S(1)} %pad_add_fusion.ids, bf16[129,8,256]{2,1,0:T(8,128)(2,1)} %collective-permute-done.2.down, ...), custom_call_target="tpu_custom_call" | custom-call | flops 805306368 | bytes 3145728 | tf_op jit(solution)/shard_map/pallas_call | solution.py:156
  36.8 0.0 collective-permute-done.4.refs_1_
  36.8 0.0 collective-permute-done.5.refs_2_
  36.9 0.0 collective-permute-done.6.refs_3_
  36.9 1.3 %collective-permute-start.7 = (bf16[4,16,8,256]{3,2,1,0:T(8,128)(2,1)S(1)}, bf16[4,16,8,256]{3,2,1,0:T(8,128)(2,1)S(1)}, u32[]{:S(2)}, u32[]{:S(2)}) collective-permute-start(bf16[4,16,8,256]{3,2,1,0:T(8,128)(2,1)S(1)} %shard_map.86), channel_id=1, source_target_pairs={{0,1},{1,0},{2,3},{3,2},{4,5},{5,4},{6,7},{7,6},{8,9},{9,8},{10,11... | collective-permute-start | bytes 786440 | tf_op jit(solution)/shard_map/ppermute | solution.py:315
  38.2 1.3 %collective-permute-start.11 = (bf16[2,16,8,256]{3,2,1,0:T(8,128)(2,1)S(1)}, bf16[2,16,8,256]{3,2,1,0:T(8,128)(2,1)S(1)}, u32[]{:S(2)}, u32[]{:S(2)}) collective-permute-start(bf16[2,16,8,256]{3,2,1,0:T(8,128)(2,1)S(1)} %get-tuple-element.38), channel_id=1, source_target_pairs={{0,2},{1,3},{2,4},{3,5},{4,6},{5,7},{6,0},{7,1},{8,10},{9,11},{10,... | collective-permute-start | bytes 393224 | tf_op jit(solution)/shard_map/ppermute | solution.py:296
  39.5 2.6 %collective-permute-start.12 = (bf16[2,16,8,256]{3,2,1,0:T(8,128)(2,1)S(1)}, bf16[2,16,8,256]{3,2,1,0:T(8,128)(2,1)S(1)}, u32[]{:S(2)}, u32[]{:S(2)}) collective-permute-start(bf16[2,16,8,256]{3,2,1,0:T(8,128)(2,1)S(1)} %get-tuple-element.39), channel_id=1, source_target_pairs={{0,4},{1,5},{2,6},{3,7},{4,0},{5,1},{6,2},{7,3},{8,12},{9,13},{10,... | collective-permute-start | bytes 393224 | tf_op jit(solution)/shard_map/ppermute | solution.py:296
  42.1 1.1 %collective-permute-start.13 = (bf16[2,16,8,256]{3,2,1,0:T(8,128)(2,1)S(1)}, bf16[2,16,8,256]{3,2,1,0:T(8,128)(2,1)S(1)}, u32[]{:S(2)}, u32[]{:S(2)}) collective-permute-start(bf16[2,16,8,256]{3,2,1,0:T(8,128)(2,1)S(1)} %get-tuple-element.40), channel_id=1, source_target_pairs={{0,6},{1,7},{2,0},{3,1},{4,2},{5,3},{6,4},{7,5},{8,14},{9,15},{10,... | collective-permute-start | bytes 393224 | tf_op jit(solution)/shard_map/ppermute | solution.py:296
  43.2 0.0 collective-permute-done.7.refs_4_
  43.2 0.0 copy-done.5
  43.2 0.0 copy-done.6
  43.2 0.0 copy-done.7
  43.2 3.1 %shard_map.87 = (bf16[2,16,8,256]{3,2,1,0:T(8,128)(2,1)S(1)}, bf16[2,16,8,256]{3,2,1,0:T(8,128)(2,1)S(1)}, bf16[2,16,8,256]{3,2,1,0:T(8,128)(2,1)S(1)}, bf16[2,16,8,256]{3,2,1,0:T(8,128)(2,1)S(1)}) custom-call(bf16[256,256]{1,0:T(8,128)(2,1)S(1)} %copy-done.5, bf16[256,256]{1,0:T(8,128)(2,1)S(1)} %copy-done.6, bf16[256,256]{1,0:T(8,128)(2,1)S(1)} %copy-done.7, ...), custom_call_target="tpu_custom_call" | custom-call | flops 1342177280 | bytes 1441792 | tf_op jit(solution)/shard_map/pallas_call | solution.py:221
  46.4 0.0 collective-permute-done.11.refs_1_
  46.4 2.2 %collective-permute-done.12.refs_2_ = bf16[2,16,8,256]{3,2,1,0:T(8,128)(2,1)S(1)} collective-permute-done((bf16[2,16,8,256]{3,2,1,0:T(8,128)(2,1)S(1)}, bf16[2,16,8,256]{3,2,1,0:T(8,128)(2,1)S(1)}, u32[]{:S(2)}, u32[]{:S(2)}) %collective-permute-start.12) | collective-permute-done | bytes 131104 | tf_op jit(solution)/shard_map/ppermute | solution.py:296
  48.5 0.0 collective-permute-done.13.refs_3_
  48.6 1.0 %collective-permute-start.14 = (bf16[4,16,8,256]{3,2,1,0:T(8,128)(2,1)S(1)}, bf16[4,16,8,256]{3,2,1,0:T(8,128)(2,1)S(1)}, u32[]{:S(2)}, u32[]{:S(2)}) collective-permute-start(bf16[4,16,8,256]{3,2,1,0:T(8,128)(2,1)S(1)} %shard_map.88), channel_id=1, source_target_pairs={{0,1},{1,0},{2,3},{3,2},{4,5},{5,4},{6,7},{7,6},{8,9},{9,8},{10,11... | collective-permute-start | bytes 786440 | tf_op jit(solution)/shard_map/ppermute | solution.py:315
  49.5 1.8 %collective-permute-start.8 = (bf16[2,16,8,256]{3,2,1,0:T(8,128)(2,1)S(1)}, bf16[2,16,8,256]{3,2,1,0:T(8,128)(2,1)S(1)}, u32[]{:S(2)}, u32[]{:S(2)}) collective-permute-start(bf16[2,16,8,256]{3,2,1,0:T(8,128)(2,1)S(1)} %get-tuple-element.34), channel_id=1, source_target_pairs={{0,6},{1,7},{2,0},{3,1},{4,2},{5,3},{6,4},{7,5},{8,14},{9,15},{10,... | collective-permute-start | bytes 393224 | tf_op jit(solution)/shard_map/ppermute | solution.py:296
  51.3 0.9 %collective-permute-start.9 = (bf16[2,16,8,256]{3,2,1,0:T(8,128)(2,1)S(1)}, bf16[2,16,8,256]{3,2,1,0:T(8,128)(2,1)S(1)}, u32[]{:S(2)}, u32[]{:S(2)}) collective-permute-start(bf16[2,16,8,256]{3,2,1,0:T(8,128)(2,1)S(1)} %get-tuple-element.35), channel_id=1, source_target_pairs={{0,4},{1,5},{2,6},{3,7},{4,0},{5,1},{6,2},{7,3},{8,12},{9,13},{10,... | collective-permute-start | bytes 393224 | tf_op jit(solution)/shard_map/ppermute | solution.py:296
  52.2 0.5 collective-permute-start.10
  52.7 0.0 collective-permute-done.14.refs_4_
  52.7 3.1 %shard_map.89 = (bf16[2,16,8,256]{3,2,1,0:T(8,128)(2,1)S(1)}, bf16[2,16,8,256]{3,2,1,0:T(8,128)(2,1)S(1)}, bf16[2,16,8,256]{3,2,1,0:T(8,128)(2,1)S(1)}, bf16[2,16,8,256]{3,2,1,0:T(8,128)(2,1)S(1)}) custom-call(bf16[256,256]{1,0:T(8,128)(2,1)S(1)} %copy-done.5, bf16[256,256]{1,0:T(8,128)(2,1)S(1)} %copy-done.6, bf16[256,256]{1,0:T(8,128)(2,1)S(1)} %copy-done.7, ...), custom_call_target="tpu_custom_call" | custom-call | flops 1342177280 | bytes 1441792 | tf_op jit(solution)/shard_map/pallas_call | solution.py:221
  55.8 2.2 %collective-permute-start.15 = (bf16[2,16,8,256]{3,2,1,0:T(8,128)(2,1)S(1)}, bf16[2,16,8,256]{3,2,1,0:T(8,128)(2,1)S(1)}, u32[]{:S(2)}, u32[]{:S(2)}) collective-permute-start(bf16[2,16,8,256]{3,2,1,0:T(8,128)(2,1)S(1)} %get-tuple-element.42), channel_id=1, source_target_pairs={{0,6},{1,7},{2,0},{3,1},{4,2},{5,3},{6,4},{7,5},{8,14},{9,15},{10,... | collective-permute-start | bytes 393224 | tf_op jit(solution)/shard_map/ppermute | solution.py:296
  58.0 0.9 %collective-permute-start.16 = (bf16[2,16,8,256]{3,2,1,0:T(8,128)(2,1)S(1)}, bf16[2,16,8,256]{3,2,1,0:T(8,128)(2,1)S(1)}, u32[]{:S(2)}, u32[]{:S(2)}) collective-permute-start(bf16[2,16,8,256]{3,2,1,0:T(8,128)(2,1)S(1)} %get-tuple-element.43), channel_id=1, source_target_pairs={{0,4},{1,5},{2,6},{3,7},{4,0},{5,1},{6,2},{7,3},{8,12},{9,13},{10,... | collective-permute-start | bytes 393224 | tf_op jit(solution)/shard_map/ppermute | solution.py:296
  58.9 0.0 collective-permute-done.8.refs_1_.refs_3_
  58.9 0.0 collective-permute-start.17
  58.9 0.0 collective-permute-done.9.refs_2_.refs_4_
  58.9 2.1 %collective-permute-done.10.refs_3_.refs_5_ = bf16[2,16,8,256]{3,2,1,0:T(8,128)(2,1)S(1)} collective-permute-done((bf16[2,16,8,256]{3,2,1,0:T(8,128)(2,1)S(1)}, bf16[2,16,8,256]{3,2,1,0:T(8,128)(2,1)S(1)}, u32[]{:S(2)}, u32[]{:S(2)}) %collective-permute-start.10) | collective-permute-done | bytes 131104 | tf_op jit(solution)/shard_map/ppermute | solution.py:296
  61.0 0.3 collective-permute-done.15.refs_5_.refs_7_
  61.4 2.1 %collective-permute-done.16.refs_6_.refs_8_ = bf16[2,16,8,256]{3,2,1,0:T(8,128)(2,1)S(1)} collective-permute-done((bf16[2,16,8,256]{3,2,1,0:T(8,128)(2,1)S(1)}, bf16[2,16,8,256]{3,2,1,0:T(8,128)(2,1)S(1)}, u32[]{:S(2)}, u32[]{:S(2)}) %collective-permute-start.16) | collective-permute-done | bytes 131104 | tf_op jit(solution)/shard_map/ppermute | solution.py:296
  63.4 3.6 %collective-permute-done.17.refs_7_.refs_9_ = bf16[2,16,8,256]{3,2,1,0:T(8,128)(2,1)S(1)} collective-permute-done((bf16[2,16,8,256]{3,2,1,0:T(8,128)(2,1)S(1)}, bf16[2,16,8,256]{3,2,1,0:T(8,128)(2,1)S(1)}, u32[]{:S(2)}, u32[]{:S(2)}) %collective-permute-start.17) | collective-permute-done | bytes 131104 | tf_op jit(solution)/shard_map/ppermute | solution.py:296
  67.1 1.3 %collective-permute-start.18 = (bf16[4,32,8,256]{3,2,1,0:T(8,128)(2,1)S(1)}, bf16[4,32,8,256]{3,2,1,0:T(8,128)(2,1)S(1)}, u32[]{:S(2)}, u32[]{:S(2)}) collective-permute-start(bf16[4,32,8,256]{3,2,1,0:T(8,128)(2,1)S(1)} %shard_map.90), channel_id=1, source_target_pairs={{0,1},{1,0},{2,3},{3,2},{4,5},{5,4},{6,7},{7,6},{8,9},{9,8},{10,11... | collective-permute-start | bytes 1572872 | tf_op jit(solution)/shard_map/ppermute | solution.py:315
  68.4 0.0 copy-done.3
  68.4 1.7 %shard_map.91.refs_3_ = bf16[256,8,256]{2,1,0:T(8,128)(2,1)} custom-call(s32[2]{0:T(128)S(1)} %pad_add_fusion.ids, bf16[256,256]{1,0:T(8,128)(2,1)S(1)} %copy-done.3, bf16[8,16,8,256]{3,2,1,0:T(8,128)(2,1)S(1)} %get-tuple-element.26.refs_0_, bf16[8,16,8,256]{3,2,1,0:T(8,128)(2,1)S(1)} %get-tuple-element.28.refs_4_.refs_1_, ...), custom_call_target="tpu_custom_call" | custom-call | flops 134217728 | bytes 1572864 | tf_op jit(solution)/shard_map/pallas_call | solution.py:267
  70.1 0.0 collective-permute-done.18.refs_2_
  70.1 1.7 %shard_map.92 = bf16[256,8,256]{2,1,0:T(8,128)(2,1)} custom-call(s32[2]{0:T(128)S(1)} %pad_add_fusion.ids, bf16[256,256]{1,0:T(8,128)(2,1)S(1)} %copy-done.3, bf16[8,16,8,256]{3,2,1,0:T(8,128)(2,1)S(1)} %get-tuple-element.26.refs_0_, bf16[8,16,8,256]{3,2,1,0:T(8,128)(2,1)S(1)} %get-tuple-element.28.refs_4_.refs_1_, ...), custom_call_target="tpu_custom_call", output_to_operand_aliasing={{}: (5, {})} | custom-call | flops 134217728 | bytes 1572864 | tf_op jit(solution)/shard_map/pallas_call | solution.py:267
  (4 shorter events, 0.1 us)
Async XLA Ops:
  0.0 22.8 %copy-start.1 = (bf16[3,3,256,256]{3,2,1,0:T(8,128)(2,1)S(1)}, bf16[3,3,256,256]{3,2,1,0:T(8,128)(2,1)}, u32[]{:S(2)}) copy-start(bf16[3,3,256,256]{3,2,1,0:T(8,128)(2,1)} %param.9) | copy-start | bytes 3538948
  0.0 22.8 %copy-start.4 = (f32[256]{0:T(256)S(1)}, f32[256]{0:T(256)}, u32[]{:S(2)}) copy-start(f32[256]{0:T(256)} %param.11) | copy-start | bytes 3076
  2.1 20.7 %collective-permute-start.1 = (bf16[129,8,256]{2,1,0:T(8,128)(2,1)}, bf16[129,8,256]{2,1,0:T(8,128)(2,1)}, u32[]{:S(2)}, u32[]{:S(2)}) collective-permute-start(bf16[129,8,256]{2,1,0:T(8,128)(2,1)} %shard_map.82), channel_id=1, source_target_pairs={{0,8},{8,16},{16,24},{24,32},{32,40},{40,48},{48,56},{56,64},{64,7... | collective-permute-start | bytes 1585160 | tf_op jit(solution)/shard_map/ppermute | solution.py:332
  4.6 18.2 %collective-permute-start = (bf16[129,8,256]{2,1,0:T(8,128)(2,1)}, bf16[129,8,256]{2,1,0:T(8,128)(2,1)}, u32[]{:S(2)}, u32[]{:S(2)}) collective-permute-start(bf16[129,8,256]{2,1,0:T(8,128)(2,1)} %shard_map.82), channel_id=1, source_target_pairs={{0,248},{8,0},{16,8},{24,16},{32,24},{40,32},{48,40},{56,48},{64,5... | collective-permute-start | bytes 1585160 | tf_op jit(solution)/shard_map/ppermute | solution.py:332
  10.8 1.3 %copy-start = (bf16[3,3,256,256]{3,2,1,0:T(8,128)(2,1)S(1)}, bf16[3,3,256,256]{3,2,1,0:T(8,128)(2,1)}, u32[]{:S(2)}) copy-start(bf16[3,3,256,256]{3,2,1,0:T(8,128)(2,1)} %param.9) | copy-start | bytes 3538948
  12.1 1.2 %copy-start.2 = (bf16[1,256,8,256]{3,2,1,0:T(8,128)(2,1)S(1)}, bf16[1,256,8,256]{3,2,1,0:T(8,128)(2,1)}, u32[]{:S(2)}) copy-start(bf16[1,256,8,256]{3,2,1,0:T(8,128)(2,1)} %param.8) | copy-start | bytes 3145732
  13.3 0.7 copy-start.8
  15.8 18.4 %collective-permute-start.3 = (bf16[129,8,256]{2,1,0:T(8,128)(2,1)}, bf16[129,8,256]{2,1,0:T(8,128)(2,1)}, u32[]{:S(2)}, u32[]{:S(2)}) collective-permute-start(bf16[129,8,256]{2,1,0:T(8,128)(2,1)} %get-tuple-element.27), channel_id=1, source_target_pairs={{0,8},{8,16},{16,24},{24,32},{32,40},{40,48},{48,56},{56,64},{64,7... | collective-permute-start | bytes 1585160 | tf_op jit(solution)/shard_map/ppermute | solution.py:332
  15.8 18.4 %collective-permute-start.2 = (bf16[129,8,256]{2,1,0:T(8,128)(2,1)}, bf16[129,8,256]{2,1,0:T(8,128)(2,1)}, u32[]{:S(2)}, u32[]{:S(2)}) collective-permute-start(bf16[129,8,256]{2,1,0:T(8,128)(2,1)} %get-tuple-element.27), channel_id=1, source_target_pairs={{0,248},{8,0},{16,8},{24,16},{32,24},{40,32},{48,40},{56,48},{64,5... | collective-permute-start | bytes 1585160 | tf_op jit(solution)/shard_map/ppermute | solution.py:332
  25.5 11.3 %collective-permute-start.4 = (bf16[2,16,8,256]{3,2,1,0:T(8,128)(2,1)S(1)}, bf16[2,16,8,256]{3,2,1,0:T(8,128)(2,1)S(1)}, u32[]{:S(2)}, u32[]{:S(2)}) collective-permute-start(bf16[2,16,8,256]{3,2,1,0:T(8,128)(2,1)S(1)} %get-tuple-element.30), channel_id=1, source_target_pairs={{0,2},{1,3},{2,4},{3,5},{4,6},{5,7},{6,0},{7,1},{8,10},{9,11},{10,... | collective-permute-start | bytes 393224 | tf_op jit(solution)/shard_map/ppermute | solution.py:296
  26.9 9.9 %collective-permute-start.5 = (bf16[2,16,8,256]{3,2,1,0:T(8,128)(2,1)S(1)}, bf16[2,16,8,256]{3,2,1,0:T(8,128)(2,1)S(1)}, u32[]{:S(2)}, u32[]{:S(2)}) collective-permute-start(bf16[2,16,8,256]{3,2,1,0:T(8,128)(2,1)S(1)} %get-tuple-element.31), channel_id=1, source_target_pairs={{0,4},{1,5},{2,6},{3,7},{4,0},{5,1},{6,2},{7,3},{8,12},{9,13},{10,... | collective-permute-start | bytes 393224 | tf_op jit(solution)/shard_map/ppermute | solution.py:296
  29.5 13.7 %copy-start.5 = (bf16[256,256]{1,0:T(8,128)(2,1)S(1)}, bf16[256,256]{1,0:T(8,128)(2,1)}, u32[]{:S(2)}) copy-start(bf16[256,256]{1,0:T(8,128)(2,1)} %wq_ref.3) | copy-start | bytes 393220
  29.5 13.7 %copy-start.6 = (bf16[256,256]{1,0:T(8,128)(2,1)S(1)}, bf16[256,256]{1,0:T(8,128)(2,1)}, u32[]{:S(2)}) copy-start(bf16[256,256]{1,0:T(8,128)(2,1)} %wk_ref.3) | copy-start | bytes 393220
  29.5 13.7 %copy-start.7 = (bf16[256,256]{1,0:T(8,128)(2,1)S(1)}, bf16[256,256]{1,0:T(8,128)(2,1)}, u32[]{:S(2)}) copy-start(bf16[256,256]{1,0:T(8,128)(2,1)} %wv_ref.3) | copy-start | bytes 393220
  29.5 7.3 %collective-permute-start.6 = (bf16[2,16,8,256]{3,2,1,0:T(8,128)(2,1)S(1)}, bf16[2,16,8,256]{3,2,1,0:T(8,128)(2,1)S(1)}, u32[]{:S(2)}, u32[]{:S(2)}) collective-permute-start(bf16[2,16,8,256]{3,2,1,0:T(8,128)(2,1)S(1)} %get-tuple-element.32), channel_id=1, source_target_pairs={{0,6},{1,7},{2,0},{3,1},{4,2},{5,3},{6,4},{7,5},{8,14},{9,15},{10,... | collective-permute-start | bytes 393224 | tf_op jit(solution)/shard_map/ppermute | solution.py:296
  36.9 6.3 %collective-permute-start.7 = (bf16[4,16,8,256]{3,2,1,0:T(8,128)(2,1)S(1)}, bf16[4,16,8,256]{3,2,1,0:T(8,128)(2,1)S(1)}, u32[]{:S(2)}, u32[]{:S(2)}) collective-permute-start(bf16[4,16,8,256]{3,2,1,0:T(8,128)(2,1)S(1)} %shard_map.86), channel_id=1, source_target_pairs={{0,1},{1,0},{2,3},{3,2},{4,5},{5,4},{6,7},{7,6},{8,9},{9,8},{10,11... | collective-permute-start | bytes 786440 | tf_op jit(solution)/shard_map/ppermute | solution.py:315
  38.2 8.2 %collective-permute-start.11 = (bf16[2,16,8,256]{3,2,1,0:T(8,128)(2,1)S(1)}, bf16[2,16,8,256]{3,2,1,0:T(8,128)(2,1)S(1)}, u32[]{:S(2)}, u32[]{:S(2)}) collective-permute-start(bf16[2,16,8,256]{3,2,1,0:T(8,128)(2,1)S(1)} %get-tuple-element.38), channel_id=1, source_target_pairs={{0,2},{1,3},{2,4},{3,5},{4,6},{5,7},{6,0},{7,1},{8,10},{9,11},{10,... | collective-permute-start | bytes 393224 | tf_op jit(solution)/shard_map/ppermute | solution.py:296
  39.5 9.0 %collective-permute-start.12 = (bf16[2,16,8,256]{3,2,1,0:T(8,128)(2,1)S(1)}, bf16[2,16,8,256]{3,2,1,0:T(8,128)(2,1)S(1)}, u32[]{:S(2)}, u32[]{:S(2)}) collective-permute-start(bf16[2,16,8,256]{3,2,1,0:T(8,128)(2,1)S(1)} %get-tuple-element.39), channel_id=1, source_target_pairs={{0,4},{1,5},{2,6},{3,7},{4,0},{5,1},{6,2},{7,3},{8,12},{9,13},{10,... | collective-permute-start | bytes 393224 | tf_op jit(solution)/shard_map/ppermute | solution.py:296
  42.1 6.4 %collective-permute-start.13 = (bf16[2,16,8,256]{3,2,1,0:T(8,128)(2,1)S(1)}, bf16[2,16,8,256]{3,2,1,0:T(8,128)(2,1)S(1)}, u32[]{:S(2)}, u32[]{:S(2)}) collective-permute-start(bf16[2,16,8,256]{3,2,1,0:T(8,128)(2,1)S(1)} %get-tuple-element.40), channel_id=1, source_target_pairs={{0,6},{1,7},{2,0},{3,1},{4,2},{5,3},{6,4},{7,5},{8,14},{9,15},{10,... | collective-permute-start | bytes 393224 | tf_op jit(solution)/shard_map/ppermute | solution.py:296
  48.6 4.1 %collective-permute-start.14 = (bf16[4,16,8,256]{3,2,1,0:T(8,128)(2,1)S(1)}, bf16[4,16,8,256]{3,2,1,0:T(8,128)(2,1)S(1)}, u32[]{:S(2)}, u32[]{:S(2)}) collective-permute-start(bf16[4,16,8,256]{3,2,1,0:T(8,128)(2,1)S(1)} %shard_map.88), channel_id=1, source_target_pairs={{0,1},{1,0},{2,3},{3,2},{4,5},{5,4},{6,7},{7,6},{8,9},{9,8},{10,11... | collective-permute-start | bytes 786440 | tf_op jit(solution)/shard_map/ppermute | solution.py:315
  49.5 9.4 %collective-permute-start.8 = (bf16[2,16,8,256]{3,2,1,0:T(8,128)(2,1)S(1)}, bf16[2,16,8,256]{3,2,1,0:T(8,128)(2,1)S(1)}, u32[]{:S(2)}, u32[]{:S(2)}) collective-permute-start(bf16[2,16,8,256]{3,2,1,0:T(8,128)(2,1)S(1)} %get-tuple-element.34), channel_id=1, source_target_pairs={{0,6},{1,7},{2,0},{3,1},{4,2},{5,3},{6,4},{7,5},{8,14},{9,15},{10,... | collective-permute-start | bytes 393224 | tf_op jit(solution)/shard_map/ppermute | solution.py:296
  51.3 7.7 %collective-permute-start.9 = (bf16[2,16,8,256]{3,2,1,0:T(8,128)(2,1)S(1)}, bf16[2,16,8,256]{3,2,1,0:T(8,128)(2,1)S(1)}, u32[]{:S(2)}, u32[]{:S(2)}) collective-permute-start(bf16[2,16,8,256]{3,2,1,0:T(8,128)(2,1)S(1)} %get-tuple-element.35), channel_id=1, source_target_pairs={{0,4},{1,5},{2,6},{3,7},{4,0},{5,1},{6,2},{7,3},{8,12},{9,13},{10,... | collective-permute-start | bytes 393224 | tf_op jit(solution)/shard_map/ppermute | solution.py:296
  52.2 16.2 %copy-start.3 = (bf16[256,256]{1,0:T(8,128)(2,1)S(1)}, bf16[256,256]{1,0:T(8,128)(2,1)}, u32[]{:S(2)}) copy-start(bf16[256,256]{1,0:T(8,128)(2,1)} %w_ref.3) | copy-start | bytes 393220
  52.2 8.9 %collective-permute-start.10 = (bf16[2,16,8,256]{3,2,1,0:T(8,128)(2,1)S(1)}, bf16[2,16,8,256]{3,2,1,0:T(8,128)(2,1)S(1)}, u32[]{:S(2)}, u32[]{:S(2)}) collective-permute-start(bf16[2,16,8,256]{3,2,1,0:T(8,128)(2,1)S(1)} %get-tuple-element.36), channel_id=1, source_target_pairs={{0,2},{1,3},{2,4},{3,5},{4,6},{5,7},{6,0},{7,1},{8,10},{9,11},{10,... | collective-permute-start | bytes 393224 | tf_op jit(solution)/shard_map/ppermute | solution.py:296
  55.8 5.5 %collective-permute-start.15 = (bf16[2,16,8,256]{3,2,1,0:T(8,128)(2,1)S(1)}, bf16[2,16,8,256]{3,2,1,0:T(8,128)(2,1)S(1)}, u32[]{:S(2)}, u32[]{:S(2)}) collective-permute-start(bf16[2,16,8,256]{3,2,1,0:T(8,128)(2,1)S(1)} %get-tuple-element.42), channel_id=1, source_target_pairs={{0,6},{1,7},{2,0},{3,1},{4,2},{5,3},{6,4},{7,5},{8,14},{9,15},{10,... | collective-permute-start | bytes 393224 | tf_op jit(solution)/shard_map/ppermute | solution.py:296
  58.0 5.4 %collective-permute-start.16 = (bf16[2,16,8,256]{3,2,1,0:T(8,128)(2,1)S(1)}, bf16[2,16,8,256]{3,2,1,0:T(8,128)(2,1)S(1)}, u32[]{:S(2)}, u32[]{:S(2)}) collective-permute-start(bf16[2,16,8,256]{3,2,1,0:T(8,128)(2,1)S(1)} %get-tuple-element.43), channel_id=1, source_target_pairs={{0,4},{1,5},{2,6},{3,7},{4,0},{5,1},{6,2},{7,3},{8,12},{9,13},{10,... | collective-permute-start | bytes 393224 | tf_op jit(solution)/shard_map/ppermute | solution.py:296
  58.9 8.1 %collective-permute-start.17 = (bf16[2,16,8,256]{3,2,1,0:T(8,128)(2,1)S(1)}, bf16[2,16,8,256]{3,2,1,0:T(8,128)(2,1)S(1)}, u32[]{:S(2)}, u32[]{:S(2)}) collective-permute-start(bf16[2,16,8,256]{3,2,1,0:T(8,128)(2,1)S(1)} %get-tuple-element.44), channel_id=1, source_target_pairs={{0,2},{1,3},{2,4},{3,5},{4,6},{5,7},{6,0},{7,1},{8,10},{9,11},{10,... | collective-permute-start | bytes 393224 | tf_op jit(solution)/shard_map/ppermute | solution.py:296
  67.1 3.0 %collective-permute-start.18 = (bf16[4,32,8,256]{3,2,1,0:T(8,128)(2,1)S(1)}, bf16[4,32,8,256]{3,2,1,0:T(8,128)(2,1)S(1)}, u32[]{:S(2)}, u32[]{:S(2)}) collective-permute-start(bf16[4,32,8,256]{3,2,1,0:T(8,128)(2,1)S(1)} %shard_map.90), channel_id=1, source_target_pairs={{0,1},{1,0},{2,3},{3,2},{4,5},{5,4},{6,7},{7,6},{8,9},{9,8},{10,11... | collective-permute-start | bytes 1572872 | tf_op jit(solution)/shard_map/ppermute | solution.py:315

commit v5 on v4

--- a/solution.py
+++ b/solution.py
@@ -74,9 +74,9 @@
 def head(x, count):
     return pl.pallas_call(
         head_kernel,
-        out_shape=pltpu.VMEM((count, *x.shape[1:]), x.dtype),
+        out_shape=pltpu.HBM((count, *x.shape[1:]), x.dtype),
         in_specs=[ANY],
-        out_specs=VMEM,
+        out_specs=ANY,
         scratch_shapes=[pltpu.SemaphoreType.DMA((8,))],
         compiler_params=params(4),
         cost_estimate=cost(0, x.size * 2),
@@ -111,8 +111,8 @@
 
 
 def place(lead, parts, k):
-    chip, core = lax.div(lead, 2), lax.rem(lead, 2)
-    return 2 * lax.rem(chip + k // 2, parts // 2) + (core if k % 2 == 0 else 1 - core)
+    chip = jnp.bitwise_and(lax.shift_right_logical(lead, 1) + k // 2, parts // 2 - 1)
+    return 2 * chip + jnp.bitwise_xor(jnp.bitwise_and(lead, 1), k % 2)
 
 
 def conv_kernel(tile, offset, start, lats, ids, down, up, acc_in, weight, gain, hidden_out, *refs):
@@ -219,7 +219,7 @@
     chips, pixels, leads, chans = far.shape
     size, times = 2 * far.size, 2 * chips * leads
     return pl.pallas_call(
-        functools.partial(attend_kernel, math.gcd(pixels, 8), chips),
+        functools.partial(attend_kernel, math.gcd(pixels, 16), chips),
         out_shape=[pltpu.VMEM((2, pixels, leads, chans), BF16)] * chips,
         in_specs=[VMEM] * (4 + chips),
         out_specs=[VMEM] * chips,

time: 72.2 us -> 87.2 us (1.21)
  Pallas kernels: 18.9 us -> 33.8 us
    pallas_call x3, Pallas kernels: 8.3 us -> 23.1 us  [the longest x1 17.2 us: head(): pl.pallas_call(head_kernel, out_shape=pltpu.HBM((count, *x.shape[1:]), x....]
  transfers between devices with their start and end apart: 19 -> 19, of which waited for: 7 -> 7; matrix products, arithmetic and copies ran while one was open for 0% -> 0% of each run, Pallas kernels for 21% -> 17%
where the time goes in v5:
time: 87.2 us; the launch traced here: 86.9 us
  Pallas kernels  33.8 us (39%)
  starting transfers between devices  33.5 us (38%)
  waiting for transfers between devices  16.1 us (18%)
  local copies, waits for them, and re-layouts  3.19 us (4%)
    pallas_call x1, Pallas kernels, head(): pl.pallas_call(head_kernel, out_shape=pltpu.HBM((count, *x.shape[1:]), x....  17.2 us
    ppermute x12, starting transfers between devices, send(): lax.ppermute(pieces[k], 'lead', [(i, (i + 2 * sign * k) % (2 * chips)) fo...  16.4 us
    ppermute x2, starting transfers between devices, shards(): lax.ppermute(piece, 'lat', south)  11 us
    ppermute x12, waiting for transfers between devices, send(): lax.ppermute(pieces[k], 'lead', [(i, (i + 2 * sign * k) % (2 * chips)) fo...  10.5 us
    pallas_call x2, Pallas kernels, attend(): pl.pallas_call(functools.partial(attend_kernel, math.gcd(pixels, 16), chi...  5.91 us
    ppermute x2, waiting for transfers between devices, shards(): lax.ppermute(piece, 'lat', north)  5.66 us
    pallas_call x2, Pallas kernels, conv_norm(): pl.pallas_call(functools.partial(conv_kernel, tile, start - low, start, l...  5.5 us
    ppermute x3, starting transfers between devices, swap(): return lax.ppermute(others, 'lead', [(i, i ^ 1) for i in range(2 * chips)])  3.53 us
  transfers between devices with their start and end apart: 19, of which 7 were waited for; matrix products, arithmetic and copies ran while one was open for 0% of the time, Pallas kernels for 17%

profile of v5, /device:TPU:1, one launch (start us, length us, event | category | flops | bytes accessed | tf_op | source)
XLA Modules:
  0.0 86.9 jit_solution(3005989950948343820)
XLA Ops:
  0.0 0.0 copy-start.1
  0.0 0.0 copy-start.4
  0.0 17.2 %shard_map.82 = bf16[129,8,256]{2,1,0:T(8,128)(2,1)} custom-call(bf16[256,8,256]{2,1,0:T(8,128)(2,1)} %bitcast.10), custom_call_target="tpu_custom_call" | custom-call | bytes 1048576 | tf_op jit(solution)/shard_map/pallas_call | solution.py:75
  17.2 2.5 %collective-permute-start.1 = (bf16[129,8,256]{2,1,0:T(8,128)(2,1)}, bf16[129,8,256]{2,1,0:T(8,128)(2,1)}, u32[]{:S(2)}, u32[]{:S(2)}) collective-permute-start(bf16[129,8,256]{2,1,0:T(8,128)(2,1)} %shard_map.82), channel_id=1, source_target_pairs={{0,8},{8,16},{16,24},{24,32},{32,40},{40,48},{48,56},{56,64},{64,7... | collective-permute-start | bytes 1585160 | tf_op jit(solution)/shard_map/ppermute | solution.py:332
  19.7 6.2 %collective-permute-start = (bf16[129,8,256]{2,1,0:T(8,128)(2,1)}, bf16[129,8,256]{2,1,0:T(8,128)(2,1)}, u32[]{:S(2)}, u32[]{:S(2)}) collective-permute-start(bf16[129,8,256]{2,1,0:T(8,128)(2,1)} %shard_map.82), channel_id=1, source_target_pairs={{0,248},{8,0},{16,8},{24,16},{32,24},{40,32},{48,40},{56,48},{64,5... | collective-permute-start | bytes 1585160 | tf_op jit(solution)/shard_map/ppermute | solution.py:332
  26.0 0.0 copy-start
  26.0 1.3 %copy-done = bf16[3,3,256,256]{3,2,1,0:T(8,128)(2,1)S(1)} copy-done((bf16[3,3,256,256]{3,2,1,0:T(8,128)(2,1)S(1)}, bf16[3,3,256,256]{3,2,1,0:T(8,128)(2,1)}, u32[]{:S(2)}) %copy-start) | copy-done | bytes 1179672
  27.2 0.0 copy-start.2
  27.2 1.2 %copy-done.2 = bf16[1,256,8,256]{3,2,1,0:T(8,128)(2,1)S(1)} copy-done((bf16[1,256,8,256]{3,2,1,0:T(8,128)(2,1)S(1)}, bf16[1,256,8,256]{3,2,1,0:T(8,128)(2,1)}, u32[]{:S(2)}) %copy-start.2) | copy-done | bytes 1048600
  28.5 0.0 copy-start.8
  28.5 0.7 copy-done.8
  29.1 1.7 %shard_map.83 = (f32[2048,256]{1,0:T(8,128)S(1)}, bf16[129,8,256]{2,1,0:T(8,128)(2,1)}) custom-call(bf16[256,8,256]{2,1,0:T(8,128)(2,1)S(1)} %bitcast.11, bf16[9,256,256]{2,1,0:T(8,128)(2,1)S(1)} %bitcast.7, f32[1,256]{1,0:T(1,128)S(1)} %bitcast.14), custom_call_target="tpu_custom_call" | custom-call | flops 805306368 | bytes 3145728 | tf_op jit(solution)/shard_map/pallas_call | solution.py:102
  30.9 0.0 collective-permute-start.3
  30.9 4.8 %collective-permute-start.2 = (bf16[129,8,256]{2,1,0:T(8,128)(2,1)}, bf16[129,8,256]{2,1,0:T(8,128)(2,1)}, u32[]{:S(2)}, u32[]{:S(2)}) collective-permute-start(bf16[129,8,256]{2,1,0:T(8,128)(2,1)} %get-tuple-element.27), channel_id=1, source_target_pairs={{0,248},{8,0},{16,8},{24,16},{32,24},{40,32},{48,40},{56,48},{64,5... | collective-permute-start | bytes 1585160 | tf_op jit(solution)/shard_map/ppermute | solution.py:332
  35.7 0.1 pad_add_fusion.ids
  35.7 2.2 %collective-permute-done.1.up = bf16[129,8,256]{2,1,0:T(8,128)(2,1)} collective-permute-done((bf16[129,8,256]{2,1,0:T(8,128)(2,1)}, bf16[129,8,256]{2,1,0:T(8,128)(2,1)}, u32[]{:S(2)}, u32[]{:S(2)}) %collective-permute-start.1) | collective-permute-done | bytes 528416 | tf_op jit(solution)/shard_map/ppermute | solution.py:332
  37.9 0.0 collective-permute-done.down
  37.9 0.0 copy-done.1
  37.9 0.0 copy-done.4
  37.9 2.8 %shard_map.84 = (bf16[8,16,8,256]{3,2,1,0:T(8,128)(2,1)S(1)}, bf16[2,16,8,256]{3,2,1,0:T(8,128)(2,1)S(1)}, bf16[2,16,8,256]{3,2,1,0:T(8,128)(2,1)S(1)}, bf16[2,1...) custom-call(s32[2]{0:T(128)S(1)} %pad_add_fusion.ids, bf16[129,8,256]{2,1,0:T(8,128)(2,1)} %collective-permute-done.down, ...), custom_call_target="tpu_custom_call" | custom-call | flops 805306368 | bytes 3145728 | tf_op jit(solution)/shard_map/pallas_call | solution.py:156
  40.7 1.4 %collective-permute-start.4 = (bf16[2,16,8,256]{3,2,1,0:T(8,128)(2,1)S(1)}, bf16[2,16,8,256]{3,2,1,0:T(8,128)(2,1)S(1)}, u32[]{:S(2)}, u32[]{:S(2)}) collective-permute-start(bf16[2,16,8,256]{3,2,1,0:T(8,128)(2,1)S(1)} %get-tuple-element.30), channel_id=1, source_target_pairs={{0,2},{1,3},{2,4},{3,5},{4,6},{5,7},{6,0},{7,1},{8,10},{9,11},{10,... | collective-permute-start | bytes 393224 | tf_op jit(solution)/shard_map/ppermute | solution.py:296
  42.1 2.6 %collective-permute-start.5 = (bf16[2,16,8,256]{3,2,1,0:T(8,128)(2,1)S(1)}, bf16[2,16,8,256]{3,2,1,0:T(8,128)(2,1)S(1)}, u32[]{:S(2)}, u32[]{:S(2)}) collective-permute-start(bf16[2,16,8,256]{3,2,1,0:T(8,128)(2,1)S(1)} %get-tuple-element.31), channel_id=1, source_target_pairs={{0,4},{1,5},{2,6},{3,7},{4,0},{5,1},{6,2},{7,3},{8,12},{9,13},{10,... | collective-permute-start | bytes 393224 | tf_op jit(solution)/shard_map/ppermute | solution.py:296
  44.7 0.0 copy-start.6
  44.7 0.0 copy-start.7
  44.7 1.1 %collective-permute-start.6 = (bf16[2,16,8,256]{3,2,1,0:T(8,128)(2,1)S(1)}, bf16[2,16,8,256]{3,2,1,0:T(8,128)(2,1)S(1)}, u32[]{:S(2)}, u32[]{:S(2)}) collective-permute-start(bf16[2,16,8,256]{3,2,1,0:T(8,128)(2,1)S(1)} %get-tuple-element.32), channel_id=1, source_target_pairs={{0,6},{1,7},{2,0},{3,1},{4,2},{5,3},{6,4},{7,5},{8,14},{9,15},{10,... | collective-permute-start | bytes 393224 | tf_op jit(solution)/shard_map/ppermute | solution.py:296
  45.8 3.5 %collective-permute-done.3.up = bf16[129,8,256]{2,1,0:T(8,128)(2,1)} collective-permute-done((bf16[129,8,256]{2,1,0:T(8,128)(2,1)}, bf16[129,8,256]{2,1,0:T(8,128)(2,1)}, u32[]{:S(2)}, u32[]{:S(2)}) %collective-permute-start.3) | collective-permute-done | bytes 528416 | tf_op jit(solution)/shard_map/ppermute | solution.py:332
  49.2 0.0 collective-permute-done.2.down
  49.2 2.7 %shard_map.85 = (bf16[8,16,8,256]{3,2,1,0:T(8,128)(2,1)S(1)}, bf16[2,16,8,256]{3,2,1,0:T(8,128)(2,1)S(1)}, bf16[2,16,8,256]{3,2,1,0:T(8,128)(2,1)S(1)}, bf16[2,1...) custom-call(s32[2]{0:T(128)S(1)} %pad_add_fusion.ids, bf16[129,8,256]{2,1,0:T(8,128)(2,1)} %collective-permute-done.2.down, ...), custom_call_target="tpu_custom_call" | custom-call | flops 805306368 | bytes 3145728 | tf_op jit(solution)/shard_map/pallas_call | solution.py:156
  52.0 0.0 collective-permute-done.4.refs_1_
  52.0 0.0 collective-permute-done.5.refs_2_
  52.0 0.0 collective-permute-done.6.refs_3_
  52.1 1.3 %collective-permute-start.7 = (bf16[4,16,8,256]{3,2,1,0:T(8,128)(2,1)S(1)}, bf16[4,16,8,256]{3,2,1,0:T(8,128)(2,1)S(1)}, u32[]{:S(2)}, u32[]{:S(2)}) collective-permute-start(bf16[4,16,8,256]{3,2,1,0:T(8,128)(2,1)S(1)} %shard_map.86), channel_id=1, source_target_pairs={{0,1},{1,0},{2,3},{3,2},{4,5},{5,4},{6,7},{7,6},{8,9},{9,8},{10,11... | collective-permute-start | bytes 786440 | tf_op jit(solution)/shard_map/ppermute | solution.py:315
  53.4 1.3 %collective-permute-start.11 = (bf16[2,16,8,256]{3,2,1,0:T(8,128)(2,1)S(1)}, bf16[2,16,8,256]{3,2,1,0:T(8,128)(2,1)S(1)}, u32[]{:S(2)}, u32[]{:S(2)}) collective-permute-start(bf16[2,16,8,256]{3,2,1,0:T(8,128)(2,1)S(1)} %get-tuple-element.38), channel_id=1, source_target_pairs={{0,2},{1,3},{2,4},{3,5},{4,6},{5,7},{6,0},{7,1},{8,10},{9,11},{10,... | collective-permute-start | bytes 393224 | tf_op jit(solution)/shard_map/ppermute | solution.py:296
  54.7 2.6 %collective-permute-start.12 = (bf16[2,16,8,256]{3,2,1,0:T(8,128)(2,1)S(1)}, bf16[2,16,8,256]{3,2,1,0:T(8,128)(2,1)S(1)}, u32[]{:S(2)}, u32[]{:S(2)}) collective-permute-start(bf16[2,16,8,256]{3,2,1,0:T(8,128)(2,1)S(1)} %get-tuple-element.39), channel_id=1, source_target_pairs={{0,4},{1,5},{2,6},{3,7},{4,0},{5,1},{6,2},{7,3},{8,12},{9,13},{10,... | collective-permute-start | bytes 393224 | tf_op jit(solution)/shard_map/ppermute | solution.py:296
  57.3 1.1 %collective-permute-start.13 = (bf16[2,16,8,256]{3,2,1,0:T(8,128)(2,1)S(1)}, bf16[2,16,8,256]{3,2,1,0:T(8,128)(2,1)S(1)}, u32[]{:S(2)}, u32[]{:S(2)}) collective-permute-start(bf16[2,16,8,256]{3,2,1,0:T(8,128)(2,1)S(1)} %get-tuple-element.40), channel_id=1, source_target_pairs={{0,6},{1,7},{2,0},{3,1},{4,2},{5,3},{6,4},{7,5},{8,14},{9,15},{10,... | collective-permute-start | bytes 393224 | tf_op jit(solution)/shard_map/ppermute | solution.py:296
  58.4 0.0 collective-permute-done.7.refs_4_
  58.4 0.0 copy-done.5
  58.4 0.0 copy-done.6
  58.4 0.0 copy-done.7
  58.4 3.0 %shard_map.87 = (bf16[2,16,8,256]{3,2,1,0:T(8,128)(2,1)S(1)}, bf16[2,16,8,256]{3,2,1,0:T(8,128)(2,1)S(1)}, bf16[2,16,8,256]{3,2,1,0:T(8,128)(2,1)S(1)}, bf16[2,16,8,256]{3,2,1,0:T(8,128)(2,1)S(1)}) custom-call(bf16[256,256]{1,0:T(8,128)(2,1)S(1)} %copy-done.5, bf16[256,256]{1,0:T(8,128)(2,1)S(1)} %copy-done.6, bf16[256,256]{1,0:T(8,128)(2,1)S(1)} %copy-done.7, ...), custom_call_target="tpu_custom_call" | custom-call | flops 1342177280 | bytes 1441792 | tf_op jit(solution)/shard_map/pallas_call | solution.py:221
  61.3 0.0 collective-permute-done.11.refs_1_
  61.4 2.3 %collective-permute-done.12.refs_2_ = bf16[2,16,8,256]{3,2,1,0:T(8,128)(2,1)S(1)} collective-permute-done((bf16[2,16,8,256]{3,2,1,0:T(8,128)(2,1)S(1)}, bf16[2,16,8,256]{3,2,1,0:T(8,128)(2,1)S(1)}, u32[]{:S(2)}, u32[]{:S(2)}) %collective-permute-start.12) | collective-permute-done | bytes 131104 | tf_op jit(solution)/shard_map/ppermute | solution.py:296
  63.7 0.0 collective-permute-done.13.refs_3_
  63.7 1.0 %collective-permute-start.14 = (bf16[4,16,8,256]{3,2,1,0:T(8,128)(2,1)S(1)}, bf16[4,16,8,256]{3,2,1,0:T(8,128)(2,1)S(1)}, u32[]{:S(2)}, u32[]{:S(2)}) collective-permute-start(bf16[4,16,8,256]{3,2,1,0:T(8,128)(2,1)S(1)} %shard_map.88), channel_id=1, source_target_pairs={{0,1},{1,0},{2,3},{3,2},{4,5},{5,4},{6,7},{7,6},{8,9},{9,8},{10,11... | collective-permute-start | bytes 786440 | tf_op jit(solution)/shard_map/ppermute | solution.py:315
  64.7 1.8 %collective-permute-start.8 = (bf16[2,16,8,256]{3,2,1,0:T(8,128)(2,1)S(1)}, bf16[2,16,8,256]{3,2,1,0:T(8,128)(2,1)S(1)}, u32[]{:S(2)}, u32[]{:S(2)}) collective-permute-start(bf16[2,16,8,256]{3,2,1,0:T(8,128)(2,1)S(1)} %get-tuple-element.34), channel_id=1, source_target_pairs={{0,6},{1,7},{2,0},{3,1},{4,2},{5,3},{6,4},{7,5},{8,14},{9,15},{10,... | collective-permute-start | bytes 393224 | tf_op jit(solution)/shard_map/ppermute | solution.py:296
  66.4 0.9 collective-permute-start.9
  67.3 0.0 copy-start.3
  67.3 0.5 collective-permute-start.10
  67.8 0.0 collective-permute-done.14.refs_4_
  67.8 3.0 %shard_map.89 = (bf16[2,16,8,256]{3,2,1,0:T(8,128)(2,1)S(1)}, bf16[2,16,8,256]{3,2,1,0:T(8,128)(2,1)S(1)}, bf16[2,16,8,256]{3,2,1,0:T(8,128)(2,1)S(1)}, bf16[2,16,8,256]{3,2,1,0:T(8,128)(2,1)S(1)}) custom-call(bf16[256,256]{1,0:T(8,128)(2,1)S(1)} %copy-done.5, bf16[256,256]{1,0:T(8,128)(2,1)S(1)} %copy-done.6, bf16[256,256]{1,0:T(8,128)(2,1)S(1)} %copy-done.7, ...), custom_call_target="tpu_custom_call" | custom-call | flops 1342177280 | bytes 1441792 | tf_op jit(solution)/shard_map/pallas_call | solution.py:221
  70.8 2.2 %collective-permute-start.15 = (bf16[2,16,8,256]{3,2,1,0:T(8,128)(2,1)S(1)}, bf16[2,16,8,256]{3,2,1,0:T(8,128)(2,1)S(1)}, u32[]{:S(2)}, u32[]{:S(2)}) collective-permute-start(bf16[2,16,8,256]{3,2,1,0:T(8,128)(2,1)S(1)} %get-tuple-element.42), channel_id=1, source_target_pairs={{0,6},{1,7},{2,0},{3,1},{4,2},{5,3},{6,4},{7,5},{8,14},{9,15},{10,... | collective-permute-start | bytes 393224 | tf_op jit(solution)/shard_map/ppermute | solution.py:296
  73.0 0.9 %collective-permute-start.16 = (bf16[2,16,8,256]{3,2,1,0:T(8,128)(2,1)S(1)}, bf16[2,16,8,256]{3,2,1,0:T(8,128)(2,1)S(1)}, u32[]{:S(2)}, u32[]{:S(2)}) collective-permute-start(bf16[2,16,8,256]{3,2,1,0:T(8,128)(2,1)S(1)} %get-tuple-element.43), channel_id=1, source_target_pairs={{0,4},{1,5},{2,6},{3,7},{4,0},{5,1},{6,2},{7,3},{8,12},{9,13},{10,... | collective-permute-start | bytes 393224 | tf_op jit(solution)/shard_map/ppermute | solution.py:296
  73.9 0.0 collective-permute-done.8.refs_1_.refs_3_
  73.9 0.0 collective-permute-start.17
  73.9 0.0 collective-permute-done.9.refs_2_.refs_4_
  73.9 2.2 %collective-permute-done.10.refs_3_.refs_5_ = bf16[2,16,8,256]{3,2,1,0:T(8,128)(2,1)S(1)} collective-permute-done((bf16[2,16,8,256]{3,2,1,0:T(8,128)(2,1)S(1)}, bf16[2,16,8,256]{3,2,1,0:T(8,128)(2,1)S(1)}, u32[]{:S(2)}, u32[]{:S(2)}) %collective-permute-start.10) | collective-permute-done | bytes 131104 | tf_op jit(solution)/shard_map/ppermute | solution.py:296
  76.2 0.2 collective-permute-done.15.refs_5_.refs_7_
  76.3 2.1 %collective-permute-done.16.refs_6_.refs_8_ = bf16[2,16,8,256]{3,2,1,0:T(8,128)(2,1)S(1)} collective-permute-done((bf16[2,16,8,256]{3,2,1,0:T(8,128)(2,1)S(1)}, bf16[2,16,8,256]{3,2,1,0:T(8,128)(2,1)S(1)}, u32[]{:S(2)}, u32[]{:S(2)}) %collective-permute-start.16) | collective-permute-done | bytes 131104 | tf_op jit(solution)/shard_map/ppermute | solution.py:296
  78.4 3.6 %collective-permute-done.17.refs_7_.refs_9_ = bf16[2,16,8,256]{3,2,1,0:T(8,128)(2,1)S(1)} collective-permute-done((bf16[2,16,8,256]{3,2,1,0:T(8,128)(2,1)S(1)}, bf16[2,16,8,256]{3,2,1,0:T(8,128)(2,1)S(1)}, u32[]{:S(2)}, u32[]{:S(2)}) %collective-permute-start.17) | collective-permute-done | bytes 131104 | tf_op jit(solution)/shard_map/ppermute | solution.py:296
  82.1 1.3 %collective-permute-start.18 = (bf16[4,32,8,256]{3,2,1,0:T(8,128)(2,1)S(1)}, bf16[4,32,8,256]{3,2,1,0:T(8,128)(2,1)S(1)}, u32[]{:S(2)}, u32[]{:S(2)}) collective-permute-start(bf16[4,32,8,256]{3,2,1,0:T(8,128)(2,1)S(1)} %shard_map.90), channel_id=1, source_target_pairs={{0,1},{1,0},{2,3},{3,2},{4,5},{5,4},{6,7},{7,6},{8,9},{9,8},{10,11... | collective-permute-start | bytes 1572872 | tf_op jit(solution)/shard_map/ppermute | solution.py:315
  83.4 0.0 copy-done.3
  83.4 1.7 %shard_map.91.refs_3_ = bf16[256,8,256]{2,1,0:T(8,128)(2,1)} custom-call(s32[2]{0:T(128)S(1)} %pad_add_fusion.ids, bf16[256,256]{1,0:T(8,128)(2,1)S(1)} %copy-done.3, bf16[8,16,8,256]{3,2,1,0:T(8,128)(2,1)S(1)} %get-tuple-element.26.refs_0_, bf16[8,16,8,256]{3,2,1,0:T(8,128)(2,1)S(1)} %get-tuple-element.28.refs_4_.refs_1_, ...), custom_call_target="tpu_custom_call" | custom-call | flops 134217728 | bytes 1572864 | tf_op jit(solution)/shard_map/pallas_call | solution.py:267
  85.1 0.0 collective-permute-done.18.refs_2_
  85.1 1.7 %shard_map.92 = bf16[256,8,256]{2,1,0:T(8,128)(2,1)} custom-call(s32[2]{0:T(128)S(1)} %pad_add_fusion.ids, bf16[256,256]{1,0:T(8,128)(2,1)S(1)} %copy-done.3, bf16[8,16,8,256]{3,2,1,0:T(8,128)(2,1)S(1)} %get-tuple-element.26.refs_0_, bf16[8,16,8,256]{3,2,1,0:T(8,128)(2,1)S(1)} %get-tuple-element.28.refs_4_.refs_1_, ...), custom_call_target="tpu_custom_call", output_to_operand_aliasing={{}: (5, {})} | custom-call | flops 134217728 | bytes 1572864 | tf_op jit(solution)/shard_map/pallas_call | solution.py:267
  (4 shorter events, 0.1 us)
Async XLA Ops:
  0.0 37.9 %copy-start.1 = (bf16[3,3,256,256]{3,2,1,0:T(8,128)(2,1)S(1)}, bf16[3,3,256,256]{3,2,1,0:T(8,128)(2,1)}, u32[]{:S(2)}) copy-start(bf16[3,3,256,256]{3,2,1,0:T(8,128)(2,1)} %param.9) | copy-start | bytes 3538948
  0.0 37.9 %copy-start.4 = (f32[256]{0:T(256)S(1)}, f32[256]{0:T(256)}, u32[]{:S(2)}) copy-start(f32[256]{0:T(256)} %param.11) | copy-start | bytes 3076
  17.2 20.7 %collective-permute-start.1 = (bf16[129,8,256]{2,1,0:T(8,128)(2,1)}, bf16[129,8,256]{2,1,0:T(8,128)(2,1)}, u32[]{:S(2)}, u32[]{:S(2)}) collective-permute-start(bf16[129,8,256]{2,1,0:T(8,128)(2,1)} %shard_map.82), channel_id=1, source_target_pairs={{0,8},{8,16},{16,24},{24,32},{32,40},{40,48},{48,56},{56,64},{64,7... | collective-permute-start | bytes 1585160 | tf_op jit(solution)/shard_map/ppermute | solution.py:332
  19.7 18.2 %collective-permute-start = (bf16[129,8,256]{2,1,0:T(8,128)(2,1)}, bf16[129,8,256]{2,1,0:T(8,128)(2,1)}, u32[]{:S(2)}, u32[]{:S(2)}) collective-permute-start(bf16[129,8,256]{2,1,0:T(8,128)(2,1)} %shard_map.82), channel_id=1, source_target_pairs={{0,248},{8,0},{16,8},{24,16},{32,24},{40,32},{48,40},{56,48},{64,5... | collective-permute-start | bytes 1585160 | tf_op jit(solution)/shard_map/ppermute | solution.py:332
  26.0 1.3 %copy-start = (bf16[3,3,256,256]{3,2,1,0:T(8,128)(2,1)S(1)}, bf16[3,3,256,256]{3,2,1,0:T(8,128)(2,1)}, u32[]{:S(2)}) copy-start(bf16[3,3,256,256]{3,2,1,0:T(8,128)(2,1)} %param.9) | copy-start | bytes 3538948
  27.2 1.2 %copy-start.2 = (bf16[1,256,8,256]{3,2,1,0:T(8,128)(2,1)S(1)}, bf16[1,256,8,256]{3,2,1,0:T(8,128)(2,1)}, u32[]{:S(2)}) copy-start(bf16[1,256,8,256]{3,2,1,0:T(8,128)(2,1)} %param.8) | copy-start | bytes 3145732
  28.5 0.7 copy-start.8
  30.9 18.4 %collective-permute-start.3 = (bf16[129,8,256]{2,1,0:T(8,128)(2,1)}, bf16[129,8,256]{2,1,0:T(8,128)(2,1)}, u32[]{:S(2)}, u32[]{:S(2)}) collective-permute-start(bf16[129,8,256]{2,1,0:T(8,128)(2,1)} %get-tuple-element.27), channel_id=1, source_target_pairs={{0,8},{8,16},{16,24},{24,32},{32,40},{40,48},{48,56},{56,64},{64,7... | collective-permute-start | bytes 1585160 | tf_op jit(solution)/shard_map/ppermute | solution.py:332
  30.9 18.4 %collective-permute-start.2 = (bf16[129,8,256]{2,1,0:T(8,128)(2,1)}, bf16[129,8,256]{2,1,0:T(8,128)(2,1)}, u32[]{:S(2)}, u32[]{:S(2)}) collective-permute-start(bf16[129,8,256]{2,1,0:T(8,128)(2,1)} %get-tuple-element.27), channel_id=1, source_target_pairs={{0,248},{8,0},{16,8},{24,16},{32,24},{40,32},{48,40},{56,48},{64,5... | collective-permute-start | bytes 1585160 | tf_op jit(solution)/shard_map/ppermute | solution.py:332
  40.7 11.3 %collective-permute-start.4 = (bf16[2,16,8,256]{3,2,1,0:T(8,128)(2,1)S(1)}, bf16[2,16,8,256]{3,2,1,0:T(8,128)(2,1)S(1)}, u32[]{:S(2)}, u32[]{:S(2)}) collective-permute-start(bf16[2,16,8,256]{3,2,1,0:T(8,128)(2,1)S(1)} %get-tuple-element.30), channel_id=1, source_target_pairs={{0,2},{1,3},{2,4},{3,5},{4,6},{5,7},{6,0},{7,1},{8,10},{9,11},{10,... | collective-permute-start | bytes 393224 | tf_op jit(solution)/shard_map/ppermute | solution.py:296
  42.1 9.9 %collective-permute-start.5 = (bf16[2,16,8,256]{3,2,1,0:T(8,128)(2,1)S(1)}, bf16[2,16,8,256]{3,2,1,0:T(8,128)(2,1)S(1)}, u32[]{:S(2)}, u32[]{:S(2)}) collective-permute-start(bf16[2,16,8,256]{3,2,1,0:T(8,128)(2,1)S(1)} %get-tuple-element.31), channel_id=1, source_target_pairs={{0,4},{1,5},{2,6},{3,7},{4,0},{5,1},{6,2},{7,3},{8,12},{9,13},{10,... | collective-permute-start | bytes 393224 | tf_op jit(solution)/shard_map/ppermute | solution.py:296
  44.7 13.7 %copy-start.5 = (bf16[256,256]{1,0:T(8,128)(2,1)S(1)}, bf16[256,256]{1,0:T(8,128)(2,1)}, u32[]{:S(2)}) copy-start(bf16[256,256]{1,0:T(8,128)(2,1)} %wq_ref.3) | copy-start | bytes 393220
  44.7 13.7 %copy-start.6 = (bf16[256,256]{1,0:T(8,128)(2,1)S(1)}, bf16[256,256]{1,0:T(8,128)(2,1)}, u32[]{:S(2)}) copy-start(bf16[256,256]{1,0:T(8,128)(2,1)} %wk_ref.3) | copy-start | bytes 393220
  44.7 13.7 %copy-start.7 = (bf16[256,256]{1,0:T(8,128)(2,1)S(1)}, bf16[256,256]{1,0:T(8,128)(2,1)}, u32[]{:S(2)}) copy-start(bf16[256,256]{1,0:T(8,128)(2,1)} %wv_ref.3) | copy-start | bytes 393220
  44.7 7.3 %collective-permute-start.6 = (bf16[2,16,8,256]{3,2,1,0:T(8,128)(2,1)S(1)}, bf16[2,16,8,256]{3,2,1,0:T(8,128)(2,1)S(1)}, u32[]{:S(2)}, u32[]{:S(2)}) collective-permute-start(bf16[2,16,8,256]{3,2,1,0:T(8,128)(2,1)S(1)} %get-tuple-element.32), channel_id=1, source_target_pairs={{0,6},{1,7},{2,0},{3,1},{4,2},{5,3},{6,4},{7,5},{8,14},{9,15},{10,... | collective-permute-start | bytes 393224 | tf_op jit(solution)/shard_map/ppermute | solution.py:296
  52.1 6.3 %collective-permute-start.7 = (bf16[4,16,8,256]{3,2,1,0:T(8,128)(2,1)S(1)}, bf16[4,16,8,256]{3,2,1,0:T(8,128)(2,1)S(1)}, u32[]{:S(2)}, u32[]{:S(2)}) collective-permute-start(bf16[4,16,8,256]{3,2,1,0:T(8,128)(2,1)S(1)} %shard_map.86), channel_id=1, source_target_pairs={{0,1},{1,0},{2,3},{3,2},{4,5},{5,4},{6,7},{7,6},{8,9},{9,8},{10,11... | collective-permute-start | bytes 786440 | tf_op jit(solution)/shard_map/ppermute | solution.py:315
  53.4 8.0 %collective-permute-start.11 = (bf16[2,16,8,256]{3,2,1,0:T(8,128)(2,1)S(1)}, bf16[2,16,8,256]{3,2,1,0:T(8,128)(2,1)S(1)}, u32[]{:S(2)}, u32[]{:S(2)}) collective-permute-start(bf16[2,16,8,256]{3,2,1,0:T(8,128)(2,1)S(1)} %get-tuple-element.38), channel_id=1, source_target_pairs={{0,2},{1,3},{2,4},{3,5},{4,6},{5,7},{6,0},{7,1},{8,10},{9,11},{10,... | collective-permute-start | bytes 393224 | tf_op jit(solution)/shard_map/ppermute | solution.py:296
  54.7 9.0 %collective-permute-start.12 = (bf16[2,16,8,256]{3,2,1,0:T(8,128)(2,1)S(1)}, bf16[2,16,8,256]{3,2,1,0:T(8,128)(2,1)S(1)}, u32[]{:S(2)}, u32[]{:S(2)}) collective-permute-start(bf16[2,16,8,256]{3,2,1,0:T(8,128)(2,1)S(1)} %get-tuple-element.39), channel_id=1, source_target_pairs={{0,4},{1,5},{2,6},{3,7},{4,0},{5,1},{6,2},{7,3},{8,12},{9,13},{10,... | collective-permute-start | bytes 393224 | tf_op jit(solution)/shard_map/ppermute | solution.py:296
  57.3 6.4 %collective-permute-start.13 = (bf16[2,16,8,256]{3,2,1,0:T(8,128)(2,1)S(1)}, bf16[2,16,8,256]{3,2,1,0:T(8,128)(2,1)S(1)}, u32[]{:S(2)}, u32[]{:S(2)}) collective-permute-start(bf16[2,16,8,256]{3,2,1,0:T(8,128)(2,1)S(1)} %get-tuple-element.40), channel_id=1, source_target_pairs={{0,6},{1,7},{2,0},{3,1},{4,2},{5,3},{6,4},{7,5},{8,14},{9,15},{10,... | collective-permute-start | bytes 393224 | tf_op jit(solution)/shard_map/ppermute | solution.py:296
  63.7 4.1 %collective-permute-start.14 = (bf16[4,16,8,256]{3,2,1,0:T(8,128)(2,1)S(1)}, bf16[4,16,8,256]{3,2,1,0:T(8,128)(2,1)S(1)}, u32[]{:S(2)}, u32[]{:S(2)}) collective-permute-start(bf16[4,16,8,256]{3,2,1,0:T(8,128)(2,1)S(1)} %shard_map.88), channel_id=1, source_target_pairs={{0,1},{1,0},{2,3},{3,2},{4,5},{5,4},{6,7},{7,6},{8,9},{9,8},{10,11... | collective-permute-start | bytes 786440 | tf_op jit(solution)/shard_map/ppermute | solution.py:315
  64.7 9.3 %collective-permute-start.8 = (bf16[2,16,8,256]{3,2,1,0:T(8,128)(2,1)S(1)}, bf16[2,16,8,256]{3,2,1,0:T(8,128)(2,1)S(1)}, u32[]{:S(2)}, u32[]{:S(2)}) collective-permute-start(bf16[2,16,8,256]{3,2,1,0:T(8,128)(2,1)S(1)} %get-tuple-element.34), channel_id=1, source_target_pairs={{0,6},{1,7},{2,0},{3,1},{4,2},{5,3},{6,4},{7,5},{8,14},{9,15},{10,... | collective-permute-start | bytes 393224 | tf_op jit(solution)/shard_map/ppermute | solution.py:296
  66.4 7.5 %collective-permute-start.9 = (bf16[2,16,8,256]{3,2,1,0:T(8,128)(2,1)S(1)}, bf16[2,16,8,256]{3,2,1,0:T(8,128)(2,1)S(1)}, u32[]{:S(2)}, u32[]{:S(2)}) collective-permute-start(bf16[2,16,8,256]{3,2,1,0:T(8,128)(2,1)S(1)} %get-tuple-element.35), channel_id=1, source_target_pairs={{0,4},{1,5},{2,6},{3,7},{4,0},{5,1},{6,2},{7,3},{8,12},{9,13},{10,... | collective-permute-start | bytes 393224 | tf_op jit(solution)/shard_map/ppermute | solution.py:296
  67.3 16.1 %copy-start.3 = (bf16[256,256]{1,0:T(8,128)(2,1)S(1)}, bf16[256,256]{1,0:T(8,128)(2,1)}, u32[]{:S(2)}) copy-start(bf16[256,256]{1,0:T(8,128)(2,1)} %w_ref.3) | copy-start | bytes 393220
  67.3 8.9 %collective-permute-start.10 = (bf16[2,16,8,256]{3,2,1,0:T(8,128)(2,1)S(1)}, bf16[2,16,8,256]{3,2,1,0:T(8,128)(2,1)S(1)}, u32[]{:S(2)}, u32[]{:S(2)}) collective-permute-start(bf16[2,16,8,256]{3,2,1,0:T(8,128)(2,1)S(1)} %get-tuple-element.36), channel_id=1, source_target_pairs={{0,2},{1,3},{2,4},{3,5},{4,6},{5,7},{6,0},{7,1},{8,10},{9,11},{10,... | collective-permute-start | bytes 393224 | tf_op jit(solution)/shard_map/ppermute | solution.py:296
  70.8 5.5 %collective-permute-start.15 = (bf16[2,16,8,256]{3,2,1,0:T(8,128)(2,1)S(1)}, bf16[2,16,8,256]{3,2,1,0:T(8,128)(2,1)S(1)}, u32[]{:S(2)}, u32[]{:S(2)}) collective-permute-start(bf16[2,16,8,256]{3,2,1,0:T(8,128)(2,1)S(1)} %get-tuple-element.42), channel_id=1, source_target_pairs={{0,6},{1,7},{2,0},{3,1},{4,2},{5,3},{6,4},{7,5},{8,14},{9,15},{10,... | collective-permute-start | bytes 393224 | tf_op jit(solution)/shard_map/ppermute | solution.py:296
  73.0 5.4 %collective-permute-start.16 = (bf16[2,16,8,256]{3,2,1,0:T(8,128)(2,1)S(1)}, bf16[2,16,8,256]{3,2,1,0:T(8,128)(2,1)S(1)}, u32[]{:S(2)}, u32[]{:S(2)}) collective-permute-start(bf16[2,16,8,256]{3,2,1,0:T(8,128)(2,1)S(1)} %get-tuple-element.43), channel_id=1, source_target_pairs={{0,4},{1,5},{2,6},{3,7},{4,0},{5,1},{6,2},{7,3},{8,12},{9,13},{10,... | collective-permute-start | bytes 393224 | tf_op jit(solution)/shard_map/ppermute | solution.py:296
  73.9 8.1 %collective-permute-start.17 = (bf16[2,16,8,256]{3,2,1,0:T(8,128)(2,1)S(1)}, bf16[2,16,8,256]{3,2,1,0:T(8,128)(2,1)S(1)}, u32[]{:S(2)}, u32[]{:S(2)}) collective-permute-start(bf16[2,16,8,256]{3,2,1,0:T(8,128)(2,1)S(1)} %get-tuple-element.44), channel_id=1, source_target_pairs={{0,2},{1,3},{2,4},{3,5},{4,6},{5,7},{6,0},{7,1},{8,10},{9,11},{10,... | collective-permute-start | bytes 393224 | tf_op jit(solution)/shard_map/ppermute | solution.py:296
  82.1 3.0 %collective-permute-start.18 = (bf16[4,32,8,256]{3,2,1,0:T(8,128)(2,1)S(1)}, bf16[4,32,8,256]{3,2,1,0:T(8,128)(2,1)S(1)}, u32[]{:S(2)}, u32[]{:S(2)}) collective-permute-start(bf16[4,32,8,256]{3,2,1,0:T(8,128)(2,1)S(1)} %shard_map.90), channel_id=1, source_target_pairs={{0,1},{1,0},{2,3},{3,2},{4,5},{5,4},{6,7},{7,6},{8,9},{9,8},{10,11... | collective-permute-start | bytes 1572872 | tf_op jit(solution)/shard_map/ppermute | solution.py:315

commit v6 on v5

--- a/solution.py
+++ b/solution.py
@@ -59,25 +59,30 @@
     return jnp.concatenate(out, axis=1)
 
 
-def head_kernel(src, dst, sems):
-    count, ways = dst.shape[0], sems.shape[0]
+def head_kernel(src, dst, held, in_sems, out_sems):
+    count, ways = dst.shape[0], in_sems.shape[0]
     cuts = [count * i // ways for i in range(ways + 1)]
-    copies = []
+    ins, outs = [], []
     for i, (low, high) in enumerate(zip(cuts, cuts[1:])):
         here = pl.ds(low, high - low)
-        copies.append(pltpu.make_async_copy(src.at[here], dst.at[here], sems.at[i]))
-        copies[-1].start()
-    for copy in copies:
+        ins.append(pltpu.make_async_copy(src.at[here], held.at[here], in_sems.at[i]))
+        outs.append(pltpu.make_async_copy(held.at[here], dst.at[here], out_sems.at[i]))
+        ins[i].start()
+    for i in range(ways):
+        ins[i].wait()
+        outs[i].start()
+    for copy in outs:
         copy.wait()
 
 
 def head(x, count):
+    shape = (count, *x.shape[1:])
     return pl.pallas_call(
         head_kernel,
-        out_shape=pltpu.HBM((count, *x.shape[1:]), x.dtype),
+        out_shape=pltpu.HBM(shape, x.dtype),
         in_specs=[ANY],
         out_specs=ANY,
-        scratch_shapes=[pltpu.SemaphoreType.DMA((8,))],
+        scratch_shapes=[pltpu.VMEM(shape, x.dtype)] + [pltpu.SemaphoreType.DMA((4,))] * 2,
         compiler_params=params(4),
         cost_estimate=cost(0, x.size * 2),
     )(pltpu.with_memory_space_constraint(x, pltpu.HBM))
@@ -233,6 +238,7 @@
     hiddens, refs = refs[: len(starts)], refs[len(starts) :]
     out_hbm, held, sems = refs[-3:]
     _, count, leads, chans = held.shape
+    copies = []
     for i in range(chips):
         if core == 0:
             x = jnp.concatenate([refs[k * chips + i][0] for k in range(len(starts))], axis=0)
@@ -242,8 +248,6 @@
         acc = jnp.dot(x.reshape(count * leads, chans), w_ref[...], preferred_element_type=F32)
         acc = acc + hidden.reshape(count * leads, chans).astype(F32)
         held[i] = acc.astype(BF16).reshape(count, leads, chans)
-    copies = []
-    for i in range(chips):
         low = 0
         for k, (start, ref) in enumerate(zip(starts, hiddens)):
             width = ref.shape[1]

time: 87.2 us -> 71.8 us (0.82)
  Pallas kernels: 33.8 us -> 18.4 us
    pallas_call x1, Pallas kernels: 17.2 us -> 1.91 us  [head(): pl.pallas_call(head_kernel, out_shape=pltpu.HBM(shape, x.dtype), in_specs...]
  transfers between devices with their start and end apart: 19 -> 19, of which waited for: 7 -> 7; matrix products, arithmetic and copies ran while one was open for 0% -> 0% of each run, Pallas kernels for 17% -> 21%
where the time goes in v6:
time: 71.8 us; the launch traced here: 71.5 us
  starting transfers between devices  33.4 us (47%)
  Pallas kernels  18.4 us (26%)
  waiting for transfers between devices  16.1 us (22%)
  local copies, waits for them, and re-layouts  3.19 us (4%)
    ppermute x12, starting transfers between devices, send(): lax.ppermute(pieces[k], 'lead', [(i, (i + 2 * sign * k) % (2 * chips)) fo...  16.4 us
    ppermute x2, starting transfers between devices, shards(): lax.ppermute(piece, 'lat', south)  11 us
    ppermute x12, waiting for transfers between devices, send(): lax.ppermute(pieces[k], 'lead', [(i, (i + 2 * sign * k) % (2 * chips)) fo...  10.5 us
    pallas_call x2, Pallas kernels, attend(): pl.pallas_call(functools.partial(attend_kernel, math.gcd(pixels, 16), chi...  5.91 us
    ppermute x2, waiting for transfers between devices, shards(): lax.ppermute(piece, 'lat', north)  5.66 us
    pallas_call x2, Pallas kernels, conv_norm(): pl.pallas_call(functools.partial(conv_kernel, tile, start - low, start, l...  5.5 us
    ppermute x3, starting transfers between devices, swap(): return lax.ppermute(others, 'lead', [(i, i ^ 1) for i in range(2 * chips)])  3.54 us
    pallas_call x2, Pallas kernels, project_out(): pl.pallas_call(functools.partial(out_kernel, starts, core, chips), out_sh...  3.25 us
  transfers between devices with their start and end apart: 19, of which 7 were waited for; matrix products, arithmetic and copies ran while one was open for 0% of the time, Pallas kernels for 21%

profile of v6, /device:TPU:1, one launch (start us, length us, event | category | flops | bytes accessed | tf_op | source)
XLA Modules:
  0.0 71.5 jit_solution(14372222638120925965)
XLA Ops:
  0.0 0.0 copy-start.1
  0.0 0.0 copy-start.4
  0.0 1.9 %shard_map.82 = bf16[129,8,256]{2,1,0:T(8,128)(2,1)} custom-call(bf16[256,8,256]{2,1,0:T(8,128)(2,1)} %bitcast.10), custom_call_target="tpu_custom_call" | custom-call | bytes 1048576 | tf_op jit(solution)/shard_map/pallas_call | solution.py:80
  1.9 2.5 %collective-permute-start.1 = (bf16[129,8,256]{2,1,0:T(8,128)(2,1)}, bf16[129,8,256]{2,1,0:T(8,128)(2,1)}, u32[]{:S(2)}, u32[]{:S(2)}) collective-permute-start(bf16[129,8,256]{2,1,0:T(8,128)(2,1)} %shard_map.82), channel_id=1, source_target_pairs={{0,8},{8,16},{16,24},{24,32},{32,40},{40,48},{48,56},{56,64},{64,7... | collective-permute-start | bytes 1585160 | tf_op jit(solution)/shard_map/ppermute | solution.py:336
  4.5 6.2 %collective-permute-start = (bf16[129,8,256]{2,1,0:T(8,128)(2,1)}, bf16[129,8,256]{2,1,0:T(8,128)(2,1)}, u32[]{:S(2)}, u32[]{:S(2)}) collective-permute-start(bf16[129,8,256]{2,1,0:T(8,128)(2,1)} %shard_map.82), channel_id=1, source_target_pairs={{0,248},{8,0},{16,8},{24,16},{32,24},{40,32},{48,40},{56,48},{64,5... | collective-permute-start | bytes 1585160 | tf_op jit(solution)/shard_map/ppermute | solution.py:336
  10.7 0.0 copy-start
  10.7 1.3 %copy-done = bf16[3,3,256,256]{3,2,1,0:T(8,128)(2,1)S(1)} copy-done((bf16[3,3,256,256]{3,2,1,0:T(8,128)(2,1)S(1)}, bf16[3,3,256,256]{3,2,1,0:T(8,128)(2,1)}, u32[]{:S(2)}) %copy-start) | copy-done | bytes 1179672
  12.0 0.0 copy-start.2
  12.0 1.2 %copy-done.2 = bf16[1,256,8,256]{3,2,1,0:T(8,128)(2,1)S(1)} copy-done((bf16[1,256,8,256]{3,2,1,0:T(8,128)(2,1)S(1)}, bf16[1,256,8,256]{3,2,1,0:T(8,128)(2,1)}, u32[]{:S(2)}) %copy-start.2) | copy-done | bytes 1048600
  13.2 0.0 copy-start.8
  13.2 0.7 copy-done.8
  13.9 1.7 %shard_map.83 = (f32[2048,256]{1,0:T(8,128)S(1)}, bf16[129,8,256]{2,1,0:T(8,128)(2,1)}) custom-call(bf16[256,8,256]{2,1,0:T(8,128)(2,1)S(1)} %bitcast.11, bf16[9,256,256]{2,1,0:T(8,128)(2,1)S(1)} %bitcast.7, f32[1,256]{1,0:T(1,128)S(1)} %bitcast.14), custom_call_target="tpu_custom_call" | custom-call | flops 805306368 | bytes 3145728 | tf_op jit(solution)/shard_map/pallas_call | solution.py:107
  15.6 0.0 collective-permute-start.3
  15.6 4.8 %collective-permute-start.2 = (bf16[129,8,256]{2,1,0:T(8,128)(2,1)}, bf16[129,8,256]{2,1,0:T(8,128)(2,1)}, u32[]{:S(2)}, u32[]{:S(2)}) collective-permute-start(bf16[129,8,256]{2,1,0:T(8,128)(2,1)} %get-tuple-element.27), channel_id=1, source_target_pairs={{0,248},{8,0},{16,8},{24,16},{32,24},{40,32},{48,40},{56,48},{64,5... | collective-permute-start | bytes 1585160 | tf_op jit(solution)/shard_map/ppermute | solution.py:336
  20.4 0.1 pad_add_fusion.ids
  20.5 2.2 %collective-permute-done.1.up = bf16[129,8,256]{2,1,0:T(8,128)(2,1)} collective-permute-done((bf16[129,8,256]{2,1,0:T(8,128)(2,1)}, bf16[129,8,256]{2,1,0:T(8,128)(2,1)}, u32[]{:S(2)}, u32[]{:S(2)}) %collective-permute-start.1) | collective-permute-done | bytes 528416 | tf_op jit(solution)/shard_map/ppermute | solution.py:336
  22.7 0.0 collective-permute-done.down
  22.7 0.0 copy-done.1
  22.7 0.0 copy-done.4
  22.7 2.8 %shard_map.84 = (bf16[8,16,8,256]{3,2,1,0:T(8,128)(2,1)S(1)}, bf16[2,16,8,256]{3,2,1,0:T(8,128)(2,1)S(1)}, bf16[2,16,8,256]{3,2,1,0:T(8,128)(2,1)S(1)}, bf16[2,1...) custom-call(s32[2]{0:T(128)S(1)} %pad_add_fusion.ids, bf16[129,8,256]{2,1,0:T(8,128)(2,1)} %collective-permute-done.down, ...), custom_call_target="tpu_custom_call" | custom-call | flops 805306368 | bytes 3145728 | tf_op jit(solution)/shard_map/pallas_call | solution.py:161
  25.4 1.4 %collective-permute-start.4 = (bf16[2,16,8,256]{3,2,1,0:T(8,128)(2,1)S(1)}, bf16[2,16,8,256]{3,2,1,0:T(8,128)(2,1)S(1)}, u32[]{:S(2)}, u32[]{:S(2)}) collective-permute-start(bf16[2,16,8,256]{3,2,1,0:T(8,128)(2,1)S(1)} %get-tuple-element.30), channel_id=1, source_target_pairs={{0,2},{1,3},{2,4},{3,5},{4,6},{5,7},{6,0},{7,1},{8,10},{9,11},{10,... | collective-permute-start | bytes 393224 | tf_op jit(solution)/shard_map/ppermute | solution.py:300
  26.8 2.6 %collective-permute-start.5 = (bf16[2,16,8,256]{3,2,1,0:T(8,128)(2,1)S(1)}, bf16[2,16,8,256]{3,2,1,0:T(8,128)(2,1)S(1)}, u32[]{:S(2)}, u32[]{:S(2)}) collective-permute-start(bf16[2,16,8,256]{3,2,1,0:T(8,128)(2,1)S(1)} %get-tuple-element.31), channel_id=1, source_target_pairs={{0,4},{1,5},{2,6},{3,7},{4,0},{5,1},{6,2},{7,3},{8,12},{9,13},{10,... | collective-permute-start | bytes 393224 | tf_op jit(solution)/shard_map/ppermute | solution.py:300
  29.4 0.0 copy-start.5
  29.4 0.0 copy-start.6
  29.4 0.0 copy-start.7
  29.4 1.1 %collective-permute-start.6 = (bf16[2,16,8,256]{3,2,1,0:T(8,128)(2,1)S(1)}, bf16[2,16,8,256]{3,2,1,0:T(8,128)(2,1)S(1)}, u32[]{:S(2)}, u32[]{:S(2)}) collective-permute-start(bf16[2,16,8,256]{3,2,1,0:T(8,128)(2,1)S(1)} %get-tuple-element.32), channel_id=1, source_target_pairs={{0,6},{1,7},{2,0},{3,1},{4,2},{5,3},{6,4},{7,5},{8,14},{9,15},{10,... | collective-permute-start | bytes 393224 | tf_op jit(solution)/shard_map/ppermute | solution.py:300
  30.5 3.5 %collective-permute-done.3.up = bf16[129,8,256]{2,1,0:T(8,128)(2,1)} collective-permute-done((bf16[129,8,256]{2,1,0:T(8,128)(2,1)}, bf16[129,8,256]{2,1,0:T(8,128)(2,1)}, u32[]{:S(2)}, u32[]{:S(2)}) %collective-permute-start.3) | collective-permute-done | bytes 528416 | tf_op jit(solution)/shard_map/ppermute | solution.py:336
  34.0 0.0 collective-permute-done.2.down
  34.0 2.7 %shard_map.85 = (bf16[8,16,8,256]{3,2,1,0:T(8,128)(2,1)S(1)}, bf16[2,16,8,256]{3,2,1,0:T(8,128)(2,1)S(1)}, bf16[2,16,8,256]{3,2,1,0:T(8,128)(2,1)S(1)}, bf16[2,1...) custom-call(s32[2]{0:T(128)S(1)} %pad_add_fusion.ids, bf16[129,8,256]{2,1,0:T(8,128)(2,1)} %collective-permute-done.2.down, ...), custom_call_target="tpu_custom_call" | custom-call | flops 805306368 | bytes 3145728 | tf_op jit(solution)/shard_map/pallas_call | solution.py:161
  36.7 0.0 collective-permute-done.4.refs_1_
  36.7 0.0 collective-permute-done.5.refs_2_
  36.8 0.0 collective-permute-done.6.refs_3_
  36.8 1.3 %collective-permute-start.7 = (bf16[4,16,8,256]{3,2,1,0:T(8,128)(2,1)S(1)}, bf16[4,16,8,256]{3,2,1,0:T(8,128)(2,1)S(1)}, u32[]{:S(2)}, u32[]{:S(2)}) collective-permute-start(bf16[4,16,8,256]{3,2,1,0:T(8,128)(2,1)S(1)} %shard_map.86), channel_id=1, source_target_pairs={{0,1},{1,0},{2,3},{3,2},{4,5},{5,4},{6,7},{7,6},{8,9},{9,8},{10,11... | collective-permute-start | bytes 786440 | tf_op jit(solution)/shard_map/ppermute | solution.py:319
  38.1 1.3 %collective-permute-start.11 = (bf16[2,16,8,256]{3,2,1,0:T(8,128)(2,1)S(1)}, bf16[2,16,8,256]{3,2,1,0:T(8,128)(2,1)S(1)}, u32[]{:S(2)}, u32[]{:S(2)}) collective-permute-start(bf16[2,16,8,256]{3,2,1,0:T(8,128)(2,1)S(1)} %get-tuple-element.38), channel_id=1, source_target_pairs={{0,2},{1,3},{2,4},{3,5},{4,6},{5,7},{6,0},{7,1},{8,10},{9,11},{10,... | collective-permute-start | bytes 393224 | tf_op jit(solution)/shard_map/ppermute | solution.py:300
  39.4 2.6 %collective-permute-start.12 = (bf16[2,16,8,256]{3,2,1,0:T(8,128)(2,1)S(1)}, bf16[2,16,8,256]{3,2,1,0:T(8,128)(2,1)S(1)}, u32[]{:S(2)}, u32[]{:S(2)}) collective-permute-start(bf16[2,16,8,256]{3,2,1,0:T(8,128)(2,1)S(1)} %get-tuple-element.39), channel_id=1, source_target_pairs={{0,4},{1,5},{2,6},{3,7},{4,0},{5,1},{6,2},{7,3},{8,12},{9,13},{10,... | collective-permute-start | bytes 393224 | tf_op jit(solution)/shard_map/ppermute | solution.py:300
  42.0 1.1 %collective-permute-start.13 = (bf16[2,16,8,256]{3,2,1,0:T(8,128)(2,1)S(1)}, bf16[2,16,8,256]{3,2,1,0:T(8,128)(2,1)S(1)}, u32[]{:S(2)}, u32[]{:S(2)}) collective-permute-start(bf16[2,16,8,256]{3,2,1,0:T(8,128)(2,1)S(1)} %get-tuple-element.40), channel_id=1, source_target_pairs={{0,6},{1,7},{2,0},{3,1},{4,2},{5,3},{6,4},{7,5},{8,14},{9,15},{10,... | collective-permute-start | bytes 393224 | tf_op jit(solution)/shard_map/ppermute | solution.py:300
  43.1 0.0 collective-permute-done.7.refs_4_
  43.1 0.0 copy-done.5
  43.1 0.0 copy-done.6
  43.1 0.0 copy-done.7
  43.1 3.0 %shard_map.87 = (bf16[2,16,8,256]{3,2,1,0:T(8,128)(2,1)S(1)}, bf16[2,16,8,256]{3,2,1,0:T(8,128)(2,1)S(1)}, bf16[2,16,8,256]{3,2,1,0:T(8,128)(2,1)S(1)}, bf16[2,16,8,256]{3,2,1,0:T(8,128)(2,1)S(1)}) custom-call(bf16[256,256]{1,0:T(8,128)(2,1)S(1)} %copy-done.5, bf16[256,256]{1,0:T(8,128)(2,1)S(1)} %copy-done.6, bf16[256,256]{1,0:T(8,128)(2,1)S(1)} %copy-done.7, ...), custom_call_target="tpu_custom_call" | custom-call | flops 1342177280 | bytes 1441792 | tf_op jit(solution)/shard_map/pallas_call | solution.py:226
  46.1 0.0 collective-permute-done.11.refs_1_
  46.1 2.3 %collective-permute-done.12.refs_2_ = bf16[2,16,8,256]{3,2,1,0:T(8,128)(2,1)S(1)} collective-permute-done((bf16[2,16,8,256]{3,2,1,0:T(8,128)(2,1)S(1)}, bf16[2,16,8,256]{3,2,1,0:T(8,128)(2,1)S(1)}, u32[]{:S(2)}, u32[]{:S(2)}) %collective-permute-start.12) | collective-permute-done | bytes 131104 | tf_op jit(solution)/shard_map/ppermute | solution.py:300
  48.4 0.0 collective-permute-done.13.refs_3_
  48.4 1.0 %collective-permute-start.14 = (bf16[4,16,8,256]{3,2,1,0:T(8,128)(2,1)S(1)}, bf16[4,16,8,256]{3,2,1,0:T(8,128)(2,1)S(1)}, u32[]{:S(2)}, u32[]{:S(2)}) collective-permute-start(bf16[4,16,8,256]{3,2,1,0:T(8,128)(2,1)S(1)} %shard_map.88), channel_id=1, source_target_pairs={{0,1},{1,0},{2,3},{3,2},{4,5},{5,4},{6,7},{7,6},{8,9},{9,8},{10,11... | collective-permute-start | bytes 786440 | tf_op jit(solution)/shard_map/ppermute | solution.py:319
  49.4 1.8 %collective-permute-start.8 = (bf16[2,16,8,256]{3,2,1,0:T(8,128)(2,1)S(1)}, bf16[2,16,8,256]{3,2,1,0:T(8,128)(2,1)S(1)}, u32[]{:S(2)}, u32[]{:S(2)}) collective-permute-start(bf16[2,16,8,256]{3,2,1,0:T(8,128)(2,1)S(1)} %get-tuple-element.34), channel_id=1, source_target_pairs={{0,6},{1,7},{2,0},{3,1},{4,2},{5,3},{6,4},{7,5},{8,14},{9,15},{10,... | collective-permute-start | bytes 393224 | tf_op jit(solution)/shard_map/ppermute | solution.py:300
  51.2 0.9 %collective-permute-start.9 = (bf16[2,16,8,256]{3,2,1,0:T(8,128)(2,1)S(1)}, bf16[2,16,8,256]{3,2,1,0:T(8,128)(2,1)S(1)}, u32[]{:S(2)}, u32[]{:S(2)}) collective-permute-start(bf16[2,16,8,256]{3,2,1,0:T(8,128)(2,1)S(1)} %get-tuple-element.35), channel_id=1, source_target_pairs={{0,4},{1,5},{2,6},{3,7},{4,0},{5,1},{6,2},{7,3},{8,12},{9,13},{10,... | collective-permute-start | bytes 393224 | tf_op jit(solution)/shard_map/ppermute | solution.py:300
  52.1 0.5 collective-permute-start.10
  52.6 0.0 collective-permute-done.14.refs_4_
  52.6 3.0 %shard_map.89 = (bf16[2,16,8,256]{3,2,1,0:T(8,128)(2,1)S(1)}, bf16[2,16,8,256]{3,2,1,0:T(8,128)(2,1)S(1)}, bf16[2,16,8,256]{3,2,1,0:T(8,128)(2,1)S(1)}, bf16[2,16,8,256]{3,2,1,0:T(8,128)(2,1)S(1)}) custom-call(bf16[256,256]{1,0:T(8,128)(2,1)S(1)} %copy-done.5, bf16[256,256]{1,0:T(8,128)(2,1)S(1)} %copy-done.6, bf16[256,256]{1,0:T(8,128)(2,1)S(1)} %copy-done.7, ...), custom_call_target="tpu_custom_call" | custom-call | flops 1342177280 | bytes 1441792 | tf_op jit(solution)/shard_map/pallas_call | solution.py:226
  55.5 2.2 %collective-permute-start.15 = (bf16[2,16,8,256]{3,2,1,0:T(8,128)(2,1)S(1)}, bf16[2,16,8,256]{3,2,1,0:T(8,128)(2,1)S(1)}, u32[]{:S(2)}, u32[]{:S(2)}) collective-permute-start(bf16[2,16,8,256]{3,2,1,0:T(8,128)(2,1)S(1)} %get-tuple-element.42), channel_id=1, source_target_pairs={{0,6},{1,7},{2,0},{3,1},{4,2},{5,3},{6,4},{7,5},{8,14},{9,15},{10,... | collective-permute-start | bytes 393224 | tf_op jit(solution)/shard_map/ppermute | solution.py:300
  57.8 0.9 %collective-permute-start.16 = (bf16[2,16,8,256]{3,2,1,0:T(8,128)(2,1)S(1)}, bf16[2,16,8,256]{3,2,1,0:T(8,128)(2,1)S(1)}, u32[]{:S(2)}, u32[]{:S(2)}) collective-permute-start(bf16[2,16,8,256]{3,2,1,0:T(8,128)(2,1)S(1)} %get-tuple-element.43), channel_id=1, source_target_pairs={{0,4},{1,5},{2,6},{3,7},{4,0},{5,1},{6,2},{7,3},{8,12},{9,13},{10,... | collective-permute-start | bytes 393224 | tf_op jit(solution)/shard_map/ppermute | solution.py:300
  58.7 0.0 collective-permute-done.8.refs_1_.refs_3_
  58.7 0.0 collective-permute-start.17
  58.7 0.0 collective-permute-done.9.refs_2_.refs_4_
  58.7 2.2 %collective-permute-done.10.refs_3_.refs_5_ = bf16[2,16,8,256]{3,2,1,0:T(8,128)(2,1)S(1)} collective-permute-done((bf16[2,16,8,256]{3,2,1,0:T(8,128)(2,1)S(1)}, bf16[2,16,8,256]{3,2,1,0:T(8,128)(2,1)S(1)}, u32[]{:S(2)}, u32[]{:S(2)}) %collective-permute-start.10) | collective-permute-done | bytes 131104 | tf_op jit(solution)/shard_map/ppermute | solution.py:300
  60.9 0.1 collective-permute-done.15.refs_5_.refs_7_
  61.1 2.1 %collective-permute-done.16.refs_6_.refs_8_ = bf16[2,16,8,256]{3,2,1,0:T(8,128)(2,1)S(1)} collective-permute-done((bf16[2,16,8,256]{3,2,1,0:T(8,128)(2,1)S(1)}, bf16[2,16,8,256]{3,2,1,0:T(8,128)(2,1)S(1)}, u32[]{:S(2)}, u32[]{:S(2)}) %collective-permute-start.16) | collective-permute-done | bytes 131104 | tf_op jit(solution)/shard_map/ppermute | solution.py:300
  63.2 3.6 %collective-permute-done.17.refs_7_.refs_9_ = bf16[2,16,8,256]{3,2,1,0:T(8,128)(2,1)S(1)} collective-permute-done((bf16[2,16,8,256]{3,2,1,0:T(8,128)(2,1)S(1)}, bf16[2,16,8,256]{3,2,1,0:T(8,128)(2,1)S(1)}, u32[]{:S(2)}, u32[]{:S(2)}) %collective-permute-start.17) | collective-permute-done | bytes 131104 | tf_op jit(solution)/shard_map/ppermute | solution.py:300
  66.8 1.3 %collective-permute-start.18 = (bf16[4,32,8,256]{3,2,1,0:T(8,128)(2,1)S(1)}, bf16[4,32,8,256]{3,2,1,0:T(8,128)(2,1)S(1)}, u32[]{:S(2)}, u32[]{:S(2)}) collective-permute-start(bf16[4,32,8,256]{3,2,1,0:T(8,128)(2,1)S(1)} %shard_map.90), channel_id=1, source_target_pairs={{0,1},{1,0},{2,3},{3,2},{4,5},{5,4},{6,7},{7,6},{8,9},{9,8},{10,11... | collective-permute-start | bytes 1572872 | tf_op jit(solution)/shard_map/ppermute | solution.py:319
  68.1 0.0 copy-done.3
  68.1 1.6 %shard_map.91.refs_3_ = bf16[256,8,256]{2,1,0:T(8,128)(2,1)} custom-call(s32[2]{0:T(128)S(1)} %pad_add_fusion.ids, bf16[256,256]{1,0:T(8,128)(2,1)S(1)} %copy-done.3, bf16[8,16,8,256]{3,2,1,0:T(8,128)(2,1)S(1)} %get-tuple-element.26.refs_0_, bf16[8,16,8,256]{3,2,1,0:T(8,128)(2,1)S(1)} %get-tuple-element.28.refs_4_.refs_1_, ...), custom_call_target="tpu_custom_call" | custom-call | flops 134217728 | bytes 1572864 | tf_op jit(solution)/shard_map/pallas_call | solution.py:271
  69.7 0.0 collective-permute-done.18.refs_2_
  69.8 1.6 %shard_map.92 = bf16[256,8,256]{2,1,0:T(8,128)(2,1)} custom-call(s32[2]{0:T(128)S(1)} %pad_add_fusion.ids, bf16[256,256]{1,0:T(8,128)(2,1)S(1)} %copy-done.3, bf16[8,16,8,256]{3,2,1,0:T(8,128)(2,1)S(1)} %get-tuple-element.26.refs_0_, bf16[8,16,8,256]{3,2,1,0:T(8,128)(2,1)S(1)} %get-tuple-element.28.refs_4_.refs_1_, ...), custom_call_target="tpu_custom_call", output_to_operand_aliasing={{}: (5, {})} | custom-call | flops 134217728 | bytes 1572864 | tf_op jit(solution)/shard_map/pallas_call | solution.py:271
  (4 shorter events, 0.1 us)
Async XLA Ops:
  0.0 22.7 %copy-start.1 = (bf16[3,3,256,256]{3,2,1,0:T(8,128)(2,1)S(1)}, bf16[3,3,256,256]{3,2,1,0:T(8,128)(2,1)}, u32[]{:S(2)}) copy-start(bf16[3,3,256,256]{3,2,1,0:T(8,128)(2,1)} %param.9) | copy-start | bytes 3538948
  0.0 22.7 %copy-start.4 = (f32[256]{0:T(256)S(1)}, f32[256]{0:T(256)}, u32[]{:S(2)}) copy-start(f32[256]{0:T(256)} %param.11) | copy-start | bytes 3076
  1.9 20.7 %collective-permute-start.1 = (bf16[129,8,256]{2,1,0:T(8,128)(2,1)}, bf16[129,8,256]{2,1,0:T(8,128)(2,1)}, u32[]{:S(2)}, u32[]{:S(2)}) collective-permute-start(bf16[129,8,256]{2,1,0:T(8,128)(2,1)} %shard_map.82), channel_id=1, source_target_pairs={{0,8},{8,16},{16,24},{24,32},{32,40},{40,48},{48,56},{56,64},{64,7... | collective-permute-start | bytes 1585160 | tf_op jit(solution)/shard_map/ppermute | solution.py:336
  4.5 18.2 %collective-permute-start = (bf16[129,8,256]{2,1,0:T(8,128)(2,1)}, bf16[129,8,256]{2,1,0:T(8,128)(2,1)}, u32[]{:S(2)}, u32[]{:S(2)}) collective-permute-start(bf16[129,8,256]{2,1,0:T(8,128)(2,1)} %shard_map.82), channel_id=1, source_target_pairs={{0,248},{8,0},{16,8},{24,16},{32,24},{40,32},{48,40},{56,48},{64,5... | collective-permute-start | bytes 1585160 | tf_op jit(solution)/shard_map/ppermute | solution.py:336
  10.7 1.3 %copy-start = (bf16[3,3,256,256]{3,2,1,0:T(8,128)(2,1)S(1)}, bf16[3,3,256,256]{3,2,1,0:T(8,128)(2,1)}, u32[]{:S(2)}) copy-start(bf16[3,3,256,256]{3,2,1,0:T(8,128)(2,1)} %param.9) | copy-start | bytes 3538948
  12.0 1.2 %copy-start.2 = (bf16[1,256,8,256]{3,2,1,0:T(8,128)(2,1)S(1)}, bf16[1,256,8,256]{3,2,1,0:T(8,128)(2,1)}, u32[]{:S(2)}) copy-start(bf16[1,256,8,256]{3,2,1,0:T(8,128)(2,1)} %param.8) | copy-start | bytes 3145732
  13.2 0.7 copy-start.8
  15.6 18.4 %collective-permute-start.3 = (bf16[129,8,256]{2,1,0:T(8,128)(2,1)}, bf16[129,8,256]{2,1,0:T(8,128)(2,1)}, u32[]{:S(2)}, u32[]{:S(2)}) collective-permute-start(bf16[129,8,256]{2,1,0:T(8,128)(2,1)} %get-tuple-element.27), channel_id=1, source_target_pairs={{0,8},{8,16},{16,24},{24,32},{32,40},{40,48},{48,56},{56,64},{64,7... | collective-permute-start | bytes 1585160 | tf_op jit(solution)/shard_map/ppermute | solution.py:336
  15.6 18.4 %collective-permute-start.2 = (bf16[129,8,256]{2,1,0:T(8,128)(2,1)}, bf16[129,8,256]{2,1,0:T(8,128)(2,1)}, u32[]{:S(2)}, u32[]{:S(2)}) collective-permute-start(bf16[129,8,256]{2,1,0:T(8,128)(2,1)} %get-tuple-element.27), channel_id=1, source_target_pairs={{0,248},{8,0},{16,8},{24,16},{32,24},{40,32},{48,40},{56,48},{64,5... | collective-permute-start | bytes 1585160 | tf_op jit(solution)/shard_map/ppermute | solution.py:336
  25.4 11.3 %collective-permute-start.4 = (bf16[2,16,8,256]{3,2,1,0:T(8,128)(2,1)S(1)}, bf16[2,16,8,256]{3,2,1,0:T(8,128)(2,1)S(1)}, u32[]{:S(2)}, u32[]{:S(2)}) collective-permute-start(bf16[2,16,8,256]{3,2,1,0:T(8,128)(2,1)S(1)} %get-tuple-element.30), channel_id=1, source_target_pairs={{0,2},{1,3},{2,4},{3,5},{4,6},{5,7},{6,0},{7,1},{8,10},{9,11},{10,... | collective-permute-start | bytes 393224 | tf_op jit(solution)/shard_map/ppermute | solution.py:300
  26.8 9.9 %collective-permute-start.5 = (bf16[2,16,8,256]{3,2,1,0:T(8,128)(2,1)S(1)}, bf16[2,16,8,256]{3,2,1,0:T(8,128)(2,1)S(1)}, u32[]{:S(2)}, u32[]{:S(2)}) collective-permute-start(bf16[2,16,8,256]{3,2,1,0:T(8,128)(2,1)S(1)} %get-tuple-element.31), channel_id=1, source_target_pairs={{0,4},{1,5},{2,6},{3,7},{4,0},{5,1},{6,2},{7,3},{8,12},{9,13},{10,... | collective-permute-start | bytes 393224 | tf_op jit(solution)/shard_map/ppermute | solution.py:300
  29.4 13.7 %copy-start.5 = (bf16[256,256]{1,0:T(8,128)(2,1)S(1)}, bf16[256,256]{1,0:T(8,128)(2,1)}, u32[]{:S(2)}) copy-start(bf16[256,256]{1,0:T(8,128)(2,1)} %wq_ref.3) | copy-start | bytes 393220
  29.4 13.7 %copy-start.6 = (bf16[256,256]{1,0:T(8,128)(2,1)S(1)}, bf16[256,256]{1,0:T(8,128)(2,1)}, u32[]{:S(2)}) copy-start(bf16[256,256]{1,0:T(8,128)(2,1)} %wk_ref.3) | copy-start | bytes 393220
  29.4 13.7 %copy-start.7 = (bf16[256,256]{1,0:T(8,128)(2,1)S(1)}, bf16[256,256]{1,0:T(8,128)(2,1)}, u32[]{:S(2)}) copy-start(bf16[256,256]{1,0:T(8,128)(2,1)} %wv_ref.3) | copy-start | bytes 393220
  29.4 7.3 %collective-permute-start.6 = (bf16[2,16,8,256]{3,2,1,0:T(8,128)(2,1)S(1)}, bf16[2,16,8,256]{3,2,1,0:T(8,128)(2,1)S(1)}, u32[]{:S(2)}, u32[]{:S(2)}) collective-permute-start(bf16[2,16,8,256]{3,2,1,0:T(8,128)(2,1)S(1)} %get-tuple-element.32), channel_id=1, source_target_pairs={{0,6},{1,7},{2,0},{3,1},{4,2},{5,3},{6,4},{7,5},{8,14},{9,15},{10,... | collective-permute-start | bytes 393224 | tf_op jit(solution)/shard_map/ppermute | solution.py:300
  36.8 6.3 %collective-permute-start.7 = (bf16[4,16,8,256]{3,2,1,0:T(8,128)(2,1)S(1)}, bf16[4,16,8,256]{3,2,1,0:T(8,128)(2,1)S(1)}, u32[]{:S(2)}, u32[]{:S(2)}) collective-permute-start(bf16[4,16,8,256]{3,2,1,0:T(8,128)(2,1)S(1)} %shard_map.86), channel_id=1, source_target_pairs={{0,1},{1,0},{2,3},{3,2},{4,5},{5,4},{6,7},{7,6},{8,9},{9,8},{10,11... | collective-permute-start | bytes 786440 | tf_op jit(solution)/shard_map/ppermute | solution.py:319
  38.1 8.0 %collective-permute-start.11 = (bf16[2,16,8,256]{3,2,1,0:T(8,128)(2,1)S(1)}, bf16[2,16,8,256]{3,2,1,0:T(8,128)(2,1)S(1)}, u32[]{:S(2)}, u32[]{:S(2)}) collective-permute-start(bf16[2,16,8,256]{3,2,1,0:T(8,128)(2,1)S(1)} %get-tuple-element.38), channel_id=1, source_target_pairs={{0,2},{1,3},{2,4},{3,5},{4,6},{5,7},{6,0},{7,1},{8,10},{9,11},{10,... | collective-permute-start | bytes 393224 | tf_op jit(solution)/shard_map/ppermute | solution.py:300
  39.4 9.0 %collective-permute-start.12 = (bf16[2,16,8,256]{3,2,1,0:T(8,128)(2,1)S(1)}, bf16[2,16,8,256]{3,2,1,0:T(8,128)(2,1)S(1)}, u32[]{:S(2)}, u32[]{:S(2)}) collective-permute-start(bf16[2,16,8,256]{3,2,1,0:T(8,128)(2,1)S(1)} %get-tuple-element.39), channel_id=1, source_target_pairs={{0,4},{1,5},{2,6},{3,7},{4,0},{5,1},{6,2},{7,3},{8,12},{9,13},{10,... | collective-permute-start | bytes 393224 | tf_op jit(solution)/shard_map/ppermute | solution.py:300
  42.0 6.4 %collective-permute-start.13 = (bf16[2,16,8,256]{3,2,1,0:T(8,128)(2,1)S(1)}, bf16[2,16,8,256]{3,2,1,0:T(8,128)(2,1)S(1)}, u32[]{:S(2)}, u32[]{:S(2)}) collective-permute-start(bf16[2,16,8,256]{3,2,1,0:T(8,128)(2,1)S(1)} %get-tuple-element.40), channel_id=1, source_target_pairs={{0,6},{1,7},{2,0},{3,1},{4,2},{5,3},{6,4},{7,5},{8,14},{9,15},{10,... | collective-permute-start | bytes 393224 | tf_op jit(solution)/shard_map/ppermute | solution.py:300
  48.4 4.1 %collective-permute-start.14 = (bf16[4,16,8,256]{3,2,1,0:T(8,128)(2,1)S(1)}, bf16[4,16,8,256]{3,2,1,0:T(8,128)(2,1)S(1)}, u32[]{:S(2)}, u32[]{:S(2)}) collective-permute-start(bf16[4,16,8,256]{3,2,1,0:T(8,128)(2,1)S(1)} %shard_map.88), channel_id=1, source_target_pairs={{0,1},{1,0},{2,3},{3,2},{4,5},{5,4},{6,7},{7,6},{8,9},{9,8},{10,11... | collective-permute-start | bytes 786440 | tf_op jit(solution)/shard_map/ppermute | solution.py:319
  49.4 9.3 %collective-permute-start.8 = (bf16[2,16,8,256]{3,2,1,0:T(8,128)(2,1)S(1)}, bf16[2,16,8,256]{3,2,1,0:T(8,128)(2,1)S(1)}, u32[]{:S(2)}, u32[]{:S(2)}) collective-permute-start(bf16[2,16,8,256]{3,2,1,0:T(8,128)(2,1)S(1)} %get-tuple-element.34), channel_id=1, source_target_pairs={{0,6},{1,7},{2,0},{3,1},{4,2},{5,3},{6,4},{7,5},{8,14},{9,15},{10,... | collective-permute-start | bytes 393224 | tf_op jit(solution)/shard_map/ppermute | solution.py:300
  51.2 7.5 %collective-permute-start.9 = (bf16[2,16,8,256]{3,2,1,0:T(8,128)(2,1)S(1)}, bf16[2,16,8,256]{3,2,1,0:T(8,128)(2,1)S(1)}, u32[]{:S(2)}, u32[]{:S(2)}) collective-permute-start(bf16[2,16,8,256]{3,2,1,0:T(8,128)(2,1)S(1)} %get-tuple-element.35), channel_id=1, source_target_pairs={{0,4},{1,5},{2,6},{3,7},{4,0},{5,1},{6,2},{7,3},{8,12},{9,13},{10,... | collective-permute-start | bytes 393224 | tf_op jit(solution)/shard_map/ppermute | solution.py:300
  52.1 16.1 %copy-start.3 = (bf16[256,256]{1,0:T(8,128)(2,1)S(1)}, bf16[256,256]{1,0:T(8,128)(2,1)}, u32[]{:S(2)}) copy-start(bf16[256,256]{1,0:T(8,128)(2,1)} %w_ref.3) | copy-start | bytes 393220
  52.1 8.9 %collective-permute-start.10 = (bf16[2,16,8,256]{3,2,1,0:T(8,128)(2,1)S(1)}, bf16[2,16,8,256]{3,2,1,0:T(8,128)(2,1)S(1)}, u32[]{:S(2)}, u32[]{:S(2)}) collective-permute-start(bf16[2,16,8,256]{3,2,1,0:T(8,128)(2,1)S(1)} %get-tuple-element.36), channel_id=1, source_target_pairs={{0,2},{1,3},{2,4},{3,5},{4,6},{5,7},{6,0},{7,1},{8,10},{9,11},{10,... | collective-permute-start | bytes 393224 | tf_op jit(solution)/shard_map/ppermute | solution.py:300
  55.5 5.5 %collective-permute-start.15 = (bf16[2,16,8,256]{3,2,1,0:T(8,128)(2,1)S(1)}, bf16[2,16,8,256]{3,2,1,0:T(8,128)(2,1)S(1)}, u32[]{:S(2)}, u32[]{:S(2)}) collective-permute-start(bf16[2,16,8,256]{3,2,1,0:T(8,128)(2,1)S(1)} %get-tuple-element.42), channel_id=1, source_target_pairs={{0,6},{1,7},{2,0},{3,1},{4,2},{5,3},{6,4},{7,5},{8,14},{9,15},{10,... | collective-permute-start | bytes 393224 | tf_op jit(solution)/shard_map/ppermute | solution.py:300
  57.8 5.4 %collective-permute-start.16 = (bf16[2,16,8,256]{3,2,1,0:T(8,128)(2,1)S(1)}, bf16[2,16,8,256]{3,2,1,0:T(8,128)(2,1)S(1)}, u32[]{:S(2)}, u32[]{:S(2)}) collective-permute-start(bf16[2,16,8,256]{3,2,1,0:T(8,128)(2,1)S(1)} %get-tuple-element.43), channel_id=1, source_target_pairs={{0,4},{1,5},{2,6},{3,7},{4,0},{5,1},{6,2},{7,3},{8,12},{9,13},{10,... | collective-permute-start | bytes 393224 | tf_op jit(solution)/shard_map/ppermute | solution.py:300
  58.7 8.1 %collective-permute-start.17 = (bf16[2,16,8,256]{3,2,1,0:T(8,128)(2,1)S(1)}, bf16[2,16,8,256]{3,2,1,0:T(8,128)(2,1)S(1)}, u32[]{:S(2)}, u32[]{:S(2)}) collective-permute-start(bf16[2,16,8,256]{3,2,1,0:T(8,128)(2,1)S(1)} %get-tuple-element.44), channel_id=1, source_target_pairs={{0,2},{1,3},{2,4},{3,5},{4,6},{5,7},{6,0},{7,1},{8,10},{9,11},{10,... | collective-permute-start | bytes 393224 | tf_op jit(solution)/shard_map/ppermute | solution.py:300
  66.8 2.9 %collective-permute-start.18 = (bf16[4,32,8,256]{3,2,1,0:T(8,128)(2,1)S(1)}, bf16[4,32,8,256]{3,2,1,0:T(8,128)(2,1)S(1)}, u32[]{:S(2)}, u32[]{:S(2)}) collective-permute-start(bf16[4,32,8,256]{3,2,1,0:T(8,128)(2,1)S(1)} %shard_map.90), channel_id=1, source_target_pairs={{0,1},{1,0},{2,3},{3,2},{4,5},{5,4},{6,7},{7,6},{8,9},{9,8},{10,11... | collective-permute-start | bytes 1572872 | tf_op jit(solution)/shard_map/ppermute | solution.py:319

commit v7 on v6

--- a/solution.py
+++ b/solution.py
@@ -285,11 +285,15 @@
     )(*args)
 
 
+def farthest_first(chips):
+    return [0] + sorted(range(1, chips), key=lambda k: abs(k - chips // 2))
+
+
 def gather_kernel(chunks, chips, *refs):
     out, low = refs[-1], 0
     for near in [refs[i * chips : (i + 1) * chips] for i in range(chunks)]:
         width = near[0].shape[1]
-        for k, ref in enumerate(near):
+        for k, ref in zip(farthest_first(chips), near):
             out[k, low : low + width] = ref[1]
         low += width
 
@@ -307,7 +311,7 @@
 def swap(nears, *before):
     chips, leads, chans = len(nears[0]), *nears[0][0].shape[2:]
     count = sum(near[0].shape[1] for near in nears)
-    flat = [x for near in nears for x in near]
+    flat = [near[k] for near in nears for k in farthest_first(chips)]
     others = pl.pallas_call(
         functools.partial(gather_kernel, len(nears), chips),
         out_shape=pltpu.VMEM((chips, count, leads, chans), BF16),

time: 71.8 us -> 70.5 us (0.982)
  waiting for transfers between devices: 16.1 us -> 14.3 us
    ppermute x12, waiting for transfers between devices: 10.5 us -> 8.66 us  [send(): lax.ppermute(pieces[k], 'lead', [(i, (i + 2 * sign * k) % (2 * chips)) fo...]
  transfers between devices with their start and end apart: 19 -> 19, of which waited for: 7 -> 6; matrix products, arithmetic and copies ran while one was open for 0% -> 0% of each run, Pallas kernels for 21% -> 21%
where the time goes in v7:
time: 70.5 us; the launch traced here: 70.3 us
  starting transfers between devices  34 us (48%)
  Pallas kernels  18.4 us (26%)
  waiting for transfers between devices  14.3 us (20%)
  local copies, waits for them, and re-layouts  3.19 us (5%)
    ppermute x12, starting transfers between devices, send(): lax.ppermute(pieces[k], 'lead', [(i, (i + 2 * sign * k) % (2 * chips)) fo...  16.7 us
    ppermute x2, starting transfers between devices, shards(): lax.ppermute(piece, 'lat', south)  11 us
    ppermute x12, waiting for transfers between devices, send(): lax.ppermute(pieces[k], 'lead', [(i, (i + 2 * sign * k) % (2 * chips)) fo...  8.66 us
    pallas_call x2, Pallas kernels, attend(): pl.pallas_call(functools.partial(attend_kernel, math.gcd(pixels, 16), chi...  5.9 us
    ppermute x2, waiting for transfers between devices, shards(): lax.ppermute(piece, 'lat', north)  5.66 us
    pallas_call x2, Pallas kernels, conv_norm(): pl.pallas_call(functools.partial(conv_kernel, tile, start - low, start, l...  5.5 us
    ppermute x3, starting transfers between devices, swap(): return lax.ppermute(others, 'lead', [(i, i ^ 1) for i in range(2 * chips)])  3.8 us
    pallas_call x2, Pallas kernels, project_out(): pl.pallas_call(functools.partial(out_kernel, starts, core, chips), out_sh...  3.25 us
  transfers between devices with their start and end apart: 19, of which 6 were waited for; matrix products, arithmetic and copies ran while one was open for 0% of the time, Pallas kernels for 21%

profile of v7, /device:TPU:1, one launch (start us, length us, event | category | flops | bytes accessed | tf_op | source)
XLA Modules:
  0.0 70.3 jit_solution(4465030859619236002)
XLA Ops:
  0.0 0.0 copy-start.1
  0.0 0.0 copy-start.4
  0.0 1.9 %shard_map.82 = bf16[129,8,256]{2,1,0:T(8,128)(2,1)} custom-call(bf16[256,8,256]{2,1,0:T(8,128)(2,1)} %bitcast.10), custom_call_target="tpu_custom_call" | custom-call | bytes 1048576 | tf_op jit(solution)/shard_map/pallas_call | solution.py:80
  1.9 2.5 %collective-permute-start.1 = (bf16[129,8,256]{2,1,0:T(8,128)(2,1)}, bf16[129,8,256]{2,1,0:T(8,128)(2,1)}, u32[]{:S(2)}, u32[]{:S(2)}) collective-permute-start(bf16[129,8,256]{2,1,0:T(8,128)(2,1)} %shard_map.82), channel_id=1, source_target_pairs={{0,8},{8,16},{16,24},{24,32},{32,40},{40,48},{48,56},{56,64},{64,7... | collective-permute-start | bytes 1585160 | tf_op jit(solution)/shard_map/ppermute | solution.py:340
  4.5 6.2 %collective-permute-start = (bf16[129,8,256]{2,1,0:T(8,128)(2,1)}, bf16[129,8,256]{2,1,0:T(8,128)(2,1)}, u32[]{:S(2)}, u32[]{:S(2)}) collective-permute-start(bf16[129,8,256]{2,1,0:T(8,128)(2,1)} %shard_map.82), channel_id=1, source_target_pairs={{0,248},{8,0},{16,8},{24,16},{32,24},{40,32},{48,40},{56,48},{64,5... | collective-permute-start | bytes 1585160 | tf_op jit(solution)/shard_map/ppermute | solution.py:340
  10.7 0.0 copy-start
  10.7 1.3 %copy-done = bf16[3,3,256,256]{3,2,1,0:T(8,128)(2,1)S(1)} copy-done((bf16[3,3,256,256]{3,2,1,0:T(8,128)(2,1)S(1)}, bf16[3,3,256,256]{3,2,1,0:T(8,128)(2,1)}, u32[]{:S(2)}) %copy-start) | copy-done | bytes 1179672
  12.0 0.0 copy-start.2
  12.0 1.2 %copy-done.2 = bf16[1,256,8,256]{3,2,1,0:T(8,128)(2,1)S(1)} copy-done((bf16[1,256,8,256]{3,2,1,0:T(8,128)(2,1)S(1)}, bf16[1,256,8,256]{3,2,1,0:T(8,128)(2,1)}, u32[]{:S(2)}) %copy-start.2) | copy-done | bytes 1048600
  13.2 0.0 copy-start.8
  13.2 0.7 copy-done.8
  13.9 1.7 %shard_map.83 = (f32[2048,256]{1,0:T(8,128)S(1)}, bf16[129,8,256]{2,1,0:T(8,128)(2,1)}) custom-call(bf16[256,8,256]{2,1,0:T(8,128)(2,1)S(1)} %bitcast.11, bf16[9,256,256]{2,1,0:T(8,128)(2,1)S(1)} %bitcast.7, f32[1,256]{1,0:T(1,128)S(1)} %bitcast.14), custom_call_target="tpu_custom_call" | custom-call | flops 805306368 | bytes 3145728 | tf_op jit(solution)/shard_map/pallas_call | solution.py:107
  15.6 0.0 collective-permute-start.3
  15.6 4.8 %collective-permute-start.2 = (bf16[129,8,256]{2,1,0:T(8,128)(2,1)}, bf16[129,8,256]{2,1,0:T(8,128)(2,1)}, u32[]{:S(2)}, u32[]{:S(2)}) collective-permute-start(bf16[129,8,256]{2,1,0:T(8,128)(2,1)} %get-tuple-element.27), channel_id=1, source_target_pairs={{0,248},{8,0},{16,8},{24,16},{32,24},{40,32},{48,40},{56,48},{64,5... | collective-permute-start | bytes 1585160 | tf_op jit(solution)/shard_map/ppermute | solution.py:340
  20.4 0.1 pad_add_fusion.ids
  20.5 2.2 %collective-permute-done.1.up = bf16[129,8,256]{2,1,0:T(8,128)(2,1)} collective-permute-done((bf16[129,8,256]{2,1,0:T(8,128)(2,1)}, bf16[129,8,256]{2,1,0:T(8,128)(2,1)}, u32[]{:S(2)}, u32[]{:S(2)}) %collective-permute-start.1) | collective-permute-done | bytes 528416 | tf_op jit(solution)/shard_map/ppermute | solution.py:340
  22.7 0.0 collective-permute-done.down
  22.7 0.0 copy-done.1
  22.7 0.0 copy-done.4
  22.7 2.8 %shard_map.84 = (bf16[8,16,8,256]{3,2,1,0:T(8,128)(2,1)S(1)}, bf16[2,16,8,256]{3,2,1,0:T(8,128)(2,1)S(1)}, bf16[2,16,8,256]{3,2,1,0:T(8,128)(2,1)S(1)}, bf16[2,1...) custom-call(s32[2]{0:T(128)S(1)} %pad_add_fusion.ids, bf16[129,8,256]{2,1,0:T(8,128)(2,1)} %collective-permute-done.down, ...), custom_call_target="tpu_custom_call" | custom-call | flops 805306368 | bytes 3145728 | tf_op jit(solution)/shard_map/pallas_call | solution.py:161
  25.4 1.4 %collective-permute-start.4 = (bf16[2,16,8,256]{3,2,1,0:T(8,128)(2,1)S(1)}, bf16[2,16,8,256]{3,2,1,0:T(8,128)(2,1)S(1)}, u32[]{:S(2)}, u32[]{:S(2)}) collective-permute-start(bf16[2,16,8,256]{3,2,1,0:T(8,128)(2,1)S(1)} %get-tuple-element.30), channel_id=1, source_target_pairs={{0,2},{1,3},{2,4},{3,5},{4,6},{5,7},{6,0},{7,1},{8,10},{9,11},{10,... | collective-permute-start | bytes 393224 | tf_op jit(solution)/shard_map/ppermute | solution.py:304
  26.8 2.6 %collective-permute-start.5 = (bf16[2,16,8,256]{3,2,1,0:T(8,128)(2,1)S(1)}, bf16[2,16,8,256]{3,2,1,0:T(8,128)(2,1)S(1)}, u32[]{:S(2)}, u32[]{:S(2)}) collective-permute-start(bf16[2,16,8,256]{3,2,1,0:T(8,128)(2,1)S(1)} %get-tuple-element.31), channel_id=1, source_target_pairs={{0,4},{1,5},{2,6},{3,7},{4,0},{5,1},{6,2},{7,3},{8,12},{9,13},{10,... | collective-permute-start | bytes 393224 | tf_op jit(solution)/shard_map/ppermute | solution.py:304
  29.4 0.0 copy-start.5
  29.4 0.0 copy-start.7
  29.4 1.1 %collective-permute-start.6 = (bf16[2,16,8,256]{3,2,1,0:T(8,128)(2,1)S(1)}, bf16[2,16,8,256]{3,2,1,0:T(8,128)(2,1)S(1)}, u32[]{:S(2)}, u32[]{:S(2)}) collective-permute-start(bf16[2,16,8,256]{3,2,1,0:T(8,128)(2,1)S(1)} %get-tuple-element.32), channel_id=1, source_target_pairs={{0,6},{1,7},{2,0},{3,1},{4,2},{5,3},{6,4},{7,5},{8,14},{9,15},{10,... | collective-permute-start | bytes 393224 | tf_op jit(solution)/shard_map/ppermute | solution.py:304
  30.5 3.5 %collective-permute-done.3.up = bf16[129,8,256]{2,1,0:T(8,128)(2,1)} collective-permute-done((bf16[129,8,256]{2,1,0:T(8,128)(2,1)}, bf16[129,8,256]{2,1,0:T(8,128)(2,1)}, u32[]{:S(2)}, u32[]{:S(2)}) %collective-permute-start.3) | collective-permute-done | bytes 528416 | tf_op jit(solution)/shard_map/ppermute | solution.py:340
  34.0 0.0 collective-permute-done.2.down
  34.0 2.7 %shard_map.85 = (bf16[8,16,8,256]{3,2,1,0:T(8,128)(2,1)S(1)}, bf16[2,16,8,256]{3,2,1,0:T(8,128)(2,1)S(1)}, bf16[2,16,8,256]{3,2,1,0:T(8,128)(2,1)S(1)}, bf16[2,1...) custom-call(s32[2]{0:T(128)S(1)} %pad_add_fusion.ids, bf16[129,8,256]{2,1,0:T(8,128)(2,1)} %collective-permute-done.2.down, ...), custom_call_target="tpu_custom_call" | custom-call | flops 805306368 | bytes 3145728 | tf_op jit(solution)/shard_map/pallas_call | solution.py:161
  36.7 0.0 collective-permute-done.4.refs_2_.refs_1_
  36.7 0.0 collective-permute-done.5.refs_1_.refs_2_
  36.8 0.0 collective-permute-done.6.refs_3_
  36.8 1.3 %collective-permute-start.7 = (bf16[4,16,8,256]{3,2,1,0:T(8,128)(2,1)S(1)}, bf16[4,16,8,256]{3,2,1,0:T(8,128)(2,1)S(1)}, u32[]{:S(2)}, u32[]{:S(2)}) collective-permute-start(bf16[4,16,8,256]{3,2,1,0:T(8,128)(2,1)S(1)} %shard_map.86), channel_id=1, source_target_pairs={{0,1},{1,0},{2,3},{3,2},{4,5},{5,4},{6,7},{7,6},{8,9},{9,8},{10,11... | collective-permute-start | bytes 786440 | tf_op jit(solution)/shard_map/ppermute | solution.py:323
  38.1 1.3 %collective-permute-start.11 = (bf16[2,16,8,256]{3,2,1,0:T(8,128)(2,1)S(1)}, bf16[2,16,8,256]{3,2,1,0:T(8,128)(2,1)S(1)}, u32[]{:S(2)}, u32[]{:S(2)}) collective-permute-start(bf16[2,16,8,256]{3,2,1,0:T(8,128)(2,1)S(1)} %get-tuple-element.38), channel_id=1, source_target_pairs={{0,2},{1,3},{2,4},{3,5},{4,6},{5,7},{6,0},{7,1},{8,10},{9,11},{10,... | collective-permute-start | bytes 393224 | tf_op jit(solution)/shard_map/ppermute | solution.py:304
  39.4 2.6 %collective-permute-start.12 = (bf16[2,16,8,256]{3,2,1,0:T(8,128)(2,1)S(1)}, bf16[2,16,8,256]{3,2,1,0:T(8,128)(2,1)S(1)}, u32[]{:S(2)}, u32[]{:S(2)}) collective-permute-start(bf16[2,16,8,256]{3,2,1,0:T(8,128)(2,1)S(1)} %get-tuple-element.39), channel_id=1, source_target_pairs={{0,4},{1,5},{2,6},{3,7},{4,0},{5,1},{6,2},{7,3},{8,12},{9,13},{10,... | collective-permute-start | bytes 393224 | tf_op jit(solution)/shard_map/ppermute | solution.py:304
  42.0 1.1 %collective-permute-start.13 = (bf16[2,16,8,256]{3,2,1,0:T(8,128)(2,1)S(1)}, bf16[2,16,8,256]{3,2,1,0:T(8,128)(2,1)S(1)}, u32[]{:S(2)}, u32[]{:S(2)}) collective-permute-start(bf16[2,16,8,256]{3,2,1,0:T(8,128)(2,1)S(1)} %get-tuple-element.40), channel_id=1, source_target_pairs={{0,6},{1,7},{2,0},{3,1},{4,2},{5,3},{6,4},{7,5},{8,14},{9,15},{10,... | collective-permute-start | bytes 393224 | tf_op jit(solution)/shard_map/ppermute | solution.py:304
  43.1 0.0 collective-permute-done.7.refs_4_
  43.1 0.0 copy-done.5
  43.1 0.0 copy-done.6
  43.1 0.0 copy-done.7
  43.1 3.0 %shard_map.87 = (bf16[2,16,8,256]{3,2,1,0:T(8,128)(2,1)S(1)}, bf16[2,16,8,256]{3,2,1,0:T(8,128)(2,1)S(1)}, bf16[2,16,8,256]{3,2,1,0:T(8,128)(2,1)S(1)}, bf16[2,16,8,256]{3,2,1,0:T(8,128)(2,1)S(1)}) custom-call(bf16[256,256]{1,0:T(8,128)(2,1)S(1)} %copy-done.5, bf16[256,256]{1,0:T(8,128)(2,1)S(1)} %copy-done.6, bf16[256,256]{1,0:T(8,128)(2,1)S(1)} %copy-done.7, ...), custom_call_target="tpu_custom_call" | custom-call | flops 1342177280 | bytes 1441792 | tf_op jit(solution)/shard_map/pallas_call | solution.py:226
  46.1 0.0 collective-permute-done.11.refs_2_.refs_1_
  46.1 2.3 %collective-permute-done.12.refs_1_.refs_2_ = bf16[2,16,8,256]{3,2,1,0:T(8,128)(2,1)S(1)} collective-permute-done((bf16[2,16,8,256]{3,2,1,0:T(8,128)(2,1)S(1)}, bf16[2,16,8,256]{3,2,1,0:T(8,128)(2,1)S(1)}, u32[]{:S(2)}, u32[]{:S(2)}) %collective-permute-start.12) | collective-permute-done | bytes 131104 | tf_op jit(solution)/shard_map/ppermute | solution.py:304
  48.4 0.0 collective-permute-done.13.refs_3_
  48.4 1.0 %collective-permute-start.14 = (bf16[4,16,8,256]{3,2,1,0:T(8,128)(2,1)S(1)}, bf16[4,16,8,256]{3,2,1,0:T(8,128)(2,1)S(1)}, u32[]{:S(2)}, u32[]{:S(2)}) collective-permute-start(bf16[4,16,8,256]{3,2,1,0:T(8,128)(2,1)S(1)} %shard_map.88), channel_id=1, source_target_pairs={{0,1},{1,0},{2,3},{3,2},{4,5},{5,4},{6,7},{7,6},{8,9},{9,8},{10,11... | collective-permute-start | bytes 786440 | tf_op jit(solution)/shard_map/ppermute | solution.py:323
  49.4 2.3 %collective-permute-start.8 = (bf16[2,16,8,256]{3,2,1,0:T(8,128)(2,1)S(1)}, bf16[2,16,8,256]{3,2,1,0:T(8,128)(2,1)S(1)}, u32[]{:S(2)}, u32[]{:S(2)}) collective-permute-start(bf16[2,16,8,256]{3,2,1,0:T(8,128)(2,1)S(1)} %get-tuple-element.34), channel_id=1, source_target_pairs={{0,4},{1,5},{2,6},{3,7},{4,0},{5,1},{6,2},{7,3},{8,12},{9,13},{10,... | collective-permute-start | bytes 393224 | tf_op jit(solution)/shard_map/ppermute | solution.py:304
  51.7 0.9 %collective-permute-start.9 = (bf16[2,16,8,256]{3,2,1,0:T(8,128)(2,1)S(1)}, bf16[2,16,8,256]{3,2,1,0:T(8,128)(2,1)S(1)}, u32[]{:S(2)}, u32[]{:S(2)}) collective-permute-start(bf16[2,16,8,256]{3,2,1,0:T(8,128)(2,1)S(1)} %get-tuple-element.35), channel_id=1, source_target_pairs={{0,6},{1,7},{2,0},{3,1},{4,2},{5,3},{6,4},{7,5},{8,14},{9,15},{10,... | collective-permute-start | bytes 393224 | tf_op jit(solution)/shard_map/ppermute | solution.py:304
  52.7 0.0 copy-start.3
  52.7 0.5 collective-permute-start.10
  53.2 0.0 collective-permute-done.14.refs_4_
  53.2 2.9 %shard_map.89 = (bf16[2,16,8,256]{3,2,1,0:T(8,128)(2,1)S(1)}, bf16[2,16,8,256]{3,2,1,0:T(8,128)(2,1)S(1)}, bf16[2,16,8,256]{3,2,1,0:T(8,128)(2,1)S(1)}, bf16[2,16,8,256]{3,2,1,0:T(8,128)(2,1)S(1)}) custom-call(bf16[256,256]{1,0:T(8,128)(2,1)S(1)} %copy-done.5, bf16[256,256]{1,0:T(8,128)(2,1)S(1)} %copy-done.6, bf16[256,256]{1,0:T(8,128)(2,1)S(1)} %copy-done.7, ...), custom_call_target="tpu_custom_call" | custom-call | flops 1342177280 | bytes 1441792 | tf_op jit(solution)/shard_map/pallas_call | solution.py:226
  56.1 0.8 %collective-permute-start.15 = (bf16[2,16,8,256]{3,2,1,0:T(8,128)(2,1)S(1)}, bf16[2,16,8,256]{3,2,1,0:T(8,128)(2,1)S(1)}, u32[]{:S(2)}, u32[]{:S(2)}) collective-permute-start(bf16[2,16,8,256]{3,2,1,0:T(8,128)(2,1)S(1)} %get-tuple-element.42), channel_id=1, source_target_pairs={{0,4},{1,5},{2,6},{3,7},{4,0},{5,1},{6,2},{7,3},{8,12},{9,13},{10,... | collective-permute-start | bytes 393224 | tf_op jit(solution)/shard_map/ppermute | solution.py:304
  56.9 1.8 %collective-permute-start.16 = (bf16[2,16,8,256]{3,2,1,0:T(8,128)(2,1)S(1)}, bf16[2,16,8,256]{3,2,1,0:T(8,128)(2,1)S(1)}, u32[]{:S(2)}, u32[]{:S(2)}) collective-permute-start(bf16[2,16,8,256]{3,2,1,0:T(8,128)(2,1)S(1)} %get-tuple-element.43), channel_id=1, source_target_pairs={{0,6},{1,7},{2,0},{3,1},{4,2},{5,3},{6,4},{7,5},{8,14},{9,15},{10,... | collective-permute-start | bytes 393224 | tf_op jit(solution)/shard_map/ppermute | solution.py:304
  58.7 0.0 collective-permute-done.8.refs_1_.refs_4_
  58.7 0.3 collective-permute-start.17
  59.0 0.0 collective-permute-done.9.refs_2_.refs_3_
  59.0 0.0 collective-permute-done.10.refs_3_.refs_5_
  59.0 2.6 %collective-permute-done.15.refs_5_.refs_8_ = bf16[2,16,8,256]{3,2,1,0:T(8,128)(2,1)S(1)} collective-permute-done((bf16[2,16,8,256]{3,2,1,0:T(8,128)(2,1)S(1)}, bf16[2,16,8,256]{3,2,1,0:T(8,128)(2,1)S(1)}, u32[]{:S(2)}, u32[]{:S(2)}) %collective-permute-start.15) | collective-permute-done | bytes 131104 | tf_op jit(solution)/shard_map/ppermute | solution.py:304
  61.5 3.0 %collective-permute-done.16.refs_6_.refs_7_ = bf16[2,16,8,256]{3,2,1,0:T(8,128)(2,1)S(1)} collective-permute-done((bf16[2,16,8,256]{3,2,1,0:T(8,128)(2,1)S(1)}, bf16[2,16,8,256]{3,2,1,0:T(8,128)(2,1)S(1)}, u32[]{:S(2)}, u32[]{:S(2)}) %collective-permute-start.16) | collective-permute-done | bytes 131104 | tf_op jit(solution)/shard_map/ppermute | solution.py:304
  64.5 0.8 %collective-permute-done.17.refs_7_.refs_9_ = bf16[2,16,8,256]{3,2,1,0:T(8,128)(2,1)S(1)} collective-permute-done((bf16[2,16,8,256]{3,2,1,0:T(8,128)(2,1)S(1)}, bf16[2,16,8,256]{3,2,1,0:T(8,128)(2,1)S(1)}, u32[]{:S(2)}, u32[]{:S(2)}) %collective-permute-start.17) | collective-permute-done | bytes 131104 | tf_op jit(solution)/shard_map/ppermute | solution.py:304
  65.3 1.5 %collective-permute-start.18 = (bf16[4,32,8,256]{3,2,1,0:T(8,128)(2,1)S(1)}, bf16[4,32,8,256]{3,2,1,0:T(8,128)(2,1)S(1)}, u32[]{:S(2)}, u32[]{:S(2)}) collective-permute-start(bf16[4,32,8,256]{3,2,1,0:T(8,128)(2,1)S(1)} %shard_map.90), channel_id=1, source_target_pairs={{0,1},{1,0},{2,3},{3,2},{4,5},{5,4},{6,7},{7,6},{8,9},{9,8},{10,11... | collective-permute-start | bytes 1572872 | tf_op jit(solution)/shard_map/ppermute | solution.py:323
  66.9 0.0 copy-done.3
  66.9 1.6 %shard_map.91.refs_3_ = bf16[256,8,256]{2,1,0:T(8,128)(2,1)} custom-call(s32[2]{0:T(128)S(1)} %pad_add_fusion.ids, bf16[256,256]{1,0:T(8,128)(2,1)S(1)} %copy-done.3, bf16[8,16,8,256]{3,2,1,0:T(8,128)(2,1)S(1)} %get-tuple-element.26.refs_0_, bf16[8,16,8,256]{3,2,1,0:T(8,128)(2,1)S(1)} %get-tuple-element.28.refs_4_.refs_1_, ...), custom_call_target="tpu_custom_call" | custom-call | flops 134217728 | bytes 1572864 | tf_op jit(solution)/shard_map/pallas_call | solution.py:271
  68.5 0.0 collective-permute-done.18.refs_2_
  68.5 1.6 %shard_map.92 = bf16[256,8,256]{2,1,0:T(8,128)(2,1)} custom-call(s32[2]{0:T(128)S(1)} %pad_add_fusion.ids, bf16[256,256]{1,0:T(8,128)(2,1)S(1)} %copy-done.3, bf16[8,16,8,256]{3,2,1,0:T(8,128)(2,1)S(1)} %get-tuple-element.26.refs_0_, bf16[8,16,8,256]{3,2,1,0:T(8,128)(2,1)S(1)} %get-tuple-element.28.refs_4_.refs_1_, ...), custom_call_target="tpu_custom_call", output_to_operand_aliasing={{}: (5, {})} | custom-call | flops 134217728 | bytes 1572864 | tf_op jit(solution)/shard_map/pallas_call | solution.py:271
  (4 shorter events, 0.1 us)
Async XLA Ops:
  0.0 22.7 %copy-start.1 = (bf16[3,3,256,256]{3,2,1,0:T(8,128)(2,1)S(1)}, bf16[3,3,256,256]{3,2,1,0:T(8,128)(2,1)}, u32[]{:S(2)}) copy-start(bf16[3,3,256,256]{3,2,1,0:T(8,128)(2,1)} %param.9) | copy-start | bytes 3538948
  0.0 22.7 %copy-start.4 = (f32[256]{0:T(256)S(1)}, f32[256]{0:T(256)}, u32[]{:S(2)}) copy-start(f32[256]{0:T(256)} %param.11) | copy-start | bytes 3076
  1.9 20.7 %collective-permute-start.1 = (bf16[129,8,256]{2,1,0:T(8,128)(2,1)}, bf16[129,8,256]{2,1,0:T(8,128)(2,1)}, u32[]{:S(2)}, u32[]{:S(2)}) collective-permute-start(bf16[129,8,256]{2,1,0:T(8,128)(2,1)} %shard_map.82), channel_id=1, source_target_pairs={{0,8},{8,16},{16,24},{24,32},{32,40},{40,48},{48,56},{56,64},{64,7... | collective-permute-start | bytes 1585160 | tf_op jit(solution)/shard_map/ppermute | solution.py:340
  4.5 18.2 %collective-permute-start = (bf16[129,8,256]{2,1,0:T(8,128)(2,1)}, bf16[129,8,256]{2,1,0:T(8,128)(2,1)}, u32[]{:S(2)}, u32[]{:S(2)}) collective-permute-start(bf16[129,8,256]{2,1,0:T(8,128)(2,1)} %shard_map.82), channel_id=1, source_target_pairs={{0,248},{8,0},{16,8},{24,16},{32,24},{40,32},{48,40},{56,48},{64,5... | collective-permute-start | bytes 1585160 | tf_op jit(solution)/shard_map/ppermute | solution.py:340
  10.7 1.3 %copy-start = (bf16[3,3,256,256]{3,2,1,0:T(8,128)(2,1)S(1)}, bf16[3,3,256,256]{3,2,1,0:T(8,128)(2,1)}, u32[]{:S(2)}) copy-start(bf16[3,3,256,256]{3,2,1,0:T(8,128)(2,1)} %param.9) | copy-start | bytes 3538948
  12.0 1.2 %copy-start.2 = (bf16[1,256,8,256]{3,2,1,0:T(8,128)(2,1)S(1)}, bf16[1,256,8,256]{3,2,1,0:T(8,128)(2,1)}, u32[]{:S(2)}) copy-start(bf16[1,256,8,256]{3,2,1,0:T(8,128)(2,1)} %param.8) | copy-start | bytes 3145732
  13.2 0.7 copy-start.8
  15.6 18.4 %collective-permute-start.3 = (bf16[129,8,256]{2,1,0:T(8,128)(2,1)}, bf16[129,8,256]{2,1,0:T(8,128)(2,1)}, u32[]{:S(2)}, u32[]{:S(2)}) collective-permute-start(bf16[129,8,256]{2,1,0:T(8,128)(2,1)} %get-tuple-element.27), channel_id=1, source_target_pairs={{0,8},{8,16},{16,24},{24,32},{32,40},{40,48},{48,56},{56,64},{64,7... | collective-permute-start | bytes 1585160 | tf_op jit(solution)/shard_map/ppermute | solution.py:340
  15.6 18.4 %collective-permute-start.2 = (bf16[129,8,256]{2,1,0:T(8,128)(2,1)}, bf16[129,8,256]{2,1,0:T(8,128)(2,1)}, u32[]{:S(2)}, u32[]{:S(2)}) collective-permute-start(bf16[129,8,256]{2,1,0:T(8,128)(2,1)} %get-tuple-element.27), channel_id=1, source_target_pairs={{0,248},{8,0},{16,8},{24,16},{32,24},{40,32},{48,40},{56,48},{64,5... | collective-permute-start | bytes 1585160 | tf_op jit(solution)/shard_map/ppermute | solution.py:340
  25.4 11.3 %collective-permute-start.4 = (bf16[2,16,8,256]{3,2,1,0:T(8,128)(2,1)S(1)}, bf16[2,16,8,256]{3,2,1,0:T(8,128)(2,1)S(1)}, u32[]{:S(2)}, u32[]{:S(2)}) collective-permute-start(bf16[2,16,8,256]{3,2,1,0:T(8,128)(2,1)S(1)} %get-tuple-element.30), channel_id=1, source_target_pairs={{0,2},{1,3},{2,4},{3,5},{4,6},{5,7},{6,0},{7,1},{8,10},{9,11},{10,... | collective-permute-start | bytes 393224 | tf_op jit(solution)/shard_map/ppermute | solution.py:304
  26.8 9.9 %collective-permute-start.5 = (bf16[2,16,8,256]{3,2,1,0:T(8,128)(2,1)S(1)}, bf16[2,16,8,256]{3,2,1,0:T(8,128)(2,1)S(1)}, u32[]{:S(2)}, u32[]{:S(2)}) collective-permute-start(bf16[2,16,8,256]{3,2,1,0:T(8,128)(2,1)S(1)} %get-tuple-element.31), channel_id=1, source_target_pairs={{0,4},{1,5},{2,6},{3,7},{4,0},{5,1},{6,2},{7,3},{8,12},{9,13},{10,... | collective-permute-start | bytes 393224 | tf_op jit(solution)/shard_map/ppermute | solution.py:304
  29.4 13.7 %copy-start.5 = (bf16[256,256]{1,0:T(8,128)(2,1)S(1)}, bf16[256,256]{1,0:T(8,128)(2,1)}, u32[]{:S(2)}) copy-start(bf16[256,256]{1,0:T(8,128)(2,1)} %wq_ref.3) | copy-start | bytes 393220
  29.4 13.7 %copy-start.6 = (bf16[256,256]{1,0:T(8,128)(2,1)S(1)}, bf16[256,256]{1,0:T(8,128)(2,1)}, u32[]{:S(2)}) copy-start(bf16[256,256]{1,0:T(8,128)(2,1)} %wk_ref.3) | copy-start | bytes 393220
  29.4 13.7 %copy-start.7 = (bf16[256,256]{1,0:T(8,128)(2,1)S(1)}, bf16[256,256]{1,0:T(8,128)(2,1)}, u32[]{:S(2)}) copy-start(bf16[256,256]{1,0:T(8,128)(2,1)} %wv_ref.3) | copy-start | bytes 393220
  29.4 7.3 %collective-permute-start.6 = (bf16[2,16,8,256]{3,2,1,0:T(8,128)(2,1)S(1)}, bf16[2,16,8,256]{3,2,1,0:T(8,128)(2,1)S(1)}, u32[]{:S(2)}, u32[]{:S(2)}) collective-permute-start(bf16[2,16,8,256]{3,2,1,0:T(8,128)(2,1)S(1)} %get-tuple-element.32), channel_id=1, source_target_pairs={{0,6},{1,7},{2,0},{3,1},{4,2},{5,3},{6,4},{7,5},{8,14},{9,15},{10,... | collective-permute-start | bytes 393224 | tf_op jit(solution)/shard_map/ppermute | solution.py:304
  36.8 6.3 %collective-permute-start.7 = (bf16[4,16,8,256]{3,2,1,0:T(8,128)(2,1)S(1)}, bf16[4,16,8,256]{3,2,1,0:T(8,128)(2,1)S(1)}, u32[]{:S(2)}, u32[]{:S(2)}) collective-permute-start(bf16[4,16,8,256]{3,2,1,0:T(8,128)(2,1)S(1)} %shard_map.86), channel_id=1, source_target_pairs={{0,1},{1,0},{2,3},{3,2},{4,5},{5,4},{6,7},{7,6},{8,9},{9,8},{10,11... | collective-permute-start | bytes 786440 | tf_op jit(solution)/shard_map/ppermute | solution.py:323
  38.1 8.0 %collective-permute-start.11 = (bf16[2,16,8,256]{3,2,1,0:T(8,128)(2,1)S(1)}, bf16[2,16,8,256]{3,2,1,0:T(8,128)(2,1)S(1)}, u32[]{:S(2)}, u32[]{:S(2)}) collective-permute-start(bf16[2,16,8,256]{3,2,1,0:T(8,128)(2,1)S(1)} %get-tuple-element.38), channel_id=1, source_target_pairs={{0,2},{1,3},{2,4},{3,5},{4,6},{5,7},{6,0},{7,1},{8,10},{9,11},{10,... | collective-permute-start | bytes 393224 | tf_op jit(solution)/shard_map/ppermute | solution.py:304
  39.4 9.0 %collective-permute-start.12 = (bf16[2,16,8,256]{3,2,1,0:T(8,128)(2,1)S(1)}, bf16[2,16,8,256]{3,2,1,0:T(8,128)(2,1)S(1)}, u32[]{:S(2)}, u32[]{:S(2)}) collective-permute-start(bf16[2,16,8,256]{3,2,1,0:T(8,128)(2,1)S(1)} %get-tuple-element.39), channel_id=1, source_target_pairs={{0,4},{1,5},{2,6},{3,7},{4,0},{5,1},{6,2},{7,3},{8,12},{9,13},{10,... | collective-permute-start | bytes 393224 | tf_op jit(solution)/shard_map/ppermute | solution.py:304
  42.0 6.4 %collective-permute-start.13 = (bf16[2,16,8,256]{3,2,1,0:T(8,128)(2,1)S(1)}, bf16[2,16,8,256]{3,2,1,0:T(8,128)(2,1)S(1)}, u32[]{:S(2)}, u32[]{:S(2)}) collective-permute-start(bf16[2,16,8,256]{3,2,1,0:T(8,128)(2,1)S(1)} %get-tuple-element.40), channel_id=1, source_target_pairs={{0,6},{1,7},{2,0},{3,1},{4,2},{5,3},{6,4},{7,5},{8,14},{9,15},{10,... | collective-permute-start | bytes 393224 | tf_op jit(solution)/shard_map/ppermute | solution.py:304
  48.4 4.7 %collective-permute-start.14 = (bf16[4,16,8,256]{3,2,1,0:T(8,128)(2,1)S(1)}, bf16[4,16,8,256]{3,2,1,0:T(8,128)(2,1)S(1)}, u32[]{:S(2)}, u32[]{:S(2)}) collective-permute-start(bf16[4,16,8,256]{3,2,1,0:T(8,128)(2,1)S(1)} %shard_map.88), channel_id=1, source_target_pairs={{0,1},{1,0},{2,3},{3,2},{4,5},{5,4},{6,7},{7,6},{8,9},{9,8},{10,11... | collective-permute-start | bytes 786440 | tf_op jit(solution)/shard_map/ppermute | solution.py:323
  49.4 9.3 %collective-permute-start.8 = (bf16[2,16,8,256]{3,2,1,0:T(8,128)(2,1)S(1)}, bf16[2,16,8,256]{3,2,1,0:T(8,128)(2,1)S(1)}, u32[]{:S(2)}, u32[]{:S(2)}) collective-permute-start(bf16[2,16,8,256]{3,2,1,0:T(8,128)(2,1)S(1)} %get-tuple-element.34), channel_id=1, source_target_pairs={{0,4},{1,5},{2,6},{3,7},{4,0},{5,1},{6,2},{7,3},{8,12},{9,13},{10,... | collective-permute-start | bytes 393224 | tf_op jit(solution)/shard_map/ppermute | solution.py:304
  51.7 7.3 %collective-permute-start.9 = (bf16[2,16,8,256]{3,2,1,0:T(8,128)(2,1)S(1)}, bf16[2,16,8,256]{3,2,1,0:T(8,128)(2,1)S(1)}, u32[]{:S(2)}, u32[]{:S(2)}) collective-permute-start(bf16[2,16,8,256]{3,2,1,0:T(8,128)(2,1)S(1)} %get-tuple-element.35), channel_id=1, source_target_pairs={{0,6},{1,7},{2,0},{3,1},{4,2},{5,3},{6,4},{7,5},{8,14},{9,15},{10,... | collective-permute-start | bytes 393224 | tf_op jit(solution)/shard_map/ppermute | solution.py:304
  52.7 14.2 %copy-start.3 = (bf16[256,256]{1,0:T(8,128)(2,1)S(1)}, bf16[256,256]{1,0:T(8,128)(2,1)}, u32[]{:S(2)}) copy-start(bf16[256,256]{1,0:T(8,128)(2,1)} %w_ref.3) | copy-start | bytes 393220
  52.7 6.3 %collective-permute-start.10 = (bf16[2,16,8,256]{3,2,1,0:T(8,128)(2,1)S(1)}, bf16[2,16,8,256]{3,2,1,0:T(8,128)(2,1)S(1)}, u32[]{:S(2)}, u32[]{:S(2)}) collective-permute-start(bf16[2,16,8,256]{3,2,1,0:T(8,128)(2,1)S(1)} %get-tuple-element.36), channel_id=1, source_target_pairs={{0,2},{1,3},{2,4},{3,5},{4,6},{5,7},{6,0},{7,1},{8,10},{9,11},{10,... | collective-permute-start | bytes 393224 | tf_op jit(solution)/shard_map/ppermute | solution.py:304
  56.1 5.4 %collective-permute-start.15 = (bf16[2,16,8,256]{3,2,1,0:T(8,128)(2,1)S(1)}, bf16[2,16,8,256]{3,2,1,0:T(8,128)(2,1)S(1)}, u32[]{:S(2)}, u32[]{:S(2)}) collective-permute-start(bf16[2,16,8,256]{3,2,1,0:T(8,128)(2,1)S(1)} %get-tuple-element.42), channel_id=1, source_target_pairs={{0,4},{1,5},{2,6},{3,7},{4,0},{5,1},{6,2},{7,3},{8,12},{9,13},{10,... | collective-permute-start | bytes 393224 | tf_op jit(solution)/shard_map/ppermute | solution.py:304
  56.9 7.6 %collective-permute-start.16 = (bf16[2,16,8,256]{3,2,1,0:T(8,128)(2,1)S(1)}, bf16[2,16,8,256]{3,2,1,0:T(8,128)(2,1)S(1)}, u32[]{:S(2)}, u32[]{:S(2)}) collective-permute-start(bf16[2,16,8,256]{3,2,1,0:T(8,128)(2,1)S(1)} %get-tuple-element.43), channel_id=1, source_target_pairs={{0,6},{1,7},{2,0},{3,1},{4,2},{5,3},{6,4},{7,5},{8,14},{9,15},{10,... | collective-permute-start | bytes 393224 | tf_op jit(solution)/shard_map/ppermute | solution.py:304
  58.7 6.6 %collective-permute-start.17 = (bf16[2,16,8,256]{3,2,1,0:T(8,128)(2,1)S(1)}, bf16[2,16,8,256]{3,2,1,0:T(8,128)(2,1)S(1)}, u32[]{:S(2)}, u32[]{:S(2)}) collective-permute-start(bf16[2,16,8,256]{3,2,1,0:T(8,128)(2,1)S(1)} %get-tuple-element.44), channel_id=1, source_target_pairs={{0,2},{1,3},{2,4},{3,5},{4,6},{5,7},{6,0},{7,1},{8,10},{9,11},{10,... | collective-permute-start | bytes 393224 | tf_op jit(solution)/shard_map/ppermute | solution.py:304
  65.3 3.2 %collective-permute-start.18 = (bf16[4,32,8,256]{3,2,1,0:T(8,128)(2,1)S(1)}, bf16[4,32,8,256]{3,2,1,0:T(8,128)(2,1)S(1)}, u32[]{:S(2)}, u32[]{:S(2)}) collective-permute-start(bf16[4,32,8,256]{3,2,1,0:T(8,128)(2,1)S(1)} %shard_map.90), channel_id=1, source_target_pairs={{0,1},{1,0},{2,3},{3,2},{4,5},{5,4},{6,7},{7,6},{8,9},{9,8},{10,11... | collective-permute-start | bytes 1572872 | tf_op jit(solution)/shard_map/ppermute | solution.py:323
